TPU v7x, 32 devices: a whole 2x2x4 slice. The times are simulated.
32 devices in a mesh: space: 8 (over z, core), spec: 4 (over y, x).
Axes of the slice: x: 2, y: 2, z: 4, core: 2. Of those that a mesh axis runs over, the one named last changes fastest.
Arguments:
- action: float32 [16, 24, 64, 512], P('spec', None, 'space'), may hold values from 0.1 to 1
- currents: float32 [2, 128, 1024], P(None, 'space', 'spec'), may hold values from -1.2 to 1.2
- wet: int32 [128, 1024], P('space', 'spec'), may hold values 0 or 1
- courant: float32 [16], replicated, may hold values from 0.1 to 0.35
- energy: float32 [16], replicated, may hold values from 0.3 to 3
- src: int32 [96, 512, 4], P('space'), may hold values from 4096 to 29695, as said below
- weights: float32 [96, 512, 4], P('space'), as said below
Outputs:
- new_action: float32 [16, 24, 64, 512], P('spec', None, 'space')
- new_currents: float32 [2, 128, 1024], P(None, 'space', 'spec')
Inputs may be any that keep to these rules, and one draw needn't show every extreme that they name: `src`: row e of block s refers to ocean rows 2 (e - 2) + 8 + j + a of the pair of ocean row blocks s and s + 1 (j 0 or 1 per wave cell, a the corner's row bit) and columns (2 x + i + b) mod 1024; the four corners of a cell are distinct; the two outer rows on each side of a block's lists refer to the same ocean cells, with the same weights, as the lists of the same wave rows in the neighbouring blocks. Positive; the 4 weights of a wave cell sum to one; rows that describe the same wave row are equal.
All inputs are finite; a program needn't handle non-finite values. No bound on the sum of `wet` on one device may be relied on, other than what follows from the above.
Results may differ from a plain program's by a relative error of at most 0.00009.
Values sent between devices are 32-bit elements; how exact they have to be, the bound alone decides.
No kernel may reach another device: no remote copies, remote signals or barrier semaphores. Data moves between devices by JAX's collectives and lax.ppermute only.
A program may use at most 128 MiB of HBM per device.

v0:
```python
import functools
import math

import jax
import jax.numpy as jnp
import numpy as np
from jax import lax
from jax.experimental import pallas as pl
from jax.experimental.pallas import tpu as pltpu
from jax.sharding import PartitionSpec as P


drift_factor = 0.2
refract_factor = 1.5
damping = 0.95
force_gain = 0.5

LANES = 128
HIGHEST = lax.Precision.HIGHEST
VMEM = pl.BlockSpec(memory_space=pltpu.VMEM)
SMEM = pl.BlockSpec(memory_space=pltpu.SMEM)


def from_offset(block, axis, offset):
    count = lax.axis_size(axis)
    return lax.ppermute(block, axis, [((i + offset) % count, i) for i in range(count)])


def from_xor(block, axis, bits):
    count = lax.axis_size(axis)
    return lax.ppermute(block, axis, [(i ^ bits, i) for i in range(count)])


def params(**kw):
    return pltpu.CompilerParams(vmem_limit_bytes=48 * 1024 * 1024, **kw)


def split_matrix(width):
    row = lax.broadcasted_iota(jnp.int32, (width, width), 0)
    col = lax.broadcasted_iota(jnp.int32, (width, width), 1)
    half = width // 2
    source = jnp.where(col < half, 2 * col, 2 * (col - half) + 1)
    return (row == source).astype(jnp.float32)


def merge_matrix(width):
    row = lax.broadcasted_iota(jnp.int32, (width, width), 0)
    col = lax.broadcasted_iota(jnp.int32, (width, width), 1)
    half = width // 2
    target = jnp.where(row < half, 2 * row, 2 * (row - half) + 1)
    return (col == target).astype(jnp.float32)


def split_kernel(own_ref, next_ref, out_ref):
    comps, rows, width = own_ref.shape
    matrix = split_matrix(width)
    for part, ref in enumerate((own_ref, next_ref)):
        cells = ref[...].reshape(comps * rows, width)
        split = jnp.dot(cells, matrix, precision=HIGHEST, preferred_element_type=jnp.float32)
        out_ref[:, part * rows : (part + 1) * rows, :] = split.reshape(comps, rows, width)


def roll_lanes(x, shift):
    lane = lax.broadcasted_iota(jnp.int32, x.shape, x.ndim - 1)
    turned = pltpu.roll(x, shift % LANES, x.ndim - 1)
    if shift == 1:
        return jnp.where(lane == 0, roll_lead(turned, 1, x.ndim - 3), turned)
    return jnp.where(lane == LANES - 1, roll_lead(turned, -1, x.ndim - 3), turned)


def roll_lead(x, shift, axis):
    count = x.shape[axis]
    cut = (-shift) % count
    if cut == 0:
        return x
    return jnp.concatenate(
        [lax.slice_in_dim(x, cut, count, axis=axis), lax.slice_in_dim(x, 0, cut, axis=axis)], axis=axis
    )


def roll_directions(x, shift):
    groups = x.shape[0]
    if shift == 1:
        edge = pltpu.roll(x[groups - 1 :], 1, 2)
        return jnp.concatenate([edge, x[: groups - 1]], axis=0)
    edge = pltpu.roll(x[:1], 7, 2)
    return jnp.concatenate([x[1:], edge], axis=0)


def row_view(ref, freq):
    return ref.at[freq].reshape(ref.shape[1] * ref.shape[2] * 8, LANES)


def row_slots(groups, tiles, row):
    return [
        [pl.ds((group * tiles + tile) * 8 + row, 8, stride=groups * tiles * 8) for tile in range(tiles)]
        for group in range(groups)
    ]


def load_row(view, groups, tiles, row):
    slots = row_slots(groups, tiles, row)
    return jnp.stack([jnp.stack([view[slot, :] for slot in line]) for line in slots])


def store_row(view, row, value):
    groups, tiles = value.shape[:2]
    for group, line in enumerate(row_slots(groups, tiles, row)):
        for tile, slot in enumerate(line):
            view[slot, :] = value[group, tile]


def prepare_kernel(ocean_cols, tail_rows, src_ref, weight_ref, field_ref, table_ref, low_ref, high_ref):
    list_rows, corners, columns = src_ref.shape
    freqs, directions, tiles, wave_rows, _ = field_ref.shape
    groups = directions // 8
    shape = (list_rows, columns)
    entry_row = lax.broadcasted_iota(jnp.int32, shape, 0)
    column = lax.broadcasted_iota(jnp.int32, shape, 1)
    base = (2 * (entry_row - 2) + wave_rows) * ocean_cols
    cell = [
        base + jnp.where(2 * column + step >= ocean_cols, 2 * column + step - ocean_cols, 2 * column + step)
        for step in range(3)
    ]
    sums = [jnp.zeros(shape, jnp.float32) for _ in range(9)]
    for corner in range(corners):
        source = src_ref[:, corner, :]
        weight = weight_ref[:, corner, :]
        for step_row in range(3):
            for step_col in range(3):
                hit = source == cell[step_col] + step_row * ocean_cols
                place = 3 * step_row + step_col
                sums[place] = sums[place] + jnp.where(hit, weight, 0.0)
    for place in range(9):
        table_ref[place] = sums[place]
    first = 2 + wave_rows // 2 - 1
    lead = freqs * 2 * groups
    for place in range(9):
        for row in range(tail_rows):
            slot = place * tail_rows + row
            line = table_ref[place, first + row : first + row + 1, :]
            for tile in range(tiles):
                low_ref[lead + slot // 8, tile, slot % 8 : slot % 8 + 1, :] = line[
                    :, tile * LANES : (tile + 1) * LANES
                ]
    for freq in range(freqs):
        view = row_view(field_ref, freq)
        for row in range(2):
            at = (freq * 2 + row) * groups
            low_ref[at : at + groups] = load_row(view, groups, tiles, wave_rows - 2 + row)
            high_ref[at : at + groups] = load_row(view, groups, tiles, row)


def advance_kernel(total_freq, axis, pieces, *refs):
    piece_refs = refs[:pieces]
    (table_ref, trig_ref, speed_ref, energy_ref, field_ref, low_ref, high_ref) = refs[pieces : pieces + 7]
    out_ref, stress_ref = refs[pieces + 7 : pieces + 9]
    ocean_ref, flow_ref, grad_ref, turn_ref, mid_ref, sum_ref, speeds_ref = refs[pieces + 9 :]
    freqs, directions, tiles, wave_rows, _ = field_ref.shape
    groups = directions // 8
    list_rows = table_ref.shape[1]
    index = lax.axis_index(axis)
    for bits, ref in enumerate(piece_refs):
        half = ref.shape[2] // 2
        count = half // LANES
        start = (index ^ bits) * count if pieces > 1 else 0
        for parity in range(2):
            for tile in range(count):
                lane = parity * half + tile * LANES
                ocean_ref[parity, start + tile] = ref[:, :, lane : lane + LANES]
    first = wave_rows - 4

    def lift(parity, comp, rows):
        return jnp.stack([ocean_ref[parity, tile, comp, rows, :] for tile in range(tiles)])

    def table(place):
        whole = table_ref[place]
        return jnp.stack([whole[:, tile * LANES : (tile + 1) * LANES] for tile in range(tiles)])

    for comp in range(2):
        total = None
        for step_row in range(3):
            rows = pl.ds(first + step_row, list_rows, stride=2)
            even, odd = lift(0, comp, rows), lift(1, comp, rows)
            for step_col, lifted in enumerate((even, odd, roll_lanes(even, -1))):
                term = table(3 * step_row + step_col) * lifted
                total = term if total is None else total + term
        flow_ref[comp, :, :list_rows] = total
    inner = list_rows - 2
    east, north = flow_ref[0, :, 1 : 1 + inner], flow_ref[1, :, 1 : 1 + inner]
    east_y = (flow_ref[0, :, 2 : 2 + inner] - flow_ref[0, :, 0:inner]) * 0.5
    north_y = (flow_ref[1, :, 2 : 2 + inner] - flow_ref[1, :, 0:inner]) * 0.5
    east_x = (roll_lanes(east, -1) - roll_lanes(east, 1)) * 0.5
    north_x = (roll_lanes(north, -1) - roll_lanes(north, 1)) * 0.5
    grad_ref[0, :, :inner] = refract_factor * (east_x - north_y)
    grad_ref[1, :, :inner] = refract_factor * east_y
    grad_ref[2, :, :inner] = refract_factor * north_x
    for comp in range(2):
        flow_ref[comp, :, :list_rows] = drift_factor * flow_ref[comp, :, :list_rows]
    full = (groups, tiles, 8, LANES)

    def spread(ref, kind, row):
        lines = [ref[kind, tile, pl.ds(row, 8, stride=0), :] for tile in range(tiles)]
        return jnp.broadcast_to(jnp.stack(lines)[None], full)

    def wide(kind):
        return jnp.broadcast_to(trig_ref[kind][:, None], full)

    cross, sin2, cos2 = wide(2), wide(3), wide(4)
    for row in range(inner):
        turn = cross * spread(grad_ref, 0, row) + sin2 * spread(grad_ref, 1, row) - cos2 * spread(grad_ref, 2, row)
        turn_ref[0, row] = jnp.maximum(turn, 0.0)
        turn_ref[1, row] = jnp.minimum(turn, 0.0)
    sum_ref[...] = jnp.zeros_like(sum_ref)
    start = index * freqs

    def one_frequency(freq, carry):
        speed = speed_ref[start + freq]
        speed_cos = jnp.broadcast_to((speed * trig_ref[0])[:, None], full)
        speed_sin = jnp.broadcast_to((speed * trig_ref[1])[:, None], full)
        source, sink = row_view(field_ref, freq), row_view(out_ref, freq)

        def cells(row):
            if row < 0:
                return low_ref[pl.ds((freq * 2 + 2 + row) * groups, groups)]
            if row >= wave_rows:
                return high_ref[pl.ds((freq * 2 + row - wave_rows) * groups, groups)]
            return load_row(source, groups, tiles, row)

        def north(row, fresh):
            if not fresh:
                return speeds_ref[2, row + 1], speeds_ref[3, row + 1]
            value = speed_sin + spread(flow_ref, 1, row + 2)
            up, down = jnp.maximum(value, 0.0), jnp.minimum(value, 0.0)
            if 0 <= row + 1 < wave_rows + 2:
                speeds_ref[2, row + 1], speeds_ref[3, row + 1] = up, down
            return up, down

        def east(row, fresh):
            if not fresh:
                return speeds_ref[0, row + 1], speeds_ref[1, row + 1]
            value = speed_cos + spread(flow_ref, 0, row + 2)
            up, down = jnp.maximum(value, 0.0), jnp.minimum(value, 0.0)
            if 0 <= row < wave_rows:
                speeds_ref[0, row + 1], speeds_ref[1, row + 1] = up, down
            return up, down

        def sweep(read, fresh, low, high, write):
            before = read(low - 1)
            here = read(low)
            up, down = north(low, fresh)
            face_before = north(low - 1, fresh)[0] * before + down * here
            for row in range(low, high):
                after = read(row + 1)
                up_after, down_after = north(row + 1, fresh)
                face_here = up * here + down_after * after
                right, left = east(row, fresh)
                face_x = right * here + roll_lanes(left * here, -1)
                face_turn = turn_ref[0, row + 1] * here + roll_directions(turn_ref[1, row + 1] * here, -1)
                write(
                    row,
                    here
                    - (face_x - roll_lanes(face_x, 1))
                    - (face_here - face_before)
                    - (face_turn - roll_directions(face_turn, 1)),
                )
                face_before, here, up = face_here, after, up_after

        def keep(row, value):
            mid_ref[row + 1] = value

        sweep(cells, True, -1, wave_rows + 1, keep)
        ratio = 0.5 + 0.5 * (start + freq).astype(jnp.float32) / (total_freq - 1)
        amplitude = energy_ref[start + freq] / math.sqrt(directions * total_freq)
        scale, rest = amplitude * ratio, amplitude * (ratio - 0.5)

        def finish(row, value):
            store_row(sink, row, value)
            plain = jnp.sum(value, axis=0)
            weighted = jnp.sum(cos2 * value, axis=0)
            mixed = jnp.sum(cross * value, axis=0)
            sum_ref[0, row] += scale * weighted + rest * plain
            sum_ref[1, row] += scale * (plain - weighted) + rest * plain
            sum_ref[2, row] += scale * mixed

        sweep(lambda row: mid_ref[row + 1], False, 0, wave_rows, finish)
        return carry

    lax.fori_loop(0, freqs, one_frequency, 0)
    for kind in range(3):
        for row in range(wave_rows):
            line = jnp.sum(sum_ref[kind, row], axis=1, keepdims=True)
            for tile in range(tiles):
                stress_ref[kind, row : row + 1, tile * LANES : (tile + 1) * LANES] = line[tile]


def force_terms(own_ref, prev_ref, table_ref, tail_ref, stress_ref, coupling_ref):
    wave_rows, columns = own_ref.shape[1:]
    half = wave_rows // 2
    count = wave_rows + 1
    behind = half + 2
    for kind in range(3):
        stress_ref[kind, 0:behind] = prev_ref[kind, wave_rows - behind : wave_rows]
        stress_ref[kind, behind : behind + half + 1] = own_ref[kind, 0 : half + 1]
    far = half - 1
    lead = tail_ref.shape[0] - -(-9 * far // 8)
    for place in range(9):
        for row in range(far):
            slot = place * far + row
            for tile in range(columns // LANES):
                coupling_ref[place, row : row + 1, tile * LANES : (tile + 1) * LANES] = tail_ref[
                    lead + slot // 8, tile, slot % 8 : slot % 8 + 1, :
                ]
        coupling_ref[place, far:count] = table_ref[place, 0 : count - far]

    def along_x(kind):
        middle = stress_ref[kind, 1 : 1 + count]
        return (pltpu.roll(middle, columns - 1, 1) - pltpu.roll(middle, 1, 1)) * 0.5

    def along_y(kind):
        return (stress_ref[kind, 2 : 2 + count] - stress_ref[kind, 0:count]) * 0.5

    forces = (-(along_x(0) + along_y(2)), -(along_x(2) + along_y(1)))
    return forces


def force_kernel(axis, own_ref, prev_ref, table_ref, tail_ref, current_ref, wet_ref, out_ref,
                 stress_ref, coupling_ref, push_ref, chunk_ref, merge_ref):
    wave_rows, _ = own_ref.shape[1:]
    width = current_ref.shape[2]
    half = width // 2
    forces = force_terms(own_ref, prev_ref, table_ref, tail_ref, stress_ref, coupling_ref)
    count = wave_rows + 1
    start = pl.multiple_of(lax.axis_index(axis) * half, LANES)
    for comp, force in enumerate(forces):
        for step_row in range(3):
            for step_col in range(3):
                push_ref[0, 3 * step_row + step_col, :count] = coupling_ref[3 * step_row + step_col] * force

        def near(place):
            return push_ref[0, place, 1:count]

        def far(place):
            return push_ref[0, place, 0 : count - 1]

        even_even = near(0) + far(6) + pltpu.roll(near(2) + far(8), 1, 1)
        even_odd = near(1) + far(7)
        odd_even = near(3) + pltpu.roll(near(5), 1, 1)
        odd_odd = near(4)
        for parity, (even, odd) in enumerate(((even_even, even_odd), (odd_even, odd_odd))):
            chunk_ref[0, comp, parity] = even
            chunk_ref[1, comp, parity] = odd
    rows = 4 * wave_rows
    even = chunk_ref[0, :, :, :, pl.ds(start, half)].reshape(rows, half)
    odd = chunk_ref[1, :, :, :, pl.ds(start, half)].reshape(rows, half)
    merged = jnp.dot(
        jnp.concatenate([even, odd], axis=1), merge_matrix(width), precision=HIGHEST,
        preferred_element_type=jnp.float32,
    ).reshape(2, 2, wave_rows, width)
    wet = wet_ref[...].astype(jnp.float32)
    for comp in range(2):
        for tile in range(width // LANES):
            lanes = slice(tile * LANES, (tile + 1) * LANES)
            for parity in range(2):
                lines = pl.ds(parity, wave_rows, stride=2)
                merge_ref[comp, tile, lines, :] = merged[comp, parity, :, lanes]
            out_ref[comp, :, lanes] = wet[:, lanes] * (
                damping * current_ref[comp, :, lanes] + force_gain * merge_ref[comp, tile]
            )


def push_kernel(own_ref, prev_ref, table_ref, tail_ref, out_ref, stress_ref, coupling_ref, push_ref):
    wave_rows, _ = own_ref.shape[1:]
    forces = force_terms(own_ref, prev_ref, table_ref, tail_ref, stress_ref, coupling_ref)
    count = wave_rows + 1
    for comp, force in enumerate(forces):
        for place in range(9):
            push_ref[0, place, :count] = coupling_ref[place] * force
        near = [push_ref[0, place, 1:count] for place in range(9)]
        far = [push_ref[0, place, 0 : count - 1] for place in range(9)]
        out_ref[0, comp, 0] = near[0] + far[6] + pltpu.roll(near[2] + far[8], 1, 1)
        out_ref[1, comp, 0] = near[1] + far[7]
        out_ref[0, comp, 1] = near[3] + pltpu.roll(near[5], 1, 1)
        out_ref[1, comp, 1] = near[4]


def window(action, currents, wet, courant, energy, src, weights):
    f32 = jnp.float32
    freqs, directions, wave_rows, columns = action.shape
    groups, tiles = directions // 8, columns // LANES
    list_rows = src.shape[0]
    ocean_rows, width = wet.shape
    spec = lax.axis_size("spec")
    ocean_cols = width * spec
    half = width // 2
    aligned = half % LANES == 0 and spec <= 4
    masked = currents * wet.astype(f32)[None]
    masked_next = from_offset(masked, "space", 1)
    field = jnp.transpose(action.reshape(freqs, directions, wave_rows, tiles, LANES), (0, 1, 3, 2, 4))
    tail_rows = wave_rows // 2 - 1
    lead = freqs * 2 * groups
    tables, low, high = pl.pallas_call(
        functools.partial(prepare_kernel, ocean_cols, tail_rows),
        out_shape=(
            jax.ShapeDtypeStruct((9, list_rows, columns), f32),
            jax.ShapeDtypeStruct((lead + -(-9 * tail_rows // 8), tiles, 8, LANES), f32),
            jax.ShapeDtypeStruct((lead, tiles, 8, LANES), f32),
        ),
        in_specs=[VMEM] * 3,
        out_specs=(VMEM,) * 3,
        compiler_params=params(),
        name="prepare",
    )(jnp.transpose(src, (0, 2, 1)), jnp.transpose(weights, (0, 2, 1)), field)
    low = from_offset(low, "space", -1)
    high = from_offset(high, "space", 1)
    if aligned:
        piece = pl.pallas_call(
            split_kernel,
            out_shape=jax.ShapeDtypeStruct((2, 2 * ocean_rows, width), f32),
            in_specs=[VMEM] * 2,
            out_specs=VMEM,
            compiler_params=params(),
            name="split",
        )(masked, masked_next)
        pieces = [piece] + [from_xor(piece, "spec", bits) for bits in range(1, spec)]
    else:
        both = lax.all_gather(jnp.concatenate([masked, masked_next], axis=1), "spec", axis=2, tiled=True)
        pieces = [jnp.concatenate([both[:, :, 0::2], both[:, :, 1::2]], axis=2)]
    angles = 2.0 * math.pi * (np.arange(directions) + 0.5) / directions
    cosine, sine = np.cos(angles), np.sin(angles)
    trig = np.stack([cosine, sine, sine * cosine, sine * sine, cosine * cosine]).astype(np.float32)
    trig = trig.reshape(5, 8, groups).transpose(0, 2, 1)
    trig = jnp.asarray(np.repeat(trig[:, :, :, None], LANES, axis=3))
    total_freq = freqs * spec
    padded = -(-list_rows // 8) * 8
    out_field, stress = pl.pallas_call(
        functools.partial(advance_kernel, total_freq, "spec", len(pieces)),
        out_shape=(
            jax.ShapeDtypeStruct(field.shape, f32),
            jax.ShapeDtypeStruct((3, wave_rows, columns), f32),
        ),
        in_specs=[VMEM] * len(pieces) + [VMEM, VMEM, SMEM, SMEM, VMEM, VMEM, VMEM],
        out_specs=(VMEM, VMEM),
        scratch_shapes=[
            pltpu.VMEM((2, tiles, 2, 2 * ocean_rows, LANES), f32),
            pltpu.VMEM((2, tiles, padded, LANES), f32),
            pltpu.VMEM((3, tiles, padded, LANES), f32),
            pltpu.VMEM((2, list_rows - 2, groups, tiles, 8, LANES), f32),
            pltpu.VMEM((wave_rows + 2, groups, tiles, 8, LANES), f32),
            pltpu.VMEM((3, wave_rows, tiles, 8, LANES), f32),
            pltpu.VMEM((4, wave_rows + 2, groups, tiles, 8, LANES), f32),
        ],
        compiler_params=params(),
        name="advance",
    )(*pieces, tables, trig, courant, energy, field, low, high)
    new_action = jnp.transpose(out_field, (0, 1, 3, 2, 4)).reshape(action.shape)
    if spec <= 4:
        stress = stress + sum(from_xor(stress, "spec", bits) for bits in range(1, spec))
    else:
        stress = lax.psum(stress, "spec")
    stress_prev = from_offset(stress, "space", -1)
    count = wave_rows + 1
    scratch = [
        pltpu.VMEM((3, 2 * wave_rows, columns), f32),
        pltpu.VMEM((9, count, columns), f32),
        pltpu.VMEM((1, 9, count, columns), f32),
    ]
    if aligned:
        updated = pl.pallas_call(
            functools.partial(force_kernel, "spec"),
            out_shape=jax.ShapeDtypeStruct(currents.shape, f32),
            in_specs=[VMEM] * 6,
            out_specs=VMEM,
            scratch_shapes=scratch
            + [
                pltpu.VMEM((2, 2, 2, wave_rows, columns), f32),
                pltpu.VMEM((2, width // LANES, ocean_rows, LANES), f32),
            ],
            compiler_params=params(),
            name="force",
        )(stress, stress_prev, tables, low, currents, wet)
    else:
        pushed = pl.pallas_call(
            push_kernel,
            out_shape=jax.ShapeDtypeStruct((2, 2, 2, wave_rows, columns), f32),
            in_specs=[VMEM] * 4,
            out_specs=VMEM,
            scratch_shapes=scratch,
            compiler_params=params(),
            name="push",
        )(stress, stress_prev, tables, low)
        grid = jnp.transpose(pushed, (1, 3, 2, 4, 0)).reshape(2, ocean_rows, ocean_cols)
        share = lax.dynamic_slice_in_dim(grid, lax.axis_index("spec") * width, width, 2)
        updated = wet.astype(f32)[None] * (damping * currents + force_gain * share)
    return (new_action, updated)


def solution(mesh):
    in_specs = (
        P("spec", None, "space", None),
        P(None, "space", "spec"),
        P("space", "spec"),
        P(),
        P(),
        P("space", None, None),
        P("space", None, None),
    )
    out_specs = (P("spec", None, "space", None), P(None, "space", "spec"))
    return jax.shard_map(window, mesh=mesh, in_specs=in_specs, out_specs=out_specs, check_vma=False)
```

profile of v0, /device:TPU:0, one launch (start us, length us, event | category | flops | bytes accessed | tf_op | source)
XLA Modules:
  0.0 46.7 jit_solution(14263576380053513087)
XLA Ops:
  0.6 0.0 copy-start.8
  0.6 0.0 copy-start.7
  0.7 0.0 copy-start
  0.7 1.4 %copy-done = f32[4,24,8,512]{3,2,1,0:T(8,128)S(1)} copy-done((f32[4,24,8,512]{3,2,1,0:T(8,128)S(1)}, f32[4,24,8,512]{3,2,1,0:T(8,128)}, u32[]{:S(2)}) %copy-start) | copy-done | bytes 1572888
  2.1 0.0 copy-start.3
  2.1 0.9 %copy-done.3 = s32[12,512,4]{1,2,0:T(4,128)S(1)} copy-done((s32[12,512,4]{1,2,0:T(4,128)S(1)}, s32[12,512,4]{1,2,0:T(4,128)}, u32[]{:S(2)}) %copy-start.3) | copy-done | bytes 98328
  3.0 0.0 copy-start.4
  3.0 0.9 %copy-done.4 = f32[12,512,4]{1,2,0:T(4,128)S(1)} copy-done((f32[12,512,4]{1,2,0:T(4,128)S(1)}, f32[12,512,4]{1,2,0:T(4,128)}, u32[]{:S(2)}) %copy-start.4) | copy-done | bytes 98328
  3.9 0.0 copy-start.5
  3.9 0.0 copy-start.2
  3.9 0.0 copy-start.1
  3.9 0.0 copy-start.6
  3.9 0.7 %prepare.1 = (f32[9,12,512]{2,1,0:T(8,128)S(1)}, f32[28,4,8,128]{3,2,1,0:T(8,128)S(1)}, f32[24,4,8,128]{3,2,1,0:T(8,128)S(1)}) custom-call(s32[12,4,512]{2,1,0:T(4,128)S(1)} %bitcast.10, f32[12,4,512]{2,1,0:T(4,128)S(1)} %bitcast.11, f32[4,24,4,8,128]{4,3,2,1,0:T(8,128)S(1)} %bitcast.8), custom_call_target="tpu_custom_call" | custom-call | tf_op jit(solution)/shard_map/prepare/pallas_call | solution.py:402
  4.6 0.5 %collective-permute-start.4 = (f32[28,4,8,128]{3,2,1,0:T(8,128)S(1)}, f32[28,4,8,128]{3,2,1,0:T(8,128)S(1)}, u32[]{:S(2)}, u32[]{:S(2)}) collective-permute-start(f32[28,4,8,128]{3,2,1,0:T(8,128)S(1)} %get-tuple-element.8), channel_id=1, source_target_pairs={{28,0},{0,4},{4,8},{8,12},{12,16},{16,20},{20,24},{24,28},{29,1},{... | collective-permute-start | bytes 1376264 | tf_op jit(solution)/shard_map/ppermute | solution.py:26
  5.1 4.1 %collective-permute-start.5 = (f32[24,4,8,128]{3,2,1,0:T(8,128)S(1)}, f32[24,4,8,128]{3,2,1,0:T(8,128)S(1)}, u32[]{:S(2)}, u32[]{:S(2)}) collective-permute-start(f32[24,4,8,128]{3,2,1,0:T(8,128)S(1)} %get-tuple-element.9), channel_id=1, source_target_pairs={{4,0},{8,4},{12,8},{16,12},{20,16},{24,20},{28,24},{0,28},{5,1},{9... | collective-permute-start | bytes 1179656 | tf_op jit(solution)/shard_map/ppermute | solution.py:26
  9.2 0.0 copy-done.5
  9.2 0.0 copy-done.2
  9.2 0.7 %collective-permute-start = (f32[2,16,256]{2,1,0:T(8,128)S(1)}, f32[2,16,256]{2,1,0:T(8,128)S(1)}, u32[]{:S(2)}, u32[]{:S(2)}) collective-permute-start(f32[2,16,256]{2,1,0:T(8,128)S(1)} %broadcast_multiply_fusion.own_ref), channel_id=1, source_target_pairs={{4,0},{8,4},{12,8},{16,12},{20,16},{24,20},{28,24},{0,28},{5,1},{9... | collective-permute-start | bytes 98312 | tf_op jit(solution)/shard_map/ppermute | solution.py:26
  10.0 7.7 %collective-permute-done.next_ref = f32[2,16,256]{2,1,0:T(8,128)S(1)} collective-permute-done((f32[2,16,256]{2,1,0:T(8,128)S(1)}, f32[2,16,256]{2,1,0:T(8,128)S(1)}, u32[]{:S(2)}, u32[]{:S(2)}) %collective-permute-start) | collective-permute-done | bytes 32800 | tf_op jit(solution)/shard_map/ppermute | solution.py:26
  17.7 0.4 split.1.refs_0_
  18.1 2.5 %collective-permute-start.3 = (f32[2,32,256]{2,1,0:T(8,128)S(1)}, f32[2,32,256]{2,1,0:T(8,128)S(1)}, u32[]{:S(2)}, u32[]{:S(2)}) collective-permute-start(f32[2,32,256]{2,1,0:T(8,128)S(1)} %split.1.refs_0_), channel_id=1, source_target_pairs={{3,0},{2,1},{1,2},{0,3},{7,4},{6,5},{5,6},{4,7},{11,8},{10,9},{9,1... | collective-permute-start | bytes 196616 | tf_op jit(solution)/shard_map/ppermute | solution.py:31
  20.6 0.5 %collective-permute-start.2 = (f32[2,32,256]{2,1,0:T(8,128)S(1)}, f32[2,32,256]{2,1,0:T(8,128)S(1)}, u32[]{:S(2)}, u32[]{:S(2)}) collective-permute-start(f32[2,32,256]{2,1,0:T(8,128)S(1)} %split.1.refs_0_), channel_id=1, source_target_pairs={{2,0},{3,1},{0,2},{1,3},{6,4},{7,5},{4,6},{5,7},{10,8},{11,9},{8,1... | collective-permute-start | bytes 196616 | tf_op jit(solution)/shard_map/ppermute | solution.py:31
  21.1 0.5 %collective-permute-start.1 = (f32[2,32,256]{2,1,0:T(8,128)S(1)}, f32[2,32,256]{2,1,0:T(8,128)S(1)}, u32[]{:S(2)}, u32[]{:S(2)}) collective-permute-start(f32[2,32,256]{2,1,0:T(8,128)S(1)} %split.1.refs_0_), channel_id=1, source_target_pairs={{1,0},{0,1},{3,2},{2,3},{5,4},{4,5},{7,6},{6,7},{9,8},{8,9},{11,10... | collective-permute-start | bytes 196616 | tf_op jit(solution)/shard_map/ppermute | solution.py:31
  21.6 1.7 %collective-permute-done.3.refs_3_ = f32[2,32,256]{2,1,0:T(8,128)S(1)} collective-permute-done((f32[2,32,256]{2,1,0:T(8,128)S(1)}, f32[2,32,256]{2,1,0:T(8,128)S(1)}, u32[]{:S(2)}, u32[]{:S(2)}) %collective-permute-start.3) | collective-permute-done | bytes 65568 | tf_op jit(solution)/shard_map/ppermute | solution.py:31
  23.3 2.0 %collective-permute-done.2.refs_2_ = f32[2,32,256]{2,1,0:T(8,128)S(1)} collective-permute-done((f32[2,32,256]{2,1,0:T(8,128)S(1)}, f32[2,32,256]{2,1,0:T(8,128)S(1)}, u32[]{:S(2)}, u32[]{:S(2)}) %collective-permute-start.2) | collective-permute-done | bytes 65568 | tf_op jit(solution)/shard_map/ppermute | solution.py:31
  25.3 0.2 collective-permute-done.1.refs_1_
  25.6 0.0 collective-permute-done.5.refs_10_
  25.6 0.0 collective-permute-done.4.refs_9_.tail_ref
  25.6 0.0 copy-done.8
  25.6 0.0 copy-done.7
  25.6 0.0 copy-done.1
  25.6 0.0 copy-done.6
  25.6 8.4 %advance.1 = (f32[4,24,4,8,128]{4,3,2,1,0:T(8,128)}, f32[3,8,512]{2,1,0:T(8,128)S(1)}) custom-call(f32[2,32,256]{2,1,0:T(8,128)S(1)} %split.1.refs_0_, f32[2,32,256]{2,1,0:T(8,128)S(1)} %collective-permute-done.1.refs_1_, f32[2,32,256]{2,1,0:T(8,128)S(1)} %collective-permute-done.2.refs_2_, f32[2,32,256]{2,1,0:T(8,128)S(1)} %collective-permute-done.3.refs_3_, ...), custom_call_target="tpu_custom_call" | custom-call | tf_op jit(solution)/shard_map/advance/pallas_call | solution.py:436
  34.0 1.4 %collective-permute-start.8 = (f32[3,8,512]{2,1,0:T(8,128)S(1)}, f32[3,8,512]{2,1,0:T(8,128)S(1)}, u32[]{:S(2)}, u32[]{:S(2)}) collective-permute-start(f32[3,8,512]{2,1,0:T(8,128)S(1)} %get-tuple-element.11), channel_id=1, source_target_pairs={{3,0},{2,1},{1,2},{0,3},{7,4},{6,5},{5,6},{4,7},{11,8},{10,9},{9,1... | collective-permute-start | bytes 147464 | tf_op jit(solution)/shard_map/ppermute | solution.py:31
  35.5 0.6 %collective-permute-start.7 = (f32[3,8,512]{2,1,0:T(8,128)S(1)}, f32[3,8,512]{2,1,0:T(8,128)S(1)}, u32[]{:S(2)}, u32[]{:S(2)}) collective-permute-start(f32[3,8,512]{2,1,0:T(8,128)S(1)} %get-tuple-element.11), channel_id=1, source_target_pairs={{2,0},{3,1},{0,2},{1,3},{6,4},{7,5},{4,6},{5,7},{10,8},{11,9},{8,1... | collective-permute-start | bytes 147464 | tf_op jit(solution)/shard_map/ppermute | solution.py:31
  36.1 1.5 %collective-permute-start.6 = (f32[3,8,512]{2,1,0:T(8,128)S(1)}, f32[3,8,512]{2,1,0:T(8,128)S(1)}, u32[]{:S(2)}, u32[]{:S(2)}) collective-permute-start(f32[3,8,512]{2,1,0:T(8,128)S(1)} %get-tuple-element.11), channel_id=1, source_target_pairs={{1,0},{0,1},{3,2},{2,3},{5,4},{4,5},{7,6},{6,7},{9,8},{8,9},{11,10... | collective-permute-start | bytes 147464 | tf_op jit(solution)/shard_map/ppermute | solution.py:31
  37.5 1.7 %collective-permute-done.8 = f32[3,8,512]{2,1,0:T(8,128)S(1)} collective-permute-done((f32[3,8,512]{2,1,0:T(8,128)S(1)}, f32[3,8,512]{2,1,0:T(8,128)S(1)}, u32[]{:S(2)}, u32[]{:S(2)}) %collective-permute-start.8) | collective-permute-done | bytes 49184 | tf_op jit(solution)/shard_map/ppermute | solution.py:31
  39.2 1.0 %collective-permute-done.7 = f32[3,8,512]{2,1,0:T(8,128)S(1)} collective-permute-done((f32[3,8,512]{2,1,0:T(8,128)S(1)}, f32[3,8,512]{2,1,0:T(8,128)S(1)}, u32[]{:S(2)}, u32[]{:S(2)}) %collective-permute-start.7) | collective-permute-done | bytes 49184 | tf_op jit(solution)/shard_map/ppermute | solution.py:31
  40.2 0.1 collective-permute-done.6
  40.3 0.1 collective-permute-start.9
  40.4 5.3 %collective-permute-done.9.prev_ref = f32[3,8,512]{2,1,0:T(8,128)S(1)} collective-permute-done((f32[3,8,512]{2,1,0:T(8,128)S(1)}, f32[3,8,512]{2,1,0:T(8,128)S(1)}, u32[]{:S(2)}, u32[]{:S(2)}) %collective-permute-start.9) | collective-permute-done | bytes 49184 | tf_op jit(solution)/shard_map/ppermute | solution.py:26
  45.7 1.1 %force.1 = f32[2,16,256]{2,1,0:T(8,128)} custom-call(f32[3,8,512]{2,1,0:T(8,128)S(1)} %add_add_fusion.own_ref, f32[3,8,512]{2,1,0:T(8,128)S(1)} %collective-permute-done.9.prev_ref, f32[9,12,512]{2,1,0:T(8,128)S(1)} %get-tuple-element.7.refs_4_.table_ref, f32[28,4,8,128]{3,2,1,0:T(8,128)S(1)} %collective-permute-done.4.refs_9_.tail_ref, ...), custom_call_target="tpu_custom_call" | custom-call | tf_op jit(solution)/shard_map/force/pallas_call | solution.py:469
  (3 shorter events, 0.0 us)
Async XLA Ops:
  0.6 24.9 %copy-start.8 = (f32[16]{0:T(128)S(1)}, f32[16]{0:T(128)}, u32[]{:S(2)}) copy-start(f32[16]{0:T(128)} %refs_7_.1) | copy-start | bytes 196
  0.6 24.9 %copy-start.7 = (f32[16]{0:T(128)S(1)}, f32[16]{0:T(128)}, u32[]{:S(2)}) copy-start(f32[16]{0:T(128)} %refs_6_.1) | copy-start | bytes 196
  0.7 1.4 %copy-start = (f32[4,24,8,512]{3,2,1,0:T(8,128)S(1)}, f32[4,24,8,512]{3,2,1,0:T(8,128)}, u32[]{:S(2)}) copy-start(f32[4,24,8,512]{3,2,1,0:T(8,128)} %param.8) | copy-start | bytes 4718596
  2.1 0.9 %copy-start.3 = (s32[12,512,4]{1,2,0:T(4,128)S(1)}, s32[12,512,4]{1,2,0:T(4,128)}, u32[]{:S(2)}) copy-start(s32[12,512,4]{1,2,0:T(4,128)} %param.13) | copy-start | bytes 294916
  3.0 0.9 %copy-start.4 = (f32[12,512,4]{1,2,0:T(4,128)S(1)}, f32[12,512,4]{1,2,0:T(4,128)}, u32[]{:S(2)}) copy-start(f32[12,512,4]{1,2,0:T(4,128)} %param.14) | copy-start | bytes 294916
  3.9 5.3 %copy-start.5 = (s32[16,256]{1,0:T(8,128)S(1)}, s32[16,256]{1,0:T(8,128)}, u32[]{:S(2)}) copy-start(s32[16,256]{1,0:T(8,128)} %wet_ref.1) | copy-start | bytes 49156
  3.9 5.3 %copy-start.2 = (f32[2,16,256]{2,1,0:T(8,128)S(1)}, f32[2,16,256]{2,1,0:T(8,128)}, u32[]{:S(2)}) copy-start(f32[2,16,256]{2,1,0:T(8,128)} %current_ref.1) | copy-start | bytes 98308
  3.9 21.7 %copy-start.1 = (f32[4,24,8,512]{3,2,1,0:T(8,128)S(1)}, f32[4,24,8,512]{3,2,1,0:T(8,128)}, u32[]{:S(2)}) copy-start(f32[4,24,8,512]{3,2,1,0:T(8,128)} %param.8) | copy-start | bytes 4718596
  3.9 21.7 %copy-start.6 = (f32[5,3,8,128]{3,2,1,0:T(8,128)S(1)}, f32[5,3,8,128]{3,2,1,0:T(8,128)}, u32[]{:S(2)}) copy-start(f32[5,3,8,128]{3,2,1,0:T(8,128)} %constant.2.clone.refs_5_) | copy-start | bytes 184324
  4.6 21.0 %collective-permute-start.4 = (f32[28,4,8,128]{3,2,1,0:T(8,128)S(1)}, f32[28,4,8,128]{3,2,1,0:T(8,128)S(1)}, u32[]{:S(2)}, u32[]{:S(2)}) collective-permute-start(f32[28,4,8,128]{3,2,1,0:T(8,128)S(1)} %get-tuple-element.8), channel_id=1, source_target_pairs={{28,0},{0,4},{4,8},{8,12},{12,16},{16,20},{20,24},{24,28},{29,1},{... | collective-permute-start | bytes 1376264 | tf_op jit(solution)/shard_map/ppermute | solution.py:26
  5.1 20.5 %collective-permute-start.5 = (f32[24,4,8,128]{3,2,1,0:T(8,128)S(1)}, f32[24,4,8,128]{3,2,1,0:T(8,128)S(1)}, u32[]{:S(2)}, u32[]{:S(2)}) collective-permute-start(f32[24,4,8,128]{3,2,1,0:T(8,128)S(1)} %get-tuple-element.9), channel_id=1, source_target_pairs={{4,0},{8,4},{12,8},{16,12},{20,16},{24,20},{28,24},{0,28},{5,1},{9... | collective-permute-start | bytes 1179656 | tf_op jit(solution)/shard_map/ppermute | solution.py:26
  9.2 8.5 %collective-permute-start = (f32[2,16,256]{2,1,0:T(8,128)S(1)}, f32[2,16,256]{2,1,0:T(8,128)S(1)}, u32[]{:S(2)}, u32[]{:S(2)}) collective-permute-start(f32[2,16,256]{2,1,0:T(8,128)S(1)} %broadcast_multiply_fusion.own_ref), channel_id=1, source_target_pairs={{4,0},{8,4},{12,8},{16,12},{20,16},{24,20},{28,24},{0,28},{5,1},{9... | collective-permute-start | bytes 98312 | tf_op jit(solution)/shard_map/ppermute | solution.py:26
  18.1 5.2 %collective-permute-start.3 = (f32[2,32,256]{2,1,0:T(8,128)S(1)}, f32[2,32,256]{2,1,0:T(8,128)S(1)}, u32[]{:S(2)}, u32[]{:S(2)}) collective-permute-start(f32[2,32,256]{2,1,0:T(8,128)S(1)} %split.1.refs_0_), channel_id=1, source_target_pairs={{3,0},{2,1},{1,2},{0,3},{7,4},{6,5},{5,6},{4,7},{11,8},{10,9},{9,1... | collective-permute-start | bytes 196616 | tf_op jit(solution)/shard_map/ppermute | solution.py:31
  20.6 4.7 %collective-permute-start.2 = (f32[2,32,256]{2,1,0:T(8,128)S(1)}, f32[2,32,256]{2,1,0:T(8,128)S(1)}, u32[]{:S(2)}, u32[]{:S(2)}) collective-permute-start(f32[2,32,256]{2,1,0:T(8,128)S(1)} %split.1.refs_0_), channel_id=1, source_target_pairs={{2,0},{3,1},{0,2},{1,3},{6,4},{7,5},{4,6},{5,7},{10,8},{11,9},{8,1... | collective-permute-start | bytes 196616 | tf_op jit(solution)/shard_map/ppermute | solution.py:31
  21.1 4.5 %collective-permute-start.1 = (f32[2,32,256]{2,1,0:T(8,128)S(1)}, f32[2,32,256]{2,1,0:T(8,128)S(1)}, u32[]{:S(2)}, u32[]{:S(2)}) collective-permute-start(f32[2,32,256]{2,1,0:T(8,128)S(1)} %split.1.refs_0_), channel_id=1, source_target_pairs={{1,0},{0,1},{3,2},{2,3},{5,4},{4,5},{7,6},{6,7},{9,8},{8,9},{11,10... | collective-permute-start | bytes 196616 | tf_op jit(solution)/shard_map/ppermute | solution.py:31
  34.0 5.2 %collective-permute-start.8 = (f32[3,8,512]{2,1,0:T(8,128)S(1)}, f32[3,8,512]{2,1,0:T(8,128)S(1)}, u32[]{:S(2)}, u32[]{:S(2)}) collective-permute-start(f32[3,8,512]{2,1,0:T(8,128)S(1)} %get-tuple-element.11), channel_id=1, source_target_pairs={{3,0},{2,1},{1,2},{0,3},{7,4},{6,5},{5,6},{4,7},{11,8},{10,9},{9,1... | collective-permute-start | bytes 147464 | tf_op jit(solution)/shard_map/ppermute | solution.py:31
  35.5 4.7 %collective-permute-start.7 = (f32[3,8,512]{2,1,0:T(8,128)S(1)}, f32[3,8,512]{2,1,0:T(8,128)S(1)}, u32[]{:S(2)}, u32[]{:S(2)}) collective-permute-start(f32[3,8,512]{2,1,0:T(8,128)S(1)} %get-tuple-element.11), channel_id=1, source_target_pairs={{2,0},{3,1},{0,2},{1,3},{6,4},{7,5},{4,6},{5,7},{10,8},{11,9},{8,1... | collective-permute-start | bytes 147464 | tf_op jit(solution)/shard_map/ppermute | solution.py:31
  36.1 4.2 %collective-permute-start.6 = (f32[3,8,512]{2,1,0:T(8,128)S(1)}, f32[3,8,512]{2,1,0:T(8,128)S(1)}, u32[]{:S(2)}, u32[]{:S(2)}) collective-permute-start(f32[3,8,512]{2,1,0:T(8,128)S(1)} %get-tuple-element.11), channel_id=1, source_target_pairs={{1,0},{0,1},{3,2},{2,3},{5,4},{4,5},{7,6},{6,7},{9,8},{8,9},{11,10... | collective-permute-start | bytes 147464 | tf_op jit(solution)/shard_map/ppermute | solution.py:31
  40.3 5.4 %collective-permute-start.9 = (f32[3,8,512]{2,1,0:T(8,128)S(1)}, f32[3,8,512]{2,1,0:T(8,128)S(1)}, u32[]{:S(2)}, u32[]{:S(2)}) collective-permute-start(f32[3,8,512]{2,1,0:T(8,128)S(1)} %add_add_fusion.own_ref), channel_id=1, source_target_pairs={{28,0},{0,4},{4,8},{8,12},{12,16},{16,20},{20,24},{24,28},{29,1},{... | collective-permute-start | bytes 147464 | tf_op jit(solution)/shard_map/ppermute | solution.py:26
where the time goes:
time: 47 us; the launch traced here: 46.7 us
  waiting for transfers between devices  19.7 us (42%)
  starting transfers between devices  12.5 us (27%)
  Pallas kernels  10.6 us (23%)
  local copies, waits for them, and re-layouts  3.22 us (7%)
  between operations  0.73 us (2%)
    ppermute x4, waiting for transfers between devices, from_offset(): lax.ppermute(block, axis, [((i + offset) % count, i) for i in range(count)])  13.1 us
    pallas_call x1, Pallas kernels, window(): pl.pallas_call(functools.partial(advance_kernel, total_freq, 'spec', len(...  8.43 us
    ppermute x6, starting transfers between devices, from_xor(): return lax.ppermute(block, axis, [(i ^ bits, i) for i in range(count)])  7.04 us
    ppermute x6, waiting for transfers between devices, from_xor(): return lax.ppermute(block, axis, [(i ^ bits, i) for i in range(count)])  6.68 us
    ppermute x4, starting transfers between devices, from_offset(): lax.ppermute(block, axis, [((i + offset) % count, i) for i in range(count)])  5.42 us
    unnamed x18, local copies, waits for them, and re-layouts  3.22 us
    pallas_call x1, Pallas kernels, window(): pl.pallas_call(functools.partial(force_kernel, 'spec'), out_shape=jax.Sha...  1.08 us
  transfers between devices with their start and end apart: 10, of which 8 were waited for; matrix products, arithmetic and copies ran while one was open for 0% of the time, Pallas kernels for 1%

commit v1 on v0

v1 whole, which is shorter than its diff:
```python
import functools
import math

import jax
import jax.numpy as jnp
import numpy as np
from jax import lax
from jax.experimental import pallas as pl
from jax.experimental.pallas import tpu as pltpu
from jax.sharding import PartitionSpec as P


drift_factor = 0.2
refract_factor = 1.5
damping = 0.95
force_gain = 0.5

LANES = 128
HIGHEST = lax.Precision.HIGHEST
VMEM = pl.BlockSpec(memory_space=pltpu.VMEM)
SMEM = pl.BlockSpec(memory_space=pltpu.SMEM)
HBM = pl.BlockSpec(memory_space=pltpu.MemorySpace.HBM)
TAIL_VREGS = 4


def from_offset(block, axis, offset):
    count = lax.axis_size(axis)
    return lax.ppermute(block, axis, [((i + offset) % count, i) for i in range(count)])


def from_mesh(block, offset, bits):
    space, spec = lax.axis_size("space"), lax.axis_size("spec")
    route = [
        (((i + offset) % space) * spec + (j ^ bits), i * spec + j) for i in range(space) for j in range(spec)
    ]
    return lax.ppermute(block, ("space", "spec"), route)


def params(**kw):
    return pltpu.CompilerParams(vmem_limit_bytes=48 * 1024 * 1024, **kw)


def split_matrix(width):
    row = lax.broadcasted_iota(jnp.int32, (width, width), 0)
    col = lax.broadcasted_iota(jnp.int32, (width, width), 1)
    half = width // 2
    source = jnp.where(col < half, 2 * col, 2 * (col - half) + 1)
    return (row == source).astype(jnp.float32)


def merge_matrix(width):
    row = lax.broadcasted_iota(jnp.int32, (width, width), 0)
    col = lax.broadcasted_iota(jnp.int32, (width, width), 1)
    half = width // 2
    target = jnp.where(row < half, 2 * row, 2 * (row - half) + 1)
    return (col == target).astype(jnp.float32)


def roll_lanes(x, shift):
    lane = lax.broadcasted_iota(jnp.int32, x.shape, x.ndim - 1)
    turned = pltpu.roll(x, shift % LANES, x.ndim - 1)
    if shift == 1:
        return jnp.where(lane == 0, roll_lead(turned, 1, x.ndim - 3), turned)
    return jnp.where(lane == LANES - 1, roll_lead(turned, -1, x.ndim - 3), turned)


def roll_lead(x, shift, axis):
    count = x.shape[axis]
    cut = (-shift) % count
    if cut == 0:
        return x
    return jnp.concatenate(
        [lax.slice_in_dim(x, cut, count, axis=axis), lax.slice_in_dim(x, 0, cut, axis=axis)], axis=axis
    )


def roll_directions(x, shift):
    groups = x.shape[0]
    if shift == 1:
        edge = pltpu.roll(x[groups - 1 :], 1, 2)
        return jnp.concatenate([edge, x[: groups - 1]], axis=0)
    edge = pltpu.roll(x[:1], 7, 2)
    return jnp.concatenate([x[1:], edge], axis=0)


def row_view(ref, freq):
    return ref.at[freq].reshape(ref.shape[1] * ref.shape[2] * 8, LANES)


def row_slots(groups, tiles, row):
    return [
        [pl.ds((group * tiles + tile) * 8 + row, 8, stride=groups * tiles * 8) for tile in range(tiles)]
        for group in range(groups)
    ]


def load_row(view, groups, tiles, row):
    slots = row_slots(groups, tiles, row)
    return jnp.stack([jnp.stack([view[slot, :] for slot in line]) for line in slots])


def store_row(view, row, value):
    groups, tiles = value.shape[:2]
    for group, line in enumerate(row_slots(groups, tiles, row)):
        for tile, slot in enumerate(line):
            view[slot, :] = value[group, tile]


def tail_slot(tiles, which, slot):
    vreg = which * TAIL_VREGS + slot // 8
    return vreg // tiles, vreg % tiles, slot % 8


def chosen_tiles(axis, aligned, tiles):
    if not aligned:
        return list(range(tiles))
    index = lax.axis_index(axis)
    return [index, lax.rem(index + tiles - 1, tiles)]


def open_kernel(
    ocean_cols, tail_rows, axis, aligned, current_hbm, wet_hbm, src_hbm, weight_hbm, field_hbm,
    masked_ref, wet_out, table_ref, field_ref, low_ref, high_ref,
    current_ref, wet_ref, src_ref, weight_ref, sems,
):
    copies = [
        pltpu.make_async_copy(source, target, sems.at[k])
        for k, (source, target) in enumerate(
            (
                (current_hbm, current_ref),
                (wet_hbm, wet_ref),
                (src_hbm, src_ref),
                (weight_hbm, weight_ref),
                (field_hbm, field_ref),
            )
        )
    ]
    for copy in copies:
        copy.start()
    list_rows, corners, columns = src_ref.shape
    freqs, directions, tiles, wave_rows, _ = field_ref.shape
    groups = directions // 8
    copies[0].wait()
    copies[1].wait()
    wet = wet_ref[...].astype(jnp.float32)
    wet_out[...] = wet
    masked_ref[...] = current_ref[...] * wet[None]
    shape = (list_rows, columns)
    entry_row = lax.broadcasted_iota(jnp.int32, shape, 0)
    column = lax.broadcasted_iota(jnp.int32, shape, 1)
    base = (2 * (entry_row - 2) + wave_rows) * ocean_cols
    cell = [
        base + jnp.where(2 * column + step >= ocean_cols, 2 * column + step - ocean_cols, 2 * column + step)
        for step in range(3)
    ]
    copies[2].wait()
    copies[3].wait()
    sums = [jnp.zeros(shape, jnp.float32) for _ in range(9)]
    for corner in range(corners):
        source = src_ref[:, corner, :]
        weight = weight_ref[:, corner, :]
        for step_row in range(3):
            for step_col in range(3):
                hit = source == cell[step_col] + step_row * ocean_cols
                place = 3 * step_row + step_col
                sums[place] = sums[place] + jnp.where(hit, weight, 0.0)
    for place in range(9):
        for tile in range(tiles):
            table_ref[place, tile, :list_rows] = sums[place][:, tile * LANES : (tile + 1) * LANES]
    first = 2 + wave_rows // 2 - 1
    lead = freqs * 2 * groups
    for which, tile in enumerate(chosen_tiles(axis, aligned, tiles)):
        for place in range(9):
            for row in range(tail_rows):
                block, at, line = tail_slot(tiles, which, place * tail_rows + row)
                low_ref[lead + block, at, line : line + 1, :] = table_ref[
                    place, tile, first + row : first + row + 1, :
                ]
    copies[4].wait()
    for freq in range(freqs):
        view = row_view(field_ref, freq)
        for row in range(2):
            at = (freq * 2 + row) * groups
            low_ref[at : at + groups] = load_row(view, groups, tiles, wave_rows - 2 + row)
            high_ref[at : at + groups] = load_row(view, groups, tiles, row)


def flow_tile(table_ref, tile, evens, odds, nexts):
    total = None
    for step_row in range(3):
        even = evens[step_row]
        list_rows = even.shape[0]
        lane = lax.broadcasted_iota(jnp.int32, even.shape, 1)
        edge = 0.0 if nexts is None else pltpu.roll(nexts[step_row], LANES - 1, 1)
        shifted = jnp.where(lane == LANES - 1, edge, pltpu.roll(even, LANES - 1, 1))
        for step_col, lifted in enumerate((even, odds[step_row], shifted)):
            term = table_ref[3 * step_row + step_col, tile, :list_rows] * lifted
            total = term if total is None else total + term
    return total


def row_steps(ref, parity, tile, comp, first, list_rows):
    return [ref[parity, tile, comp, pl.ds(first + step, list_rows, stride=2), :] for step in range(3)]


def flow_kernel(axis, list_rows, first, own_ref, x_ref, z_ref, xz_ref, table_ref, part_ref, ocean_ref):
    comps, rows, width = own_ref.shape
    tiles = table_ref.shape[1]
    half = width // 2
    index = lax.axis_index(axis)
    place = lax.rem(index, 2)
    matrix = split_matrix(width)
    cells = jnp.concatenate(
        [ref[...].reshape(comps * rows, width) for ref in (own_ref, z_ref, x_ref, xz_ref)], axis=0
    )
    split = jnp.dot(cells, matrix, precision=HIGHEST, preferred_element_type=jnp.float32)
    split = split.reshape(4, comps, rows, width)
    for parity in range(2):
        lanes = slice(parity * half, (parity + 1) * half)
        for block in range(2):
            at = slice(block * rows, (block + 1) * rows)
            ocean_ref[parity, place, :, at] = split[block, :, :, lanes]
            ocean_ref[parity, 1 - place, :, at] = split[2 + block, :, :, lanes]
    tile = index - place
    before = lax.rem(tile + tiles - 1, tiles)
    for comp in range(comps):
        evens = [row_steps(ocean_ref, 0, k, comp, first, list_rows) for k in range(2)]
        odds = [row_steps(ocean_ref, 1, k, comp, first, list_rows) for k in range(2)]
        part_ref[0, comp, :list_rows] = flow_tile(table_ref, tile, evens[0], odds[0], evens[1])
        part_ref[1, comp, :list_rows] = flow_tile(table_ref, tile + 1, evens[1], odds[1], None)
        lane = lax.broadcasted_iota(jnp.int32, (list_rows, LANES), 1)
        spill = None
        for step in range(3):
            edge = jnp.where(lane == LANES - 1, pltpu.roll(evens[0][step], LANES - 1, 1), 0.0)
            term = table_ref[3 * step + 2, before, :list_rows] * edge
            spill = term if spill is None else spill + term
        part_ref[2, comp, :list_rows] = spill


def flow_all_kernel(list_rows, first, ocean_ref, table_ref, flow_ref):
    tiles = table_ref.shape[1]
    for comp in range(2):
        evens = [row_steps(ocean_ref, 0, k, comp, first, list_rows) for k in range(tiles)]
        odds = [row_steps(ocean_ref, 1, k, comp, first, list_rows) for k in range(tiles)]
        for tile in range(tiles):
            flow_ref[tile, comp, :list_rows] = flow_tile(
                table_ref, tile, evens[tile], odds[tile], evens[(tile + 1) % tiles]
            )


def advance_kernel(total_freq, axis, list_rows, parts, *refs):
    part_refs = refs[:parts]
    (trig_ref, speed_ref, energy_ref, field_ref, low_ref, high_ref) = refs[parts : parts + 6]
    out_ref, stress_ref = refs[parts + 6 : parts + 8]
    flow_ref, grad_ref, turn_ref, mid_ref, sum_ref, speeds_ref = refs[parts + 8 :]
    freqs, directions, tiles, wave_rows, _ = field_ref.shape
    groups = directions // 8
    index = lax.axis_index(axis)
    for comp in range(2):
        if parts == 1:
            for tile in range(tiles):
                flow_ref[comp, tile] = part_refs[0][tile, comp]
        else:
            tile = index - lax.rem(index, 2)
            other = tiles // 2 - tile
            own, theirs = part_refs
            flow_ref[comp, tile] = own[0, comp]
            flow_ref[comp, tile + 1] = own[1, comp] + theirs[2, comp]
            flow_ref[comp, other] = theirs[0, comp]
            flow_ref[comp, other + 1] = theirs[1, comp] + own[2, comp]
    inner = list_rows - 2
    east, north = flow_ref[0, :, 1 : 1 + inner], flow_ref[1, :, 1 : 1 + inner]
    east_y = (flow_ref[0, :, 2 : 2 + inner] - flow_ref[0, :, 0:inner]) * 0.5
    north_y = (flow_ref[1, :, 2 : 2 + inner] - flow_ref[1, :, 0:inner]) * 0.5
    east_x = (roll_lanes(east, -1) - roll_lanes(east, 1)) * 0.5
    north_x = (roll_lanes(north, -1) - roll_lanes(north, 1)) * 0.5
    grad_ref[0, :, :inner] = refract_factor * (east_x - north_y)
    grad_ref[1, :, :inner] = refract_factor * east_y
    grad_ref[2, :, :inner] = refract_factor * north_x
    for comp in range(2):
        flow_ref[comp, :, :list_rows] = drift_factor * flow_ref[comp, :, :list_rows]
    full = (groups, tiles, 8, LANES)

    def spread(ref, kind, row):
        lines = [ref[kind, tile, pl.ds(row, 8, stride=0), :] for tile in range(tiles)]
        return jnp.broadcast_to(jnp.stack(lines)[None], full)

    def wide(kind):
        return jnp.broadcast_to(trig_ref[kind][:, None], full)

    cross, sin2, cos2 = wide(2), wide(3), wide(4)
    for row in range(inner):
        turn = cross * spread(grad_ref, 0, row) + sin2 * spread(grad_ref, 1, row) - cos2 * spread(grad_ref, 2, row)
        turn_ref[0, row] = jnp.maximum(turn, 0.0)
        turn_ref[1, row] = jnp.minimum(turn, 0.0)
    sum_ref[...] = jnp.zeros_like(sum_ref)
    start = index * freqs

    def one_frequency(freq, carry):
        speed = speed_ref[start + freq]
        speed_cos = jnp.broadcast_to((speed * trig_ref[0])[:, None], full)
        speed_sin = jnp.broadcast_to((speed * trig_ref[1])[:, None], full)
        source, sink = row_view(field_ref, freq), row_view(out_ref, freq)

        def cells(row):
            if row < 0:
                return low_ref[pl.ds((freq * 2 + 2 + row) * groups, groups)]
            if row >= wave_rows:
                return high_ref[pl.ds((freq * 2 + row - wave_rows) * groups, groups)]
            return load_row(source, groups, tiles, row)

        def north(row, fresh):
            if not fresh:
                return speeds_ref[2, row + 1], speeds_ref[3, row + 1]
            value = speed_sin + spread(flow_ref, 1, row + 2)
            up, down = jnp.maximum(value, 0.0), jnp.minimum(value, 0.0)
            if 0 <= row + 1 < wave_rows + 2:
                speeds_ref[2, row + 1], speeds_ref[3, row + 1] = up, down
            return up, down

        def east(row, fresh):
            if not fresh:
                return speeds_ref[0, row + 1], speeds_ref[1, row + 1]
            value = speed_cos + spread(flow_ref, 0, row + 2)
            up, down = jnp.maximum(value, 0.0), jnp.minimum(value, 0.0)
            if 0 <= row < wave_rows:
                speeds_ref[0, row + 1], speeds_ref[1, row + 1] = up, down
            return up, down

        def sweep(read, fresh, low, high, write):
            before = read(low - 1)
            here = read(low)
            up, down = north(low, fresh)
            face_before = north(low - 1, fresh)[0] * before + down * here
            for row in range(low, high):
                after = read(row + 1)
                up_after, down_after = north(row + 1, fresh)
                face_here = up * here + down_after * after
                right, left = east(row, fresh)
                face_x = right * here + roll_lanes(left * here, -1)
                face_turn = turn_ref[0, row + 1] * here + roll_directions(turn_ref[1, row + 1] * here, -1)
                write(
                    row,
                    here
                    - (face_x - roll_lanes(face_x, 1))
                    - (face_here - face_before)
                    - (face_turn - roll_directions(face_turn, 1)),
                )
                face_before, here, up = face_here, after, up_after

        def keep(row, value):
            mid_ref[row + 1] = value

        sweep(cells, True, -1, wave_rows + 1, keep)
        ratio = 0.5 + 0.5 * (start + freq).astype(jnp.float32) / (total_freq - 1)
        amplitude = energy_ref[start + freq] / math.sqrt(directions * total_freq)
        scale, rest = amplitude * ratio, amplitude * (ratio - 0.5)

        def finish(row, value):
            store_row(sink, row, value)
            plain = jnp.sum(value, axis=0)
            weighted = jnp.sum(cos2 * value, axis=0)
            mixed = jnp.sum(cross * value, axis=0)
            sum_ref[0, row] += scale * weighted + rest * plain
            sum_ref[1, row] += scale * (plain - weighted) + rest * plain
            sum_ref[2, row] += scale * mixed

        sweep(lambda row: mid_ref[row + 1], False, 0, wave_rows, finish)
        return carry

    lax.fori_loop(0, freqs, one_frequency, 0)
    for kind in range(3):
        for row in range(wave_rows):
            line = jnp.sum(sum_ref[kind, row], axis=1, keepdims=True)
            for tile in range(tiles):
                stress_ref[kind, tile, row : row + 1] = line[tile]


def stress_column(own, prev, half):
    return prev[prev.shape[0] - half - 2 :], own[: half + 1]


def edge_tile(after, before):
    lane = lax.broadcasted_iota(jnp.int32, after.shape, after.ndim - 1)
    return jnp.where(lane < LANES // 2, after, before)


def pair_kernel(axis, own_ref, x_ref, z_ref, xz_ref, keep_ref, send_ref):
    kinds, tiles, wave_rows, _ = own_ref.shape
    half = wave_rows // 2
    index = lax.axis_index(axis)
    for target, out_ref in ((index, keep_ref), (index ^ 2, send_ref)):
        after = lax.rem(target + 1, tiles)
        before = lax.rem(target + tiles - 1, tiles)
        for kind in range(kinds):

            def own(tile):
                return own_ref[kind, tile] + x_ref[kind, tile]

            def prev(tile):
                return z_ref[kind, tile] + xz_ref[kind, tile]

            upper, lower = stress_column(own(target), prev(target), half)
            out_ref[0, kind, 0 : half + 2] = upper
            out_ref[0, kind, half + 2 : wave_rows + 3] = lower
            upper, lower = stress_column(
                edge_tile(own(after), own(before)), edge_tile(prev(after), prev(before)), half
            )
            out_ref[1, kind, 0 : half + 2] = upper
            out_ref[1, kind, half + 2 : wave_rows + 3] = lower


def settle_kernel(axis, aligned, tail_rows, field_ref, low_ref, table_ref, out_hbm, coupling_ref, sem):
    copy = pltpu.make_async_copy(field_ref, out_hbm, sem)
    copy.start()
    freqs, directions, tiles, wave_rows, _ = field_ref.shape
    lead = freqs * 2 * (directions // 8)
    count = wave_rows + 1
    for which, tile in enumerate(chosen_tiles(axis, aligned, tiles)):
        for place in range(9):
            for row in range(tail_rows):
                block, at, line = tail_slot(tiles, which, place * tail_rows + row)
                coupling_ref[which, place, row : row + 1, :] = low_ref[lead + block, at, line : line + 1, :]
            coupling_ref[which, place, tail_rows:count] = table_ref[place, tile, 0 : count - tail_rows]
    copy.wait()


def push_tile(stress_ref, coupling_ref, here, edge, push_ref, count):
    lane = lax.broadcasted_iota(jnp.int32, (count, LANES), 1)

    def middle(part, kind):
        return stress_ref[part, kind, 1 : 1 + count]

    def along_y(part, kind):
        return (stress_ref[part, kind, 2 : 2 + count] - stress_ref[part, kind, 0:count]) * 0.5

    def along_x(part, kind):
        tile, rim = middle(0, kind), middle(1, kind)
        after = jnp.where(lane == LANES - 1, pltpu.roll(rim, LANES - 1, 1), pltpu.roll(tile, LANES - 1, 1))
        if part == 0:
            before = jnp.where(lane == 0, pltpu.roll(rim, 1, 1), pltpu.roll(tile, 1, 1))
            return (after - before) * 0.5
        return (pltpu.roll(tile, LANES - 1, 1) - pltpu.roll(rim, 1, 1)) * 0.5

    def forces(part):
        return (
            -(along_x(part, 0) + along_y(part, 2)),
            -(along_x(part, 2) + along_y(part, 1)),
        )

    inner, rim = forces(0), forces(1)
    result = []
    for comp in range(2):
        for place in range(9):
            value = coupling_ref[here, place, :count] * inner[comp]
            if place % 3 == 2:
                spill = coupling_ref[edge, place, :count] * rim[comp]
                value = jnp.where(lane == 0, pltpu.roll(spill, 1, 1), pltpu.roll(value, 1, 1))
            push_ref[place, :count] = value
        near = [push_ref[place, 1:count] for place in range(9)]
        far = [push_ref[place, 0 : count - 1] for place in range(9)]
        result.append(
            (
                (near[0] + far[6] + near[2] + far[8], near[1] + far[7]),
                (near[3] + near[5], near[4]),
            )
        )
    return result


def force_kernel(keep_ref, come_ref, coupling_ref, masked_ref, wet_ref, out_ref, stress_ref, push_ref, merge_ref):
    ocean_rows, width = wet_ref.shape
    wave_rows = ocean_rows // 2
    count = wave_rows + 1
    stress_ref[...] = keep_ref[...] + come_ref[...]
    pushed = push_tile(stress_ref, coupling_ref, 0, 1, push_ref, count)
    cells = jnp.concatenate(
        [
            jnp.concatenate([even, odd], axis=1)
            for component in pushed
            for even, odd in component
        ],
        axis=0,
    )
    merged = jnp.dot(
        cells, merge_matrix(width), precision=HIGHEST, preferred_element_type=jnp.float32
    ).reshape(2, 2, wave_rows, width)
    wet = wet_ref[...]
    for comp in range(2):
        for tile in range(width // LANES):
            lanes = slice(tile * LANES, (tile + 1) * LANES)
            for parity in range(2):
                lines = pl.ds(parity, wave_rows, stride=2)
                merge_ref[comp, tile, lines, :] = merged[comp, parity, :, lanes]
            out_ref[comp, :, lanes] = (
                damping * masked_ref[comp, :, lanes] + force_gain * wet[:, lanes] * merge_ref[comp, tile]
            )


def push_all_kernel(own_ref, prev_ref, coupling_ref, out_ref, stress_ref, push_ref):
    kinds, tiles, wave_rows, _ = own_ref.shape
    half = wave_rows // 2
    for tile in range(tiles):
        after, before = (tile + 1) % tiles, (tile - 1) % tiles
        for kind in range(kinds):
            upper, lower = stress_column(own_ref[kind, tile], prev_ref[kind, tile], half)
            stress_ref[0, kind, 0 : half + 2] = upper
            stress_ref[0, kind, half + 2 : wave_rows + 3] = lower
            upper, lower = stress_column(
                edge_tile(own_ref[kind, after], own_ref[kind, before]),
                edge_tile(prev_ref[kind, after], prev_ref[kind, before]),
                half,
            )
            stress_ref[1, kind, 0 : half + 2] = upper
            stress_ref[1, kind, half + 2 : wave_rows + 3] = lower
        pushed = push_tile(stress_ref, coupling_ref, tile, before, push_ref, wave_rows + 1)
        for comp in range(2):
            for parity in range(2):
                for side in range(2):
                    out_ref[side, comp, parity, tile] = pushed[comp][parity][side]


def call(kernel, outs, ins, out_specs=None, **kw):
    f32 = jnp.float32
    shapes = tuple(jax.ShapeDtypeStruct(shape, f32) for shape in outs)
    if out_specs is None:
        out_specs = (VMEM,) * len(outs)
    return pl.pallas_call(kernel, out_shape=shapes, in_specs=ins, out_specs=out_specs, compiler_params=params(), **kw)


def window(action, currents, wet, courant, energy, src, weights):
    f32 = jnp.float32
    freqs, directions, wave_rows, columns = action.shape
    groups, tiles = directions // 8, columns // LANES
    list_rows = src.shape[0]
    ocean_rows, width = wet.shape
    spec = lax.axis_size("spec")
    ocean_cols = width * spec
    aligned = width == 2 * LANES and spec == 4
    tail_rows = wave_rows // 2 - 1
    lead = freqs * 2 * groups
    chosen = 2 if aligned else tiles
    padded = -(-list_rows // 8) * 8
    first = wave_rows - 4
    field = jnp.transpose(action.reshape(freqs, directions, wave_rows, tiles, LANES), (0, 1, 3, 2, 4))
    source, weight = jnp.transpose(src, (0, 2, 1)), jnp.transpose(weights, (0, 2, 1))
    masked, wet_float, tables, held, low, high = call(
        functools.partial(open_kernel, ocean_cols, tail_rows, "spec", aligned),
        (
            currents.shape,
            wet.shape,
            (9, tiles, padded, LANES),
            field.shape,
            (lead + -(-chosen * TAIL_VREGS // tiles), tiles, 8, LANES),
            (lead, tiles, 8, LANES),
        ),
        [HBM] * 5,
        scratch_shapes=[
            pltpu.VMEM(currents.shape, f32),
            pltpu.VMEM(wet.shape, jnp.int32),
            pltpu.VMEM(source.shape, jnp.int32),
            pltpu.VMEM(weight.shape, f32),
            pltpu.SemaphoreType.DMA((5,)),
        ],
    )(*(pltpu.with_memory_space_constraint(x, pltpu.MemorySpace.HBM) for x in (currents, wet, source, weight, field)))
    if aligned:
        z = from_mesh(masked, 1, 0)
        xz = from_mesh(masked, 1, 1)
        x = from_mesh(masked, 0, 1)
    else:
        z = from_offset(masked, "space", 1)
    low = from_offset(low, "space", -1)
    high = from_offset(high, "space", 1)
    if aligned:
        (part,) = call(
            functools.partial(flow_kernel, "spec", list_rows, first),
            ((3, 2, padded, LANES),),
            [VMEM] * 5,
            scratch_shapes=[pltpu.VMEM((2, 2, 2, 2 * ocean_rows, LANES), f32)],
        )(masked, x, z, xz, tables)
        parts = [part, from_mesh(part, 0, 2)]
    else:
        both = lax.all_gather(jnp.concatenate([masked, z], axis=1), "spec", axis=2, tiled=True)
        ocean = both.reshape(2, 2 * ocean_rows, tiles, LANES, 2).transpose(4, 2, 0, 1, 3)
        parts = call(
            functools.partial(flow_all_kernel, list_rows, first), ((tiles, 2, padded, LANES),), [VMEM] * 2
        )(ocean, tables)
    angles = 2.0 * math.pi * (np.arange(directions) + 0.5) / directions
    cosine, sine = np.cos(angles), np.sin(angles)
    trig = np.stack([cosine, sine, sine * cosine, sine * sine, cosine * cosine]).astype(np.float32)
    trig = trig.reshape(5, 8, groups).transpose(0, 2, 1)
    trig = jnp.asarray(np.repeat(trig[:, :, :, None], LANES, axis=3))
    cell = (groups, tiles, 8, LANES)
    moved, stress = call(
        functools.partial(advance_kernel, freqs * spec, "spec", list_rows, len(parts)),
        (field.shape, (3, tiles, wave_rows, LANES)),
        [VMEM] * (len(parts) + 1) + [SMEM] * 2 + [VMEM] * 3,
        scratch_shapes=[
            pltpu.VMEM((2, tiles, padded, LANES), f32),
            pltpu.VMEM((3, tiles, padded, LANES), f32),
            pltpu.VMEM((2, list_rows - 2) + cell, f32),
            pltpu.VMEM((wave_rows + 2,) + cell, f32),
            pltpu.VMEM((3, wave_rows, tiles, 8, LANES), f32),
            pltpu.VMEM((4, wave_rows + 2) + cell, f32),
        ],
    )(*parts, trig, courant, energy, held, low, high)
    if aligned:
        z = from_mesh(stress, -1, 0)
        xz = from_mesh(stress, -1, 1)
        x = from_mesh(stress, 0, 1)
    out_field, coupling = call(
        functools.partial(settle_kernel, "spec", aligned, tail_rows),
        (field.shape, (chosen, 9, 2 * wave_rows, LANES)),
        [VMEM] * 3,
        out_specs=(HBM, VMEM),
        scratch_shapes=[pltpu.SemaphoreType.DMA(())],
    )(moved, low, tables)
    new_action = jnp.transpose(out_field, (0, 1, 3, 2, 4)).reshape(action.shape)
    column = (2, 3, 2 * wave_rows, LANES)
    scratch = [pltpu.VMEM(column, f32), pltpu.VMEM((9, 2 * wave_rows, LANES), f32)]
    if aligned:
        keep, send = call(functools.partial(pair_kernel, "spec"), (column, column), [VMEM] * 4)(stress, x, z, xz)
        come = from_mesh(send, 0, 2)
        (updated,) = call(
            force_kernel,
            (currents.shape,),
            [VMEM] * 5,
            scratch_shapes=scratch + [pltpu.VMEM((2, width // LANES, ocean_rows, LANES), f32)],
        )(keep, come, coupling, masked, wet_float)
    else:
        stress = lax.psum(stress, "spec")
        prev = from_offset(stress, "space", -1)
        (pushed,) = call(
            push_all_kernel, ((2, 2, 2, tiles, wave_rows, LANES),), [VMEM] * 3, scratch_shapes=scratch
        )(stress, prev, coupling)
        grid = jnp.transpose(pushed, (1, 4, 2, 3, 5, 0)).reshape(2, ocean_rows, ocean_cols)
        share = lax.dynamic_slice_in_dim(grid, lax.axis_index("spec") * width, width, 2)
        updated = damping * masked + force_gain * wet_float[None] * share
    return (new_action, updated)


def solution(mesh):
    in_specs = (
        P("spec", None, "space", None),
        P(None, "space", "spec"),
        P("space", "spec"),
        P(),
        P(),
        P("space", None, None),
        P("space", None, None),
    )
    out_specs = (P("spec", None, "space", None), P(None, "space", "spec"))
    return jax.shard_map(window, mesh=mesh, in_specs=in_specs, out_specs=out_specs, check_vma=False)
```

time: 47 us -> 40.9 us (0.87)
  waiting for transfers between devices: 19.7 us -> 12.6 us
  local copies, waits for them, and re-layouts: 3.22 us -> 0.02 us
  starting transfers between devices: 12.5 us -> 15.5 us
  Pallas kernels: 10.6 us -> 11.9 us
    ppermute x4 -> x2, waiting for transfers between devices: 13.1 us -> 0.01 us  [from_offset(): lax.ppermute(block, axis, [((i + offset) % count, i) for i in range(count)])]
    ppermute x6 -> x8, waiting for transfers between devices: 6.68 us -> 12.6 us  [from_mesh(): return lax.ppermute(block, ('space', 'spec'), route)]
    ppermute x6 -> x8, starting transfers between devices: 7.04 us -> 10.9 us  [from_mesh(): return lax.ppermute(block, ('space', 'spec'), route)]
    unnamed x18 -> x6, local copies, waits for them, and re-layouts: 3.22 us -> 0.02 us
    pallas_call x4 -> x6, Pallas kernels: 10.6 us -> 11.9 us  [the longest x1 7.22 us: window(): call(functools.partial(advance_kernel, freqs * spec, 'spec', list_rows, l...]
    ppermute x4 -> x2, starting transfers between devices: 5.42 us -> 4.64 us  [from_offset(): lax.ppermute(block, axis, [((i + offset) % count, i) for i in range(count)])]
  transfers between devices with their start and end apart: 10 -> 10, of which waited for: 8 -> 6; matrix products, arithmetic and copies ran while one was open for 0% -> 0% of each run, Pallas kernels for 1% -> 4%
where the time goes in v1:
time: 40.9 us; the launch traced here: 40.7 us
  starting transfers between devices  15.5 us (38%)
  waiting for transfers between devices  12.6 us (31%)
  Pallas kernels  11.9 us (29%)
  between operations  0.72 us (2%)
    ppermute x8, waiting for transfers between devices, from_mesh(): return lax.ppermute(block, ('space', 'spec'), route)  12.6 us
    ppermute x8, starting transfers between devices, from_mesh(): return lax.ppermute(block, ('space', 'spec'), route)  10.9 us
    pallas_call x1, Pallas kernels, window(): call(functools.partial(advance_kernel, freqs * spec, 'spec', list_rows, l...  7.22 us
    ppermute x2, starting transfers between devices, from_offset(): lax.ppermute(block, axis, [((i + offset) % count, i) for i in range(count)])  4.64 us
    pallas_call x1, Pallas kernels, window(): call(functools.partial(open_kernel, ocean_cols, tail_rows, 'spec', aligne...  2.08 us
    pallas_call x1, Pallas kernels, window(): call(functools.partial(settle_kernel, 'spec', aligned, tail_rows), (field...  1.15 us
    pallas_call x1, Pallas kernels, window(): call(force_kernel, (currents.shape,), [VMEM] * 5, scratch_shapes=scratch...  0.99 us
  transfers between devices with their start and end apart: 10, of which 6 were waited for; matrix products, arithmetic and copies ran while one was open for 0% of the time, Pallas kernels for 4%

profile of v1, /device:TPU:0, one launch (start us, length us, event | category | flops | bytes accessed | tf_op | source)
XLA Modules:
  0.0 40.7 jit_solution(10711598444775616523)
XLA Ops:
  0.6 0.0 copy-start
  0.6 0.0 copy-start.2
  0.7 0.0 copy-start.1
  0.7 2.1 %shard_map.95 = (f32[2,16,256]{2,1,0:T(8,128)S(1)}, f32[16,256]{1,0:T(8,128)S(1)}, f32[9,4,16,128]{3,2,1,0:T(8,128)S(1)}, f32[4,24,4,8,128]{4,3,2,1,0:T(8,128)S(...) custom-call(f32[2,16,256]{2,1,0:T(8,128)} %current_hbm.1, s32[16,256]{1,0:T(8,128)} %wet_hbm.1, ...), custom_call_target="tpu_custom_call" | custom-call | tf_op jit(solution)/shard_map/pallas_call | solution.py:547
  2.8 0.5 %collective-permute-start.4 = (f32[26,4,8,128]{3,2,1,0:T(8,128)S(1)}, f32[26,4,8,128]{3,2,1,0:T(8,128)S(1)}, u32[]{:S(2)}, u32[]{:S(2)}) collective-permute-start(f32[26,4,8,128]{3,2,1,0:T(8,128)S(1)} %get-tuple-element.17), channel_id=1, source_target_pairs={{28,0},{0,4},{4,8},{8,12},{12,16},{16,20},{20,24},{24,28},{29,1},{... | collective-permute-start | bytes 1277960 | tf_op jit(solution)/shard_map/ppermute | solution.py:28
  3.3 4.1 %collective-permute-start.5 = (f32[24,4,8,128]{3,2,1,0:T(8,128)S(1)}, f32[24,4,8,128]{3,2,1,0:T(8,128)S(1)}, u32[]{:S(2)}, u32[]{:S(2)}) collective-permute-start(f32[24,4,8,128]{3,2,1,0:T(8,128)S(1)} %get-tuple-element.18), channel_id=1, source_target_pairs={{4,0},{8,4},{12,8},{16,12},{20,16},{24,20},{28,24},{0,28},{5,1},{9... | collective-permute-start | bytes 1179656 | tf_op jit(solution)/shard_map/ppermute | solution.py:28
  7.4 1.6 %collective-permute-start.2 = (f32[2,16,256]{2,1,0:T(8,128)S(1)}, f32[2,16,256]{2,1,0:T(8,128)S(1)}, u32[]{:S(2)}, u32[]{:S(2)}) collective-permute-start(f32[2,16,256]{2,1,0:T(8,128)S(1)} %get-tuple-element.14.own_ref.masked_ref), channel_id=1, source_target_pairs={{5,0},{4,1},{7,2},{6,3},{9,4},{8,5},{11,6},{10,7},{13,8},{12,9},{1... | collective-permute-start | bytes 98312 | tf_op jit(solution)/shard_map/ppermute | solution.py:36
  9.0 1.8 %collective-permute-start.1 = (f32[2,16,256]{2,1,0:T(8,128)S(1)}, f32[2,16,256]{2,1,0:T(8,128)S(1)}, u32[]{:S(2)}, u32[]{:S(2)}) collective-permute-start(f32[2,16,256]{2,1,0:T(8,128)S(1)} %get-tuple-element.14.own_ref.masked_ref), channel_id=1, source_target_pairs={{4,0},{5,1},{6,2},{7,3},{8,4},{9,5},{10,6},{11,7},{12,8},{13,9},{1... | collective-permute-start | bytes 98312 | tf_op jit(solution)/shard_map/ppermute | solution.py:36
  10.8 0.5 %collective-permute-start = (f32[2,16,256]{2,1,0:T(8,128)S(1)}, f32[2,16,256]{2,1,0:T(8,128)S(1)}, u32[]{:S(2)}, u32[]{:S(2)}) collective-permute-start(f32[2,16,256]{2,1,0:T(8,128)S(1)} %get-tuple-element.14.own_ref.masked_ref), channel_id=1, source_target_pairs={{1,0},{0,1},{3,2},{2,3},{5,4},{4,5},{7,6},{6,7},{9,8},{8,9},{11,10... | collective-permute-start | bytes 98312 | tf_op jit(solution)/shard_map/ppermute | solution.py:36
  11.4 4.2 %collective-permute-done.2.xz_ref = f32[2,16,256]{2,1,0:T(8,128)S(1)} collective-permute-done((f32[2,16,256]{2,1,0:T(8,128)S(1)}, f32[2,16,256]{2,1,0:T(8,128)S(1)}, u32[]{:S(2)}, u32[]{:S(2)}) %collective-permute-start.2) | collective-permute-done | bytes 32800 | tf_op jit(solution)/shard_map/ppermute | solution.py:36
  15.5 0.4 collective-permute-done.1.z_ref
  15.9 0.0 collective-permute-done.x_ref
  15.9 0.4 shard_map.96.refs_0_
  16.3 1.6 %collective-permute-start.3 = (f32[3,2,16,128]{3,2,1,0:T(8,128)S(1)}, f32[3,2,16,128]{3,2,1,0:T(8,128)S(1)}, u32[]{:S(2)}, u32[]{:S(2)}) collective-permute-start(f32[3,2,16,128]{3,2,1,0:T(8,128)S(1)} %shard_map.96.refs_0_), channel_id=1, source_target_pairs={{2,0},{3,1},{0,2},{1,3},{6,4},{7,5},{4,6},{5,7},{10,8},{11,9},{8,1... | collective-permute-start | bytes 147464 | tf_op jit(solution)/shard_map/ppermute | solution.py:36
  17.9 2.6 %collective-permute-done.3.refs_1_ = f32[3,2,16,128]{3,2,1,0:T(8,128)S(1)} collective-permute-done((f32[3,2,16,128]{3,2,1,0:T(8,128)S(1)}, f32[3,2,16,128]{3,2,1,0:T(8,128)S(1)}, u32[]{:S(2)}, u32[]{:S(2)}) %collective-permute-start.3) | collective-permute-done | bytes 49184 | tf_op jit(solution)/shard_map/ppermute | solution.py:36
  20.4 0.0 collective-permute-done.5.refs_7_
  20.4 0.0 collective-permute-done.4.refs_6_.low_ref
  20.5 0.0 copy-done
  20.5 0.0 copy-done.2
  20.5 0.0 copy-done.1
  20.5 7.2 %shard_map.97 = (f32[4,24,4,8,128]{4,3,2,1,0:T(8,128)S(1)}, f32[3,4,8,128]{3,2,1,0:T(8,128)S(1)}) custom-call(f32[3,2,16,128]{3,2,1,0:T(8,128)S(1)} %shard_map.96.refs_0_, f32[3,2,16,128]{3,2,1,0:T(8,128)S(1)} %collective-permute-done.3.refs_1_, f32[5,3,8,128]{3,2,1,0:T(8,128)S(1)} %copy-done, f32[16]{0:T(128)S(1)} %copy-done.1, f32[16]{0:T(128)S(1)} %copy-done.2, ...), custom_call_target="tpu_custom_call" | custom-call | tf_op jit(solution)/shard_map/pallas_call | solution.py:594
  27.7 2.5 %collective-permute-start.8 = (f32[3,4,8,128]{3,2,1,0:T(8,128)S(1)}, f32[3,4,8,128]{3,2,1,0:T(8,128)S(1)}, u32[]{:S(2)}, u32[]{:S(2)}) collective-permute-start(f32[3,4,8,128]{3,2,1,0:T(8,128)S(1)} %get-tuple-element.21.own_ref), channel_id=1, source_target_pairs={{29,0},{28,1},{31,2},{30,3},{1,4},{0,5},{3,6},{2,7},{5,8},{4,9},{7... | collective-permute-start | bytes 147464 | tf_op jit(solution)/shard_map/ppermute | solution.py:36
  30.2 1.2 %collective-permute-start.7 = (f32[3,4,8,128]{3,2,1,0:T(8,128)S(1)}, f32[3,4,8,128]{3,2,1,0:T(8,128)S(1)}, u32[]{:S(2)}, u32[]{:S(2)}) collective-permute-start(f32[3,4,8,128]{3,2,1,0:T(8,128)S(1)} %get-tuple-element.21.own_ref), channel_id=1, source_target_pairs={{28,0},{29,1},{30,2},{31,3},{0,4},{1,5},{2,6},{3,7},{4,8},{5,9},{6... | collective-permute-start | bytes 147464 | tf_op jit(solution)/shard_map/ppermute | solution.py:36
  31.4 0.0 collective-permute-start.6
  31.4 2.6 %collective-permute-done.8.xz_ref = f32[3,4,8,128]{3,2,1,0:T(8,128)S(1)} collective-permute-done((f32[3,4,8,128]{3,2,1,0:T(8,128)S(1)}, f32[3,4,8,128]{3,2,1,0:T(8,128)S(1)}, u32[]{:S(2)}, u32[]{:S(2)}) %collective-permute-start.8) | collective-permute-done | bytes 49184 | tf_op jit(solution)/shard_map/ppermute | solution.py:36
  34.0 1.5 %collective-permute-done.7.z_ref = f32[3,4,8,128]{3,2,1,0:T(8,128)S(1)} collective-permute-done((f32[3,4,8,128]{3,2,1,0:T(8,128)S(1)}, f32[3,4,8,128]{3,2,1,0:T(8,128)S(1)}, u32[]{:S(2)}, u32[]{:S(2)}) %collective-permute-start.7) | collective-permute-done | bytes 49184 | tf_op jit(solution)/shard_map/ppermute | solution.py:36
  35.5 0.0 collective-permute-done.6.x_ref
  35.5 1.6 %collective-permute-start.9 = (f32[2,3,16,128]{3,2,1,0:T(8,128)S(1)}, f32[2,3,16,128]{3,2,1,0:T(8,128)S(1)}, u32[]{:S(2)}, u32[]{:S(2)}) collective-permute-start(f32[2,3,16,128]{3,2,1,0:T(8,128)S(1)} %get-tuple-element.23), channel_id=1, source_target_pairs={{2,0},{3,1},{0,2},{1,3},{6,4},{7,5},{4,6},{5,7},{10,8},{11,9},{8,1... | collective-permute-start | bytes 147464 | tf_op jit(solution)/shard_map/ppermute | solution.py:36
  37.1 1.2 %shard_map.98 = (f32[4,24,4,8,128]{4,3,2,1,0:T(8,128)}, f32[2,9,16,128]{3,2,1,0:T(8,128)S(1)}) custom-call(f32[4,24,4,8,128]{4,3,2,1,0:T(8,128)S(1)} %get-tuple-element.19.field_ref, f32[26,4,8,128]{3,2,1,0:T(8,128)S(1)} %collective-permute-done.4.refs_6_.low_ref, f32[9,4,16,128]{3,2,1,0:T(8,128)S(1)} %get-tuple-element.15.table_ref), custom_call_target="tpu_custom_call" | custom-call | tf_op jit(solution)/shard_map/pallas_call | solution.py:611
  38.3 1.4 %collective-permute-done.9.come_ref = f32[2,3,16,128]{3,2,1,0:T(8,128)S(1)} collective-permute-done((f32[2,3,16,128]{3,2,1,0:T(8,128)S(1)}, f32[2,3,16,128]{3,2,1,0:T(8,128)S(1)}, u32[]{:S(2)}, u32[]{:S(2)}) %collective-permute-start.9) | collective-permute-done | bytes 49184 | tf_op jit(solution)/shard_map/ppermute | solution.py:36
  39.7 1.0 %shard_map.100 = f32[2,16,256]{2,1,0:T(8,128)} custom-call(f32[2,3,16,128]{3,2,1,0:T(8,128)S(1)} %get-tuple-element.22.keep_ref, f32[2,3,16,128]{3,2,1,0:T(8,128)S(1)} %collective-permute-done.9.come_ref, f32[2,9,16,128]{3,2,1,0:T(8,128)S(1)} %get-tuple-element.24.coupling_ref, f32[2,16,256]{2,1,0:T(8,128)S(1)} %get-tuple-element.14.own_ref.masked_ref, ...), custom_call_target="tpu_custom_call" | custom-call | tf_op jit(solution)/shard_map/pallas_call | solution.py:624
  (1 shorter events, 0.0 us)
Async XLA Ops:
  0.6 19.8 %copy-start = (f32[5,3,8,128]{3,2,1,0:T(8,128)S(1)}, f32[5,3,8,128]{3,2,1,0:T(8,128)}, u32[]{:S(2)}) copy-start(f32[5,3,8,128]{3,2,1,0:T(8,128)} %constant.2.clone.refs_2_) | copy-start | bytes 184324
  0.6 19.8 %copy-start.2 = (f32[16]{0:T(128)S(1)}, f32[16]{0:T(128)}, u32[]{:S(2)}) copy-start(f32[16]{0:T(128)} %refs_4_.1) | copy-start | bytes 196
  0.7 19.8 %copy-start.1 = (f32[16]{0:T(128)S(1)}, f32[16]{0:T(128)}, u32[]{:S(2)}) copy-start(f32[16]{0:T(128)} %refs_3_.1) | copy-start | bytes 196
  2.8 17.7 %collective-permute-start.4 = (f32[26,4,8,128]{3,2,1,0:T(8,128)S(1)}, f32[26,4,8,128]{3,2,1,0:T(8,128)S(1)}, u32[]{:S(2)}, u32[]{:S(2)}) collective-permute-start(f32[26,4,8,128]{3,2,1,0:T(8,128)S(1)} %get-tuple-element.17), channel_id=1, source_target_pairs={{28,0},{0,4},{4,8},{8,12},{12,16},{16,20},{20,24},{24,28},{29,1},{... | collective-permute-start | bytes 1277960 | tf_op jit(solution)/shard_map/ppermute | solution.py:28
  3.3 17.2 %collective-permute-start.5 = (f32[24,4,8,128]{3,2,1,0:T(8,128)S(1)}, f32[24,4,8,128]{3,2,1,0:T(8,128)S(1)}, u32[]{:S(2)}, u32[]{:S(2)}) collective-permute-start(f32[24,4,8,128]{3,2,1,0:T(8,128)S(1)} %get-tuple-element.18), channel_id=1, source_target_pairs={{4,0},{8,4},{12,8},{16,12},{20,16},{24,20},{28,24},{0,28},{5,1},{9... | collective-permute-start | bytes 1179656 | tf_op jit(solution)/shard_map/ppermute | solution.py:28
  7.4 8.2 %collective-permute-start.2 = (f32[2,16,256]{2,1,0:T(8,128)S(1)}, f32[2,16,256]{2,1,0:T(8,128)S(1)}, u32[]{:S(2)}, u32[]{:S(2)}) collective-permute-start(f32[2,16,256]{2,1,0:T(8,128)S(1)} %get-tuple-element.14.own_ref.masked_ref), channel_id=1, source_target_pairs={{5,0},{4,1},{7,2},{6,3},{9,4},{8,5},{11,6},{10,7},{13,8},{12,9},{1... | collective-permute-start | bytes 98312 | tf_op jit(solution)/shard_map/ppermute | solution.py:36
  9.0 6.9 %collective-permute-start.1 = (f32[2,16,256]{2,1,0:T(8,128)S(1)}, f32[2,16,256]{2,1,0:T(8,128)S(1)}, u32[]{:S(2)}, u32[]{:S(2)}) collective-permute-start(f32[2,16,256]{2,1,0:T(8,128)S(1)} %get-tuple-element.14.own_ref.masked_ref), channel_id=1, source_target_pairs={{4,0},{5,1},{6,2},{7,3},{8,4},{9,5},{10,6},{11,7},{12,8},{13,9},{1... | collective-permute-start | bytes 98312 | tf_op jit(solution)/shard_map/ppermute | solution.py:36
  10.8 5.1 %collective-permute-start = (f32[2,16,256]{2,1,0:T(8,128)S(1)}, f32[2,16,256]{2,1,0:T(8,128)S(1)}, u32[]{:S(2)}, u32[]{:S(2)}) collective-permute-start(f32[2,16,256]{2,1,0:T(8,128)S(1)} %get-tuple-element.14.own_ref.masked_ref), channel_id=1, source_target_pairs={{1,0},{0,1},{3,2},{2,3},{5,4},{4,5},{7,6},{6,7},{9,8},{8,9},{11,10... | collective-permute-start | bytes 98312 | tf_op jit(solution)/shard_map/ppermute | solution.py:36
  16.3 4.2 %collective-permute-start.3 = (f32[3,2,16,128]{3,2,1,0:T(8,128)S(1)}, f32[3,2,16,128]{3,2,1,0:T(8,128)S(1)}, u32[]{:S(2)}, u32[]{:S(2)}) collective-permute-start(f32[3,2,16,128]{3,2,1,0:T(8,128)S(1)} %shard_map.96.refs_0_), channel_id=1, source_target_pairs={{2,0},{3,1},{0,2},{1,3},{6,4},{7,5},{4,6},{5,7},{10,8},{11,9},{8,1... | collective-permute-start | bytes 147464 | tf_op jit(solution)/shard_map/ppermute | solution.py:36
  27.7 6.3 %collective-permute-start.8 = (f32[3,4,8,128]{3,2,1,0:T(8,128)S(1)}, f32[3,4,8,128]{3,2,1,0:T(8,128)S(1)}, u32[]{:S(2)}, u32[]{:S(2)}) collective-permute-start(f32[3,4,8,128]{3,2,1,0:T(8,128)S(1)} %get-tuple-element.21.own_ref), channel_id=1, source_target_pairs={{29,0},{28,1},{31,2},{30,3},{1,4},{0,5},{3,6},{2,7},{5,8},{4,9},{7... | collective-permute-start | bytes 147464 | tf_op jit(solution)/shard_map/ppermute | solution.py:36
  30.2 5.3 %collective-permute-start.7 = (f32[3,4,8,128]{3,2,1,0:T(8,128)S(1)}, f32[3,4,8,128]{3,2,1,0:T(8,128)S(1)}, u32[]{:S(2)}, u32[]{:S(2)}) collective-permute-start(f32[3,4,8,128]{3,2,1,0:T(8,128)S(1)} %get-tuple-element.21.own_ref), channel_id=1, source_target_pairs={{28,0},{29,1},{30,2},{31,3},{0,4},{1,5},{2,6},{3,7},{4,8},{5,9},{6... | collective-permute-start | bytes 147464 | tf_op jit(solution)/shard_map/ppermute | solution.py:36
  31.4 4.1 %collective-permute-start.6 = (f32[3,4,8,128]{3,2,1,0:T(8,128)S(1)}, f32[3,4,8,128]{3,2,1,0:T(8,128)S(1)}, u32[]{:S(2)}, u32[]{:S(2)}) collective-permute-start(f32[3,4,8,128]{3,2,1,0:T(8,128)S(1)} %get-tuple-element.21.own_ref), channel_id=1, source_target_pairs={{1,0},{0,1},{3,2},{2,3},{5,4},{4,5},{7,6},{6,7},{9,8},{8,9},{11,10... | collective-permute-start | bytes 147464 | tf_op jit(solution)/shard_map/ppermute | solution.py:36
  35.5 4.2 %collective-permute-start.9 = (f32[2,3,16,128]{3,2,1,0:T(8,128)S(1)}, f32[2,3,16,128]{3,2,1,0:T(8,128)S(1)}, u32[]{:S(2)}, u32[]{:S(2)}) collective-permute-start(f32[2,3,16,128]{3,2,1,0:T(8,128)S(1)} %get-tuple-element.23), channel_id=1, source_target_pairs={{2,0},{3,1},{0,2},{1,3},{6,4},{7,5},{4,6},{5,7},{10,8},{11,9},{8,1... | collective-permute-start | bytes 147464 | tf_op jit(solution)/shard_map/ppermute | solution.py:36

commit v2 on v1

--- a/solution.py
+++ b/solution.py
@@ -34,6 +34,15 @@
         (((i + offset) % space) * spec + (j ^ bits), i * spec + j) for i in range(space) for j in range(spec)
     ]
     return lax.ppermute(block, ("space", "spec"), route)
+
+
+def swap_pairs(block, axis, first):
+    count = lax.axis_size(axis)
+    route = []
+    for i in range(first, first + count, 2):
+        low, high = i % count, (i + 1) % count
+        route += [(low, high), (high, low)]
+    return lax.ppermute(block, axis, route)
 
 
 def params(**kw):
@@ -106,9 +115,8 @@
             view[slot, :] = value[group, tile]
 
 
-def tail_slot(tiles, which, slot):
-    vreg = which * TAIL_VREGS + slot // 8
-    return vreg // tiles, vreg % tiles, slot % 8
+def tail_slot(which, slot):
+    return which * TAIL_VREGS + slot // 8, slot % 8
 
 
 def chosen_tiles(axis, aligned, tiles):
@@ -119,25 +127,17 @@
 
 
 def open_kernel(
-    ocean_cols, tail_rows, axis, aligned, current_hbm, wet_hbm, src_hbm, weight_hbm, field_hbm,
-    masked_ref, wet_out, table_ref, field_ref, low_ref, high_ref,
-    current_ref, wet_ref, src_ref, weight_ref, sems,
+    axis, current_hbm, wet_hbm, field_hbm, masked_ref, wet_out, field_ref, near_ref, far_ref,
+    current_ref, wet_ref, sems,
 ):
     copies = [
         pltpu.make_async_copy(source, target, sems.at[k])
         for k, (source, target) in enumerate(
-            (
-                (current_hbm, current_ref),
-                (wet_hbm, wet_ref),
-                (src_hbm, src_ref),
-                (weight_hbm, weight_ref),
-                (field_hbm, field_ref),
-            )
+            ((current_hbm, current_ref), (wet_hbm, wet_ref), (field_hbm, field_ref))
         )
     ]
     for copy in copies:
         copy.start()
-    list_rows, corners, columns = src_ref.shape
     freqs, directions, tiles, wave_rows, _ = field_ref.shape
     groups = directions // 8
     copies[0].wait()
@@ -145,6 +145,29 @@
     wet = wet_ref[...].astype(jnp.float32)
     wet_out[...] = wet
     masked_ref[...] = current_ref[...] * wet[None]
+    odd = lax.rem(lax.axis_index(axis), 2)
+    last = wave_rows - 2
+    copies[2].wait()
+    for freq in range(freqs):
+        view = row_view(field_ref, freq)
+        for row in range(2):
+            at = (freq * 2 + row) * groups
+            near_ref[at : at + groups] = load_row(view, groups, tiles, last * (1 - odd) + row)
+            far_ref[at : at + groups] = load_row(view, groups, tiles, last * odd + row)
+
+
+def tables_kernel(
+    ocean_cols, wave_rows, tail_rows, axis, aligned, src_hbm, weight_hbm, table_ref, tail_ref,
+    src_ref, weight_ref, sems,
+):
+    copies = [
+        pltpu.make_async_copy(src_hbm, src_ref, sems.at[0]),
+        pltpu.make_async_copy(weight_hbm, weight_ref, sems.at[1]),
+    ]
+    for copy in copies:
+        copy.start()
+    list_rows, corners, columns = src_ref.shape
+    tiles = columns // LANES
     shape = (list_rows, columns)
     entry_row = lax.broadcasted_iota(jnp.int32, shape, 0)
     column = lax.broadcasted_iota(jnp.int32, shape, 1)
@@ -153,8 +176,8 @@
         base + jnp.where(2 * column + step >= ocean_cols, 2 * column + step - ocean_cols, 2 * column + step)
         for step in range(3)
     ]
-    copies[2].wait()
-    copies[3].wait()
+    for copy in copies:
+        copy.wait()
     sums = [jnp.zeros(shape, jnp.float32) for _ in range(9)]
     for corner in range(corners):
         source = src_ref[:, corner, :]
@@ -168,21 +191,11 @@
         for tile in range(tiles):
             table_ref[place, tile, :list_rows] = sums[place][:, tile * LANES : (tile + 1) * LANES]
     first = 2 + wave_rows // 2 - 1
-    lead = freqs * 2 * groups
     for which, tile in enumerate(chosen_tiles(axis, aligned, tiles)):
         for place in range(9):
             for row in range(tail_rows):
-                block, at, line = tail_slot(tiles, which, place * tail_rows + row)
-                low_ref[lead + block, at, line : line + 1, :] = table_ref[
-                    place, tile, first + row : first + row + 1, :
-                ]
-    copies[4].wait()
-    for freq in range(freqs):
-        view = row_view(field_ref, freq)
-        for row in range(2):
-            at = (freq * 2 + row) * groups
-            low_ref[at : at + groups] = load_row(view, groups, tiles, wave_rows - 2 + row)
-            high_ref[at : at + groups] = load_row(view, groups, tiles, row)
+                vreg, line = tail_slot(which, place * tail_rows + row)
+                tail_ref[vreg, line : line + 1, :] = table_ref[place, tile, first + row : first + row + 1, :]
 
 
 def flow_tile(table_ref, tile, evens, odds, nexts):
@@ -248,11 +261,75 @@
             )
 
 
-def advance_kernel(total_freq, axis, list_rows, parts, *refs):
+def spread_row(ref, lead, row, groups):
+    tiles = ref.shape[-3]
+    lines = [ref[(*lead, tile, pl.ds(row, 8, stride=0), slice(None))] for tile in range(tiles)]
+    return jnp.broadcast_to(jnp.stack(lines)[None], (groups, tiles, 8, LANES))
+
+
+class Speeds:
+    def __init__(self, speed, trig_ref, flow_ref, keep_ref):
+        groups, tiles = trig_ref.shape[1], flow_ref.shape[1]
+        shape = (groups, tiles, 8, LANES)
+        self.groups, self.flow_ref, self.keep_ref = groups, flow_ref, keep_ref
+        self.base = [jnp.broadcast_to((speed * trig_ref[k])[:, None], shape) for k in range(2)]
+        self.seen = set()
+
+    def parts(self, comp, row):
+        slot = row + 2
+        if (comp, row) in self.seen:
+            return self.keep_ref[2 * comp, slot], self.keep_ref[2 * comp + 1, slot]
+        value = self.base[comp] + spread_row(self.flow_ref, (comp,), slot, self.groups)
+        up, down = jnp.maximum(value, 0.0), jnp.minimum(value, 0.0)
+        self.keep_ref[2 * comp, slot], self.keep_ref[2 * comp + 1, slot] = up, down
+        self.seen.add((comp, row))
+        return up, down
+
+
+def sweep(read, speeds, turn_ref, low, high, write):
+    here = read(low)
+    up, down = speeds.parts(1, low)
+    face_before = speeds.parts(1, low - 1)[0] * read(low - 1) + down * here
+    for row in range(low, high):
+        after = read(row + 1)
+        up_after, down_after = speeds.parts(1, row + 1)
+        face_here = up * here + down_after * after
+        right, left = speeds.parts(0, row)
+        face_x = right * here + roll_lanes(left * here, -1)
+        face_turn = turn_ref[0, row + 1] * here + roll_directions(turn_ref[1, row + 1] * here, -1)
+        write(
+            row,
+            here
+            - (face_x - roll_lanes(face_x, 1))
+            - (face_here - face_before)
+            - (face_turn - roll_directions(face_turn, 1)),
+        )
+        face_before, here, up = face_here, after, up_after
+
+
+def add_stress(value, trig_ref, scale, rest, sum_ref, slot):
+    shape = value.shape
+    cross = jnp.broadcast_to(trig_ref[2][:, None], shape)
+    cos2 = jnp.broadcast_to(trig_ref[4][:, None], shape)
+    plain = jnp.sum(value, axis=0)
+    weighted = jnp.sum(cos2 * value, axis=0)
+    mixed = jnp.sum(cross * value, axis=0)
+    sum_ref[0, slot] += scale * weighted + rest * plain
+    sum_ref[1, slot] += scale * (plain - weighted) + rest * plain
+    sum_ref[2, slot] += scale * mixed
+
+
+def stress_scales(energy_ref, number, total_freq, directions):
+    ratio = 0.5 + 0.5 * number.astype(jnp.float32) / (total_freq - 1)
+    amplitude = energy_ref[number] / math.sqrt(directions * total_freq)
+    return amplitude * ratio, amplitude * (ratio - 0.5)
+
+
+def inner_kernel(total_freq, axis, list_rows, parts, *refs):
     part_refs = refs[:parts]
-    (trig_ref, speed_ref, energy_ref, field_ref, low_ref, high_ref) = refs[parts : parts + 6]
-    out_ref, stress_ref = refs[parts + 6 : parts + 8]
-    flow_ref, grad_ref, turn_ref, mid_ref, sum_ref, speeds_ref = refs[parts + 8 :]
+    (trig_ref, speed_ref, energy_ref, field_ref) = refs[parts : parts + 4]
+    flow_ref, turn_ref, mid_ref, out_ref, sum_ref = refs[parts + 4 : parts + 9]
+    grad_ref, keep_ref = refs[parts + 9 :]
     freqs, directions, tiles, wave_rows, _ = field_ref.shape
     groups = directions // 8
     index = lax.axis_index(axis)
@@ -279,99 +356,83 @@
     grad_ref[2, :, :inner] = refract_factor * north_x
     for comp in range(2):
         flow_ref[comp, :, :list_rows] = drift_factor * flow_ref[comp, :, :list_rows]
-    full = (groups, tiles, 8, LANES)
-
-    def spread(ref, kind, row):
-        lines = [ref[kind, tile, pl.ds(row, 8, stride=0), :] for tile in range(tiles)]
-        return jnp.broadcast_to(jnp.stack(lines)[None], full)
-
-    def wide(kind):
-        return jnp.broadcast_to(trig_ref[kind][:, None], full)
-
-    cross, sin2, cos2 = wide(2), wide(3), wide(4)
+    cross, sin2, cos2 = (
+        jnp.broadcast_to(trig_ref[k][:, None], (groups, tiles, 8, LANES)) for k in (2, 3, 4)
+    )
     for row in range(inner):
-        turn = cross * spread(grad_ref, 0, row) + sin2 * spread(grad_ref, 1, row) - cos2 * spread(grad_ref, 2, row)
+        first, second, third = (spread_row(grad_ref, (k,), row, groups) for k in range(3))
+        turn = cross * first + sin2 * second - cos2 * third
         turn_ref[0, row] = jnp.maximum(turn, 0.0)
         turn_ref[1, row] = jnp.minimum(turn, 0.0)
     sum_ref[...] = jnp.zeros_like(sum_ref)
     start = index * freqs
 
     def one_frequency(freq, carry):
-        speed = speed_ref[start + freq]
-        speed_cos = jnp.broadcast_to((speed * trig_ref[0])[:, None], full)
-        speed_sin = jnp.broadcast_to((speed * trig_ref[1])[:, None], full)
-        source, sink = row_view(field_ref, freq), row_view(out_ref, freq)
+        speeds = Speeds(speed_ref[start + freq], trig_ref, flow_ref, keep_ref)
+        source = row_view(field_ref, freq)
+
+        def keep(row, value):
+            mid_ref[freq, row - 1] = value
+
+        sweep(lambda row: load_row(source, groups, tiles, row), speeds, turn_ref, 1, wave_rows - 1, keep)
+        scale, rest = stress_scales(energy_ref, start + freq, total_freq, directions)
+
+        def finish(row, value):
+            out_ref[freq, row - 2] = value
+            add_stress(value, trig_ref, scale, rest, sum_ref, row - 2)
+
+        sweep(lambda row: mid_ref[freq, row - 1], speeds, turn_ref, 2, wave_rows - 2, finish)
+        return carry
+
+    lax.fori_loop(0, freqs, one_frequency, 0)
+
+
+def outer_kernel(
+    total_freq, axes, trig_ref, speed_ref, energy_ref, field_ref, near_ref, far_ref, flow_ref, turn_ref,
+    mid_ref, inner_ref, out_ref, stress_ref, rim_ref, sum_ref, keep_ref,
+):
+    freqs, directions, tiles, wave_rows, _ = field_ref.shape
+    groups = directions // 8
+    start = lax.axis_index(axes[1]) * freqs
+    odd = lax.rem(lax.axis_index(axes[0]), 2) == 1
+    sum_ref[...] = jnp.zeros_like(sum_ref)
+    rim = {-1: 0, 0: 1, wave_rows - 1: 2, wave_rows: 3}
+    last = {0: 0, 1: 1, wave_rows - 2: 2, wave_rows - 1: 3}
+
+    def one_frequency(freq, carry):
+        speeds = Speeds(speed_ref[start + freq], trig_ref, flow_ref, keep_ref)
+        source = row_view(field_ref, freq)
 
         def cells(row):
-            if row < 0:
-                return low_ref[pl.ds((freq * 2 + 2 + row) * groups, groups)]
-            if row >= wave_rows:
-                return high_ref[pl.ds((freq * 2 + row - wave_rows) * groups, groups)]
-            return load_row(source, groups, tiles, row)
-
-        def north(row, fresh):
-            if not fresh:
-                return speeds_ref[2, row + 1], speeds_ref[3, row + 1]
-            value = speed_sin + spread(flow_ref, 1, row + 2)
-            up, down = jnp.maximum(value, 0.0), jnp.minimum(value, 0.0)
-            if 0 <= row + 1 < wave_rows + 2:
-                speeds_ref[2, row + 1], speeds_ref[3, row + 1] = up, down
-            return up, down
-
-        def east(row, fresh):
-            if not fresh:
-                return speeds_ref[0, row + 1], speeds_ref[1, row + 1]
-            value = speed_cos + spread(flow_ref, 0, row + 2)
-            up, down = jnp.maximum(value, 0.0), jnp.minimum(value, 0.0)
             if 0 <= row < wave_rows:
-                speeds_ref[0, row + 1], speeds_ref[1, row + 1] = up, down
-            return up, down
-
-        def sweep(read, fresh, low, high, write):
-            before = read(low - 1)
-            here = read(low)
-            up, down = north(low, fresh)
-            face_before = north(low - 1, fresh)[0] * before + down * here
-            for row in range(low, high):
-                after = read(row + 1)
-                up_after, down_after = north(row + 1, fresh)
-                face_here = up * here + down_after * after
-                right, left = east(row, fresh)
-                face_x = right * here + roll_lanes(left * here, -1)
-                face_turn = turn_ref[0, row + 1] * here + roll_directions(turn_ref[1, row + 1] * here, -1)
-                write(
-                    row,
-                    here
-                    - (face_x - roll_lanes(face_x, 1))
-                    - (face_here - face_before)
-                    - (face_turn - roll_directions(face_turn, 1)),
-                )
-                face_before, here, up = face_here, after, up_after
+                return load_row(source, groups, tiles, row)
+            at = pl.ds((freq * 2 + row % 2) * groups, groups)
+            near, far = near_ref[at], far_ref[at]
+            return jnp.where(odd, near, far) if row < 0 else jnp.where(odd, far, near)
 
         def keep(row, value):
-            mid_ref[row + 1] = value
-
-        sweep(cells, True, -1, wave_rows + 1, keep)
-        ratio = 0.5 + 0.5 * (start + freq).astype(jnp.float32) / (total_freq - 1)
-        amplitude = energy_ref[start + freq] / math.sqrt(directions * total_freq)
-        scale, rest = amplitude * ratio, amplitude * (ratio - 0.5)
+            rim_ref[rim[row]] = value
+
+        def middle(row):
+            return rim_ref[rim[row]] if row in rim else mid_ref[freq, row - 1]
+
+        scale, rest = stress_scales(energy_ref, start + freq, total_freq, directions)
 
         def finish(row, value):
-            store_row(sink, row, value)
-            plain = jnp.sum(value, axis=0)
-            weighted = jnp.sum(cos2 * value, axis=0)
-            mixed = jnp.sum(cross * value, axis=0)
-            sum_ref[0, row] += scale * weighted + rest * plain
-            sum_ref[1, row] += scale * (plain - weighted) + rest * plain
-            sum_ref[2, row] += scale * mixed
-
-        sweep(lambda row: mid_ref[row + 1], False, 0, wave_rows, finish)
+            out_ref[freq, last[row]] = value
+            add_stress(value, trig_ref, scale, rest, sum_ref, last[row])
+
+        sweep(cells, speeds, turn_ref, -1, 1, keep)
+        sweep(cells, speeds, turn_ref, wave_rows - 1, wave_rows + 1, keep)
+        sweep(middle, speeds, turn_ref, 0, 2, finish)
+        sweep(middle, speeds, turn_ref, wave_rows - 2, wave_rows, finish)
         return carry
 
     lax.fori_loop(0, freqs, one_frequency, 0)
     for kind in range(3):
         for row in range(wave_rows):
-            line = jnp.sum(sum_ref[kind, row], axis=1, keepdims=True)
+            part = sum_ref[kind, last[row]] if row in last else inner_ref[kind, row - 2]
+            line = jnp.sum(part, axis=1, keepdims=True)
             for tile in range(tiles):
                 stress_ref[kind, tile, row : row + 1] = line[tile]
 
@@ -410,19 +471,29 @@
             out_ref[1, kind, half + 2 : wave_rows + 3] = lower
 
 
-def settle_kernel(axis, aligned, tail_rows, field_ref, low_ref, table_ref, out_hbm, coupling_ref, sem):
-    copy = pltpu.make_async_copy(field_ref, out_hbm, sem)
-    copy.start()
-    freqs, directions, tiles, wave_rows, _ = field_ref.shape
-    lead = freqs * 2 * (directions // 8)
+def settle_kernel(
+    axis, aligned, tail_rows, inner_ref, outer_ref, tail_ref, table_ref, out_hbm, coupling_ref, field_ref, sems
+):
+    freqs, _, tiles, wave_rows, _ = field_ref.shape
+    copies = []
+    for freq in range(freqs):
+        sink = row_view(field_ref, freq)
+        for row in range(wave_rows):
+            if 2 <= row < wave_rows - 2:
+                store_row(sink, row, inner_ref[freq, row - 2])
+            else:
+                store_row(sink, row, outer_ref[freq, row if row < 2 else row - wave_rows + 4])
+        copies.append(pltpu.make_async_copy(field_ref.at[freq], out_hbm.at[freq], sems.at[freq]))
+        copies[-1].start()
     count = wave_rows + 1
     for which, tile in enumerate(chosen_tiles(axis, aligned, tiles)):
         for place in range(9):
             for row in range(tail_rows):
-                block, at, line = tail_slot(tiles, which, place * tail_rows + row)
-                coupling_ref[which, place, row : row + 1, :] = low_ref[lead + block, at, line : line + 1, :]
+                vreg, line = tail_slot(which, place * tail_rows + row)
+                coupling_ref[which, place, row : row + 1, :] = tail_ref[vreg, line : line + 1, :]
             coupling_ref[which, place, tail_rows:count] = table_ref[place, tile, 0 : count - tail_rows]
-    copy.wait()
+    for copy in copies:
+        copy.wait()
 
 
 def push_tile(stress_ref, coupling_ref, here, edge, push_ref, count):
@@ -528,6 +599,10 @@
     return pl.pallas_call(kernel, out_shape=shapes, in_specs=ins, out_specs=out_specs, compiler_params=params(), **kw)
 
 
+def in_hbm(*arrays):
+    return [pltpu.with_memory_space_constraint(x, pltpu.MemorySpace.HBM) for x in arrays]
+
+
 def window(action, currents, wet, courant, energy, src, weights):
     f32 = jnp.float32
     freqs, directions, wave_rows, columns = action.shape
@@ -544,33 +619,36 @@
     first = wave_rows - 4
     field = jnp.transpose(action.reshape(freqs, directions, wave_rows, tiles, LANES), (0, 1, 3, 2, 4))
     source, weight = jnp.transpose(src, (0, 2, 1)), jnp.transpose(weights, (0, 2, 1))
-    masked, wet_float, tables, held, low, high = call(
-        functools.partial(open_kernel, ocean_cols, tail_rows, "spec", aligned),
-        (
-            currents.shape,
-            wet.shape,
-            (9, tiles, padded, LANES),
-            field.shape,
-            (lead + -(-chosen * TAIL_VREGS // tiles), tiles, 8, LANES),
-            (lead, tiles, 8, LANES),
-        ),
-        [HBM] * 5,
+    cell = (groups, tiles, 8, LANES)
+    masked, wet_float, held, near, far = call(
+        functools.partial(open_kernel, "space"),
+        (currents.shape, wet.shape, field.shape, (lead, tiles, 8, LANES), (lead, tiles, 8, LANES)),
+        [HBM] * 3,
         scratch_shapes=[
             pltpu.VMEM(currents.shape, f32),
             pltpu.VMEM(wet.shape, jnp.int32),
-            pltpu.VMEM(source.shape, jnp.int32),
-            pltpu.VMEM(weight.shape, f32),
-            pltpu.SemaphoreType.DMA((5,)),
+            pltpu.SemaphoreType.DMA((3,)),
         ],
-    )(*(pltpu.with_memory_space_constraint(x, pltpu.MemorySpace.HBM) for x in (currents, wet, source, weight, field)))
+    )(*in_hbm(currents, wet, field))
     if aligned:
+        xz = from_mesh(masked, 1, 1)
         z = from_mesh(masked, 1, 0)
-        xz = from_mesh(masked, 1, 1)
         x = from_mesh(masked, 0, 1)
     else:
         z = from_offset(masked, "space", 1)
-    low = from_offset(low, "space", -1)
-    high = from_offset(high, "space", 1)
+    far = swap_pairs(far, "space", 1)
+    near = swap_pairs(near, "space", 0)
+    tables, tail = call(
+        functools.partial(tables_kernel, ocean_cols, wave_rows, tail_rows, "spec", aligned),
+        ((9, tiles, padded, LANES), (chosen * TAIL_VREGS, 8, LANES)),
+        [HBM] * 2,
+        scratch_shapes=[
+            pltpu.VMEM(source.shape, jnp.int32),
+            pltpu.VMEM(weight.shape, f32),
+            pltpu.SemaphoreType.DMA((2,)),
+        ],
+    )(*in_hbm(source, weight))
+    tail = from_offset(tail, "space", -1)
     if aligned:
         (part,) = call(
             functools.partial(flow_kernel, "spec", list_rows, first),
@@ -590,31 +668,42 @@
     trig = np.stack([cosine, sine, sine * cosine, sine * sine, cosine * cosine]).astype(np.float32)
     trig = trig.reshape(5, 8, groups).transpose(0, 2, 1)
     trig = jnp.asarray(np.repeat(trig[:, :, :, None], LANES, axis=3))
-    cell = (groups, tiles, 8, LANES)
-    moved, stress = call(
-        functools.partial(advance_kernel, freqs * spec, "spec", list_rows, len(parts)),
-        (field.shape, (3, tiles, wave_rows, LANES)),
-        [VMEM] * (len(parts) + 1) + [SMEM] * 2 + [VMEM] * 3,
+    flow, turn, middle, inner, inner_stress = call(
+        functools.partial(inner_kernel, freqs * spec, "spec", list_rows, len(parts)),
+        (
+            (2, tiles, padded, LANES),
+            (2, list_rows - 2) + cell,
+            (freqs, wave_rows - 2) + cell,
+            (freqs, wave_rows - 4) + cell,
+            (3, wave_rows - 4, tiles, 8, LANES),
+        ),
+        [VMEM] * (len(parts) + 1) + [SMEM] * 2 + [VMEM],
         scratch_shapes=[
-            pltpu.VMEM((2, tiles, padded, LANES), f32),
             pltpu.VMEM((3, tiles, padded, LANES), f32),
-            pltpu.VMEM((2, list_rows - 2) + cell, f32),
-            pltpu.VMEM((wave_rows + 2,) + cell, f32),
-            pltpu.VMEM((3, wave_rows, tiles, 8, LANES), f32),
-            pltpu.VMEM((4, wave_rows + 2) + cell, f32),
+            pltpu.VMEM((4, list_rows) + cell, f32),
         ],
-    )(*parts, trig, courant, energy, held, low, high)
+    )(*parts, trig, courant, energy, held)
+    outer, stress = call(
+        functools.partial(outer_kernel, freqs * spec, ("space", "spec")),
+        ((freqs, 4) + cell, (3, tiles, wave_rows, LANES)),
+        [VMEM] + [SMEM] * 2 + [VMEM] * 7,
+        scratch_shapes=[
+            pltpu.VMEM((4,) + cell, f32),
+            pltpu.VMEM((3, 4, tiles, 8, LANES), f32),
+            pltpu.VMEM((4, list_rows) + cell, f32),
+        ],
+    )(trig, courant, energy, held, near, far, flow, turn, middle, inner_stress)
     if aligned:
+        xz = from_mesh(stress, -1, 1)
         z = from_mesh(stress, -1, 0)
-        xz = from_mesh(stress, -1, 1)
         x = from_mesh(stress, 0, 1)
     out_field, coupling = call(
         functools.partial(settle_kernel, "spec", aligned, tail_rows),
         (field.shape, (chosen, 9, 2 * wave_rows, LANES)),
-        [VMEM] * 3,
+        [VMEM] * 4,
         out_specs=(HBM, VMEM),
-        scratch_shapes=[pltpu.SemaphoreType.DMA(())],
-    )(moved, low, tables)
+        scratch_shapes=[pltpu.VMEM(field.shape, f32), pltpu.SemaphoreType.DMA((freqs,))],
+    )(inner, outer, tail, tables)
     new_action = jnp.transpose(out_field, (0, 1, 3, 2, 4)).reshape(action.shape)
     column = (2, 3, 2 * wave_rows, LANES)
     scratch = [pltpu.VMEM(column, f32), pltpu.VMEM((9, 2 * wave_rows, LANES), f32)]

time: 40.9 us -> 43.7 us (1.068)
  waiting for transfers between devices: 12.6 us -> 16.9 us
  starting transfers between devices: 15.5 us -> 12.8 us
  Pallas kernels: 11.9 us -> 13.1 us
    ppermute x0 -> x2, starting transfers between devices: none -> 5.26 us  [swap_pairs(): return lax.ppermute(block, axis, route)]
    ppermute x2 -> x1, waiting for transfers between devices: 0.01 us -> 5.13 us  [from_offset(): lax.ppermute(block, axis, [((i + offset) % count, i) for i in range(count)])]
    ppermute x2 -> x1, starting transfers between devices: 4.64 us -> 0.01 us  [from_offset(): lax.ppermute(block, axis, [((i + offset) % count, i) for i in range(count)])]
    ppermute x8, starting transfers between devices: 10.9 us -> 7.57 us  [from_mesh(): return lax.ppermute(block, ('space', 'spec'), route)]
    ppermute x8, waiting for transfers between devices: 12.6 us -> 11.8 us  [from_mesh(): return lax.ppermute(block, ('space', 'spec'), route)]
    pallas_call x2 -> x4, Pallas kernels: 9.3 us -> 9.96 us  [the longest x1 3.79 us: window(): call(functools.partial(inner_kernel, freqs * spec, 'spec', list_rows, len...]
    pallas_call x1, Pallas kernels: 1.15 us -> 1.66 us  [window(): call(functools.partial(settle_kernel, 'spec', aligned, tail_rows), (field...]
  transfers between devices with their start and end apart: 10 -> 11, of which waited for: 6 -> 7; matrix products, arithmetic and copies ran while one was open for 0% -> 0% of each run, Pallas kernels for 4% -> 16%
where the time goes in v2:
time: 43.7 us; the launch traced here: 43.5 us
  waiting for transfers between devices  16.9 us (39%)
  Pallas kernels  13.1 us (30%)
  starting transfers between devices  12.8 us (29%)
  between operations  0.74 us (2%)
    ppermute x8, waiting for transfers between devices, from_mesh(): return lax.ppermute(block, ('space', 'spec'), route)  11.8 us
    ppermute x8, starting transfers between devices, from_mesh(): return lax.ppermute(block, ('space', 'spec'), route)  7.57 us
    ppermute x2, starting transfers between devices, swap_pairs(): return lax.ppermute(block, axis, route)  5.26 us
    ppermute x1, waiting for transfers between devices, from_offset(): lax.ppermute(block, axis, [((i + offset) % count, i) for i in range(count)])  5.13 us
    pallas_call x1, Pallas kernels, window(): call(functools.partial(inner_kernel, freqs * spec, 'spec', list_rows, len...  3.79 us
    pallas_call x1, Pallas kernels, window(): call(functools.partial(outer_kernel, freqs * spec, ('space', 'spec')), ((...  3.04 us
    pallas_call x1, Pallas kernels, window(): call(functools.partial(open_kernel, 'space'), (currents.shape, wet.shape,...  1.96 us
    pallas_call x1, Pallas kernels, window(): call(functools.partial(settle_kernel, 'spec', aligned, tail_rows), (field...  1.66 us
  transfers between devices with their start and end apart: 11, of which 7 were waited for; matrix products, arithmetic and copies ran while one was open for 0% of the time, Pallas kernels for 16%

profile of v2, /device:TPU:0, one launch (start us, length us, event | category | flops | bytes accessed | tf_op | source)
XLA Modules:
  0.0 43.5 jit_solution(2143580302876295964)
XLA Ops:
  0.6 0.0 copy-start
  0.6 0.0 copy-start.2
  0.7 0.0 copy-start.1
  0.7 2.0 %shard_map.95 = (f32[2,16,256]{2,1,0:T(8,128)S(1)}, f32[16,256]{1,0:T(8,128)S(1)}, f32[4,24,4,8,128]{4,3,2,1,0:T(8,128)S(1)}, f32[24,4,8,128]{3,2,1,0:T(8,128)S(1)}, f32[24,4,8,128]{3,2,1,0:T(8,128)S(1)}) custom-call(f32[2,16,256]{2,1,0:T(8,128)} %current_hbm.1, s32[16,256]{1,0:T(8,128)} %wet_hbm.1, f32[4,24,4,8,128]{4,3,2,1,0:T(8,128)} %bitcast.8), custom_call_target="tpu_custom_call" | custom-call | tf_op jit(solution)/shard_map/pallas_call | solution.py:623
  2.6 0.6 %collective-permute-start.4 = (f32[24,4,8,128]{3,2,1,0:T(8,128)S(1)}, f32[24,4,8,128]{3,2,1,0:T(8,128)S(1)}, u32[]{:S(2)}, u32[]{:S(2)}) collective-permute-start(f32[24,4,8,128]{3,2,1,0:T(8,128)S(1)} %get-tuple-element.24), channel_id=1, source_target_pairs={{0,4},{4,0},{8,12},{12,8},{16,20},{20,16},{24,28},{28,24},{1,5},{5... | collective-permute-start | bytes 1179656 | tf_op jit(solution)/shard_map/ppermute | solution.py:45
  3.2 4.7 %collective-permute-start.5 = (f32[24,4,8,128]{3,2,1,0:T(8,128)S(1)}, f32[24,4,8,128]{3,2,1,0:T(8,128)S(1)}, u32[]{:S(2)}, u32[]{:S(2)}) collective-permute-start(f32[24,4,8,128]{3,2,1,0:T(8,128)S(1)} %get-tuple-element.25), channel_id=1, source_target_pairs={{4,8},{8,4},{12,16},{16,12},{20,24},{24,20},{28,0},{0,28},{5,9},{9... | collective-permute-start | bytes 1179656 | tf_op jit(solution)/shard_map/ppermute | solution.py:45
  7.9 0.9 %collective-permute-start.2 = (f32[2,16,256]{2,1,0:T(8,128)S(1)}, f32[2,16,256]{2,1,0:T(8,128)S(1)}, u32[]{:S(2)}, u32[]{:S(2)}) collective-permute-start(f32[2,16,256]{2,1,0:T(8,128)S(1)} %get-tuple-element.20.own_ref.masked_ref), channel_id=1, source_target_pairs={{5,0},{4,1},{7,2},{6,3},{9,4},{8,5},{11,6},{10,7},{13,8},{12,9},{1... | collective-permute-start | bytes 98312 | tf_op jit(solution)/shard_map/ppermute | solution.py:36
  8.8 0.7 %collective-permute-start.1 = (f32[2,16,256]{2,1,0:T(8,128)S(1)}, f32[2,16,256]{2,1,0:T(8,128)S(1)}, u32[]{:S(2)}, u32[]{:S(2)}) collective-permute-start(f32[2,16,256]{2,1,0:T(8,128)S(1)} %get-tuple-element.20.own_ref.masked_ref), channel_id=1, source_target_pairs={{4,0},{5,1},{6,2},{7,3},{8,4},{9,5},{10,6},{11,7},{12,8},{13,9},{1... | collective-permute-start | bytes 98312 | tf_op jit(solution)/shard_map/ppermute | solution.py:36
  9.6 0.5 %collective-permute-start = (f32[2,16,256]{2,1,0:T(8,128)S(1)}, f32[2,16,256]{2,1,0:T(8,128)S(1)}, u32[]{:S(2)}, u32[]{:S(2)}) collective-permute-start(f32[2,16,256]{2,1,0:T(8,128)S(1)} %get-tuple-element.20.own_ref.masked_ref), channel_id=1, source_target_pairs={{1,0},{0,1},{3,2},{2,3},{5,4},{4,5},{7,6},{6,7},{9,8},{8,9},{11,10... | collective-permute-start | bytes 98312 | tf_op jit(solution)/shard_map/ppermute | solution.py:36
  10.1 1.2 %shard_map.96 = (f32[9,4,16,128]{3,2,1,0:T(8,128)S(1)}, f32[8,8,128]{2,1,0:T(8,128)S(1)}) custom-call(s32[12,4,512]{2,1,0:T(4,128)} %bitcast.9, f32[12,4,512]{2,1,0:T(4,128)} %bitcast.10), custom_call_target="tpu_custom_call" | custom-call | tf_op jit(solution)/shard_map/pallas_call | solution.py:641
  11.3 3.9 %collective-permute-done.2.xz_ref = f32[2,16,256]{2,1,0:T(8,128)S(1)} collective-permute-done((f32[2,16,256]{2,1,0:T(8,128)S(1)}, f32[2,16,256]{2,1,0:T(8,128)S(1)}, u32[]{:S(2)}, u32[]{:S(2)}) %collective-permute-start.2) | collective-permute-done | bytes 32800 | tf_op jit(solution)/shard_map/ppermute | solution.py:36
  15.2 0.4 collective-permute-done.1.z_ref
  15.5 0.0 collective-permute-done.x_ref
  15.5 0.4 shard_map.97.refs_0_
  15.9 1.6 %collective-permute-start.3 = (f32[3,2,16,128]{3,2,1,0:T(8,128)S(1)}, f32[3,2,16,128]{3,2,1,0:T(8,128)S(1)}, u32[]{:S(2)}, u32[]{:S(2)}) collective-permute-start(f32[3,2,16,128]{3,2,1,0:T(8,128)S(1)} %shard_map.97.refs_0_), channel_id=1, source_target_pairs={{2,0},{3,1},{0,2},{1,3},{6,4},{7,5},{4,6},{5,7},{10,8},{11,9},{8,1... | collective-permute-start | bytes 147464 | tf_op jit(solution)/shard_map/ppermute | solution.py:36
  17.5 2.6 %collective-permute-done.3.refs_1_ = f32[3,2,16,128]{3,2,1,0:T(8,128)S(1)} collective-permute-done((f32[3,2,16,128]{3,2,1,0:T(8,128)S(1)}, f32[3,2,16,128]{3,2,1,0:T(8,128)S(1)}, u32[]{:S(2)}, u32[]{:S(2)}) %collective-permute-start.3) | collective-permute-done | bytes 49184 | tf_op jit(solution)/shard_map/ppermute | solution.py:36
  20.1 0.0 copy-done
  20.1 0.0 copy-done.2
  20.1 0.0 copy-done.1
  20.1 3.8 %shard_map.98 = (f32[2,4,16,128]{3,2,1,0:T(8,128)S(1)}, f32[2,10,3,4,8,128]{5,4,3,2,1,0:T(8,128)S(1)}, f32[4,6,3,4,8,128]{5,4,3,2,1,0:T(8,128)S(1)}, f32[4,4,3,4...) custom-call(f32[3,2,16,128]{3,2,1,0:T(8,128)S(1)} %shard_map.97.refs_0_, ...), custom_call_target="tpu_custom_call" | custom-call | tf_op jit(solution)/shard_map/pallas_call | solution.py:671
  23.9 0.0 collective-permute-done.4.near_ref
  23.9 0.0 collective-permute-done.5.far_ref
  23.9 3.0 %shard_map.99 = (f32[4,4,3,4,8,128]{5,4,3,2,1,0:T(8,128)S(1)}, f32[3,4,8,128]{3,2,1,0:T(8,128)S(1)}) custom-call(f32[5,3,8,128]{3,2,1,0:T(8,128)S(1)} %copy-done, f32[16]{0:T(128)S(1)} %copy-done.1, f32[16]{0:T(128)S(1)} %copy-done.2, f32[4,24,4,8,128]{4,3,2,1,0:T(8,128)S(1)} %get-tuple-element.22.refs_5_.field_ref, ...), custom_call_target="tpu_custom_call" | custom-call | tf_op jit(solution)/shard_map/pallas_call | solution.py:686
  26.9 1.5 %collective-permute-start.9 = (f32[3,4,8,128]{3,2,1,0:T(8,128)S(1)}, f32[3,4,8,128]{3,2,1,0:T(8,128)S(1)}, u32[]{:S(2)}, u32[]{:S(2)}) collective-permute-start(f32[3,4,8,128]{3,2,1,0:T(8,128)S(1)} %get-tuple-element.33.own_ref), channel_id=1, source_target_pairs={{29,0},{28,1},{31,2},{30,3},{1,4},{0,5},{3,6},{2,7},{5,8},{4,9},{7... | collective-permute-start | bytes 147464 | tf_op jit(solution)/shard_map/ppermute | solution.py:36
  28.4 0.6 %collective-permute-start.8 = (f32[3,4,8,128]{3,2,1,0:T(8,128)S(1)}, f32[3,4,8,128]{3,2,1,0:T(8,128)S(1)}, u32[]{:S(2)}, u32[]{:S(2)}) collective-permute-start(f32[3,4,8,128]{3,2,1,0:T(8,128)S(1)} %get-tuple-element.33.own_ref), channel_id=1, source_target_pairs={{28,0},{29,1},{30,2},{31,3},{0,4},{1,5},{2,6},{3,7},{4,8},{5,9},{6... | collective-permute-start | bytes 147464 | tf_op jit(solution)/shard_map/ppermute | solution.py:36
  29.1 0.1 collective-permute-start.7
  29.2 4.2 %collective-permute-done.9.xz_ref = f32[3,4,8,128]{3,2,1,0:T(8,128)S(1)} collective-permute-done((f32[3,4,8,128]{3,2,1,0:T(8,128)S(1)}, f32[3,4,8,128]{3,2,1,0:T(8,128)S(1)}, u32[]{:S(2)}, u32[]{:S(2)}) %collective-permute-start.9) | collective-permute-done | bytes 49184 | tf_op jit(solution)/shard_map/ppermute | solution.py:36
  33.3 0.5 %collective-permute-done.8.z_ref = f32[3,4,8,128]{3,2,1,0:T(8,128)S(1)} collective-permute-done((f32[3,4,8,128]{3,2,1,0:T(8,128)S(1)}, f32[3,4,8,128]{3,2,1,0:T(8,128)S(1)}, u32[]{:S(2)}, u32[]{:S(2)}) %collective-permute-start.8) | collective-permute-done | bytes 49184 | tf_op jit(solution)/shard_map/ppermute | solution.py:36
  33.8 0.3 collective-permute-done.7.x_ref
  34.1 1.6 %collective-permute-start.10 = (f32[2,3,16,128]{3,2,1,0:T(8,128)S(1)}, f32[2,3,16,128]{3,2,1,0:T(8,128)S(1)}, u32[]{:S(2)}, u32[]{:S(2)}) collective-permute-start(f32[2,3,16,128]{3,2,1,0:T(8,128)S(1)} %get-tuple-element.35), channel_id=1, source_target_pairs={{2,0},{3,1},{0,2},{1,3},{6,4},{7,5},{4,6},{5,7},{10,8},{11,9},{8,1... | collective-permute-start | bytes 147464 | tf_op jit(solution)/shard_map/ppermute | solution.py:36
  35.7 0.0 collective-permute-start.6
  35.7 5.1 %collective-permute-done.6.tail_ref = f32[8,8,128]{2,1,0:T(8,128)S(1)} collective-permute-done((f32[8,8,128]{2,1,0:T(8,128)S(1)}, f32[8,8,128]{2,1,0:T(8,128)S(1)}, u32[]{:S(2)}, u32[]{:S(2)}) %collective-permute-start.6) | collective-permute-done | bytes 32800 | tf_op jit(solution)/shard_map/ppermute | solution.py:28
  40.9 1.7 %shard_map.100 = (f32[4,24,4,8,128]{4,3,2,1,0:T(8,128)}, f32[2,9,16,128]{3,2,1,0:T(8,128)S(1)}) custom-call(f32[4,4,3,4,8,128]{5,4,3,2,1,0:T(8,128)S(1)} %get-tuple-element.23.inner_ref, f32[4,4,3,4,8,128]{5,4,3,2,1,0:T(8,128)S(1)} %get-tuple-element.30.outer_ref, f32[8,8,128]{2,1,0:T(8,128)S(1)} %collective-permute-done.6.tail_ref, ...), custom_call_target="tpu_custom_call" | custom-call | tf_op jit(solution)/shard_map/pallas_call | solution.py:700
  42.5 0.0 collective-permute-done.10.come_ref
  42.6 1.0 %shard_map.102 = f32[2,16,256]{2,1,0:T(8,128)} custom-call(f32[2,3,16,128]{3,2,1,0:T(8,128)S(1)} %get-tuple-element.34.keep_ref, f32[2,3,16,128]{3,2,1,0:T(8,128)S(1)} %collective-permute-done.10.come_ref, f32[2,9,16,128]{3,2,1,0:T(8,128)S(1)} %get-tuple-element.36.coupling_ref, f32[2,16,256]{2,1,0:T(8,128)S(1)} %get-tuple-element.20.own_ref.masked_ref, ...), custom_call_target="tpu_custom_call" | custom-call | tf_op jit(solution)/shard_map/pallas_call | solution.py:713
  (1 shorter events, 0.0 us)
Async XLA Ops:
  0.6 19.4 %copy-start = (f32[5,3,8,128]{3,2,1,0:T(8,128)S(1)}, f32[5,3,8,128]{3,2,1,0:T(8,128)}, u32[]{:S(2)}) copy-start(f32[5,3,8,128]{3,2,1,0:T(8,128)} %constant.2.clone.refs_2_.trig_ref) | copy-start | bytes 184324
  0.6 19.4 %copy-start.2 = (f32[16]{0:T(128)S(1)}, f32[16]{0:T(128)}, u32[]{:S(2)}) copy-start(f32[16]{0:T(128)} %energy_ref.1) | copy-start | bytes 196
  0.7 19.4 %copy-start.1 = (f32[16]{0:T(128)S(1)}, f32[16]{0:T(128)}, u32[]{:S(2)}) copy-start(f32[16]{0:T(128)} %speed_ref.1) | copy-start | bytes 196
  2.6 21.2 %collective-permute-start.4 = (f32[24,4,8,128]{3,2,1,0:T(8,128)S(1)}, f32[24,4,8,128]{3,2,1,0:T(8,128)S(1)}, u32[]{:S(2)}, u32[]{:S(2)}) collective-permute-start(f32[24,4,8,128]{3,2,1,0:T(8,128)S(1)} %get-tuple-element.24), channel_id=1, source_target_pairs={{0,4},{4,0},{8,12},{12,8},{16,20},{20,16},{24,28},{28,24},{1,5},{5... | collective-permute-start | bytes 1179656 | tf_op jit(solution)/shard_map/ppermute | solution.py:45
  3.2 20.7 %collective-permute-start.5 = (f32[24,4,8,128]{3,2,1,0:T(8,128)S(1)}, f32[24,4,8,128]{3,2,1,0:T(8,128)S(1)}, u32[]{:S(2)}, u32[]{:S(2)}) collective-permute-start(f32[24,4,8,128]{3,2,1,0:T(8,128)S(1)} %get-tuple-element.25), channel_id=1, source_target_pairs={{4,8},{8,4},{12,16},{16,12},{20,24},{24,20},{28,0},{0,28},{5,9},{9... | collective-permute-start | bytes 1179656 | tf_op jit(solution)/shard_map/ppermute | solution.py:45
  7.9 7.3 %collective-permute-start.2 = (f32[2,16,256]{2,1,0:T(8,128)S(1)}, f32[2,16,256]{2,1,0:T(8,128)S(1)}, u32[]{:S(2)}, u32[]{:S(2)}) collective-permute-start(f32[2,16,256]{2,1,0:T(8,128)S(1)} %get-tuple-element.20.own_ref.masked_ref), channel_id=1, source_target_pairs={{5,0},{4,1},{7,2},{6,3},{9,4},{8,5},{11,6},{10,7},{13,8},{12,9},{1... | collective-permute-start | bytes 98312 | tf_op jit(solution)/shard_map/ppermute | solution.py:36
  8.8 6.7 %collective-permute-start.1 = (f32[2,16,256]{2,1,0:T(8,128)S(1)}, f32[2,16,256]{2,1,0:T(8,128)S(1)}, u32[]{:S(2)}, u32[]{:S(2)}) collective-permute-start(f32[2,16,256]{2,1,0:T(8,128)S(1)} %get-tuple-element.20.own_ref.masked_ref), channel_id=1, source_target_pairs={{4,0},{5,1},{6,2},{7,3},{8,4},{9,5},{10,6},{11,7},{12,8},{13,9},{1... | collective-permute-start | bytes 98312 | tf_op jit(solution)/shard_map/ppermute | solution.py:36
  9.6 6.0 %collective-permute-start = (f32[2,16,256]{2,1,0:T(8,128)S(1)}, f32[2,16,256]{2,1,0:T(8,128)S(1)}, u32[]{:S(2)}, u32[]{:S(2)}) collective-permute-start(f32[2,16,256]{2,1,0:T(8,128)S(1)} %get-tuple-element.20.own_ref.masked_ref), channel_id=1, source_target_pairs={{1,0},{0,1},{3,2},{2,3},{5,4},{4,5},{7,6},{6,7},{9,8},{8,9},{11,10... | collective-permute-start | bytes 98312 | tf_op jit(solution)/shard_map/ppermute | solution.py:36
  15.9 4.2 %collective-permute-start.3 = (f32[3,2,16,128]{3,2,1,0:T(8,128)S(1)}, f32[3,2,16,128]{3,2,1,0:T(8,128)S(1)}, u32[]{:S(2)}, u32[]{:S(2)}) collective-permute-start(f32[3,2,16,128]{3,2,1,0:T(8,128)S(1)} %shard_map.97.refs_0_), channel_id=1, source_target_pairs={{2,0},{3,1},{0,2},{1,3},{6,4},{7,5},{4,6},{5,7},{10,8},{11,9},{8,1... | collective-permute-start | bytes 147464 | tf_op jit(solution)/shard_map/ppermute | solution.py:36
  26.9 6.4 %collective-permute-start.9 = (f32[3,4,8,128]{3,2,1,0:T(8,128)S(1)}, f32[3,4,8,128]{3,2,1,0:T(8,128)S(1)}, u32[]{:S(2)}, u32[]{:S(2)}) collective-permute-start(f32[3,4,8,128]{3,2,1,0:T(8,128)S(1)} %get-tuple-element.33.own_ref), channel_id=1, source_target_pairs={{29,0},{28,1},{31,2},{30,3},{1,4},{0,5},{3,6},{2,7},{5,8},{4,9},{7... | collective-permute-start | bytes 147464 | tf_op jit(solution)/shard_map/ppermute | solution.py:36
  28.4 5.4 %collective-permute-start.8 = (f32[3,4,8,128]{3,2,1,0:T(8,128)S(1)}, f32[3,4,8,128]{3,2,1,0:T(8,128)S(1)}, u32[]{:S(2)}, u32[]{:S(2)}) collective-permute-start(f32[3,4,8,128]{3,2,1,0:T(8,128)S(1)} %get-tuple-element.33.own_ref), channel_id=1, source_target_pairs={{28,0},{29,1},{30,2},{31,3},{0,4},{1,5},{2,6},{3,7},{4,8},{5,9},{6... | collective-permute-start | bytes 147464 | tf_op jit(solution)/shard_map/ppermute | solution.py:36
  29.1 5.0 %collective-permute-start.7 = (f32[3,4,8,128]{3,2,1,0:T(8,128)S(1)}, f32[3,4,8,128]{3,2,1,0:T(8,128)S(1)}, u32[]{:S(2)}, u32[]{:S(2)}) collective-permute-start(f32[3,4,8,128]{3,2,1,0:T(8,128)S(1)} %get-tuple-element.33.own_ref), channel_id=1, source_target_pairs={{1,0},{0,1},{3,2},{2,3},{5,4},{4,5},{7,6},{6,7},{9,8},{8,9},{11,10... | collective-permute-start | bytes 147464 | tf_op jit(solution)/shard_map/ppermute | solution.py:36
  34.1 8.4 %collective-permute-start.10 = (f32[2,3,16,128]{3,2,1,0:T(8,128)S(1)}, f32[2,3,16,128]{3,2,1,0:T(8,128)S(1)}, u32[]{:S(2)}, u32[]{:S(2)}) collective-permute-start(f32[2,3,16,128]{3,2,1,0:T(8,128)S(1)} %get-tuple-element.35), channel_id=1, source_target_pairs={{2,0},{3,1},{0,2},{1,3},{6,4},{7,5},{4,6},{5,7},{10,8},{11,9},{8,1... | collective-permute-start | bytes 147464 | tf_op jit(solution)/shard_map/ppermute | solution.py:36
  35.7 5.1 %collective-permute-start.6 = (f32[8,8,128]{2,1,0:T(8,128)S(1)}, f32[8,8,128]{2,1,0:T(8,128)S(1)}, u32[]{:S(2)}, u32[]{:S(2)}) collective-permute-start(f32[8,8,128]{2,1,0:T(8,128)S(1)} %get-tuple-element.31), channel_id=1, source_target_pairs={{28,0},{0,4},{4,8},{8,12},{12,16},{16,20},{20,24},{24,28},{29,1},{... | collective-permute-start | bytes 98312 | tf_op jit(solution)/shard_map/ppermute | solution.py:28

commit v3 on v2

--- a/solution.py
+++ b/solution.py
@@ -34,15 +34,6 @@
         (((i + offset) % space) * spec + (j ^ bits), i * spec + j) for i in range(space) for j in range(spec)
     ]
     return lax.ppermute(block, ("space", "spec"), route)
-
-
-def swap_pairs(block, axis, first):
-    count = lax.axis_size(axis)
-    route = []
-    for i in range(first, first + count, 2):
-        low, high = i % count, (i + 1) % count
-        route += [(low, high), (high, low)]
-    return lax.ppermute(block, axis, route)
 
 
 def params(**kw):
@@ -98,7 +89,7 @@
 
 def row_slots(groups, tiles, row):
     return [
-        [pl.ds((group * tiles + tile) * 8 + row, 8, stride=groups * tiles * 8) for tile in range(tiles)]
+        [pl.ds((tile * 8 * groups + group) * 8 + row, 8, stride=groups * 8) for tile in range(tiles)]
         for group in range(groups)
     ]
 
@@ -126,48 +117,43 @@
     return [index, lax.rem(index + tiles - 1, tiles)]
 
 
+def tile_copies(tiled, whole, sems, out):
+    freqs, tiles = tiled.shape[:2]
+    for freq in range(freqs):
+        for tile in range(tiles):
+            ends = (tiled.at[freq, tile], whole.at[freq, :, tile])
+            yield freq, pltpu.make_async_copy(*(ends if out else ends[::-1]), sems.at[freq, tile])
+
+
 def open_kernel(
-    axis, current_hbm, wet_hbm, field_hbm, masked_ref, wet_out, field_ref, near_ref, far_ref,
-    current_ref, wet_ref, sems,
+    ocean_cols, tail_rows, axis, aligned, current_hbm, wet_hbm, src_hbm, weight_hbm, field_hbm,
+    masked_ref, wet_out, table_ref, tail_ref, field_ref, low_ref, high_ref,
+    current_ref, wet_ref, src_ref, weight_ref, sems, field_sems,
 ):
     copies = [
         pltpu.make_async_copy(source, target, sems.at[k])
         for k, (source, target) in enumerate(
-            ((current_hbm, current_ref), (wet_hbm, wet_ref), (field_hbm, field_ref))
+            (
+                (current_hbm, current_ref),
+                (wet_hbm, wet_ref),
+                (src_hbm, src_ref),
+                (weight_hbm, weight_ref),
+            )
         )
     ]
+    moves = list(tile_copies(field_ref, field_hbm, field_sems, False))
     for copy in copies:
         copy.start()
-    freqs, directions, tiles, wave_rows, _ = field_ref.shape
+    for _, copy in moves:
+        copy.start()
+    list_rows, corners, columns = src_ref.shape
+    freqs, tiles, directions, wave_rows, _ = field_ref.shape
     groups = directions // 8
     copies[0].wait()
     copies[1].wait()
     wet = wet_ref[...].astype(jnp.float32)
     wet_out[...] = wet
     masked_ref[...] = current_ref[...] * wet[None]
-    odd = lax.rem(lax.axis_index(axis), 2)
-    last = wave_rows - 2
-    copies[2].wait()
-    for freq in range(freqs):
-        view = row_view(field_ref, freq)
-        for row in range(2):
-            at = (freq * 2 + row) * groups
-            near_ref[at : at + groups] = load_row(view, groups, tiles, last * (1 - odd) + row)
-            far_ref[at : at + groups] = load_row(view, groups, tiles, last * odd + row)
-
-
-def tables_kernel(
-    ocean_cols, wave_rows, tail_rows, axis, aligned, src_hbm, weight_hbm, table_ref, tail_ref,
-    src_ref, weight_ref, sems,
-):
-    copies = [
-        pltpu.make_async_copy(src_hbm, src_ref, sems.at[0]),
-        pltpu.make_async_copy(weight_hbm, weight_ref, sems.at[1]),
-    ]
-    for copy in copies:
-        copy.start()
-    list_rows, corners, columns = src_ref.shape
-    tiles = columns // LANES
     shape = (list_rows, columns)
     entry_row = lax.broadcasted_iota(jnp.int32, shape, 0)
     column = lax.broadcasted_iota(jnp.int32, shape, 1)
@@ -176,8 +162,8 @@
         base + jnp.where(2 * column + step >= ocean_cols, 2 * column + step - ocean_cols, 2 * column + step)
         for step in range(3)
     ]
-    for copy in copies:
-        copy.wait()
+    copies[2].wait()
+    copies[3].wait()
     sums = [jnp.zeros(shape, jnp.float32) for _ in range(9)]
     for corner in range(corners):
         source = src_ref[:, corner, :]
@@ -196,6 +182,15 @@
             for row in range(tail_rows):
                 vreg, line = tail_slot(which, place * tail_rows + row)
                 tail_ref[vreg, line : line + 1, :] = table_ref[place, tile, first + row : first + row + 1, :]
+    for freq in range(freqs):
+        for other, copy in moves:
+            if other == freq:
+                copy.wait()
+        view = row_view(field_ref, freq)
+        for row in range(2):
+            at = (freq * 2 + row) * groups
+            low_ref[at : at + groups] = load_row(view, groups, tiles, wave_rows - 2 + row)
+            high_ref[at : at + groups] = load_row(view, groups, tiles, row)
 
 
 def flow_tile(table_ref, tile, evens, odds, nexts):
@@ -330,7 +325,7 @@
     (trig_ref, speed_ref, energy_ref, field_ref) = refs[parts : parts + 4]
     flow_ref, turn_ref, mid_ref, out_ref, sum_ref = refs[parts + 4 : parts + 9]
     grad_ref, keep_ref = refs[parts + 9 :]
-    freqs, directions, tiles, wave_rows, _ = field_ref.shape
+    freqs, tiles, directions, wave_rows, _ = field_ref.shape
     groups = directions // 8
     index = lax.axis_index(axis)
     for comp in range(2):
@@ -388,13 +383,12 @@
 
 
 def outer_kernel(
-    total_freq, axes, trig_ref, speed_ref, energy_ref, field_ref, near_ref, far_ref, flow_ref, turn_ref,
+    total_freq, axis, trig_ref, speed_ref, energy_ref, field_ref, low_ref, high_ref, flow_ref, turn_ref,
     mid_ref, inner_ref, out_ref, stress_ref, rim_ref, sum_ref, keep_ref,
 ):
-    freqs, directions, tiles, wave_rows, _ = field_ref.shape
+    freqs, tiles, directions, wave_rows, _ = field_ref.shape
     groups = directions // 8
-    start = lax.axis_index(axes[1]) * freqs
-    odd = lax.rem(lax.axis_index(axes[0]), 2) == 1
+    start = lax.axis_index(axis) * freqs
     sum_ref[...] = jnp.zeros_like(sum_ref)
     rim = {-1: 0, 0: 1, wave_rows - 1: 2, wave_rows: 3}
     last = {0: 0, 1: 1, wave_rows - 2: 2, wave_rows - 1: 3}
@@ -407,8 +401,7 @@
             if 0 <= row < wave_rows:
                 return load_row(source, groups, tiles, row)
             at = pl.ds((freq * 2 + row % 2) * groups, groups)
-            near, far = near_ref[at], far_ref[at]
-            return jnp.where(odd, near, far) if row < 0 else jnp.where(odd, far, near)
+            return low_ref[at] if row < 0 else high_ref[at]
 
         def keep(row, value):
             rim_ref[rim[row]] = value
@@ -435,10 +428,6 @@
             line = jnp.sum(part, axis=1, keepdims=True)
             for tile in range(tiles):
                 stress_ref[kind, tile, row : row + 1] = line[tile]
-
-
-def stress_column(own, prev, half):
-    return prev[prev.shape[0] - half - 2 :], own[: half + 1]
 
 
 def edge_tile(after, before):
@@ -461,30 +450,28 @@
             def prev(tile):
                 return z_ref[kind, tile] + xz_ref[kind, tile]
 
-            upper, lower = stress_column(own(target), prev(target), half)
-            out_ref[0, kind, 0 : half + 2] = upper
-            out_ref[0, kind, half + 2 : wave_rows + 3] = lower
-            upper, lower = stress_column(
-                edge_tile(own(after), own(before)), edge_tile(prev(after), prev(before)), half
-            )
-            out_ref[1, kind, 0 : half + 2] = upper
-            out_ref[1, kind, half + 2 : wave_rows + 3] = lower
+            out_ref[0, kind, 0 : half + 2] = prev(target)[wave_rows - half - 2 :]
+            out_ref[0, kind, half + 2 : wave_rows + 3] = own(target)[: half + 1]
+            out_ref[1, kind, 0 : half + 2] = edge_tile(prev(after), prev(before))[wave_rows - half - 2 :]
+            out_ref[1, kind, half + 2 : wave_rows + 3] = edge_tile(own(after), own(before))[: half + 1]
 
 
 def settle_kernel(
     axis, aligned, tail_rows, inner_ref, outer_ref, tail_ref, table_ref, out_hbm, coupling_ref, field_ref, sems
 ):
-    freqs, _, tiles, wave_rows, _ = field_ref.shape
-    copies = []
+    freqs, tiles, _, wave_rows, _ = field_ref.shape
+    moves = list(tile_copies(field_ref, out_hbm, sems, True))
     for freq in range(freqs):
         sink = row_view(field_ref, freq)
         for row in range(wave_rows):
             if 2 <= row < wave_rows - 2:
-                store_row(sink, row, inner_ref[freq, row - 2])
+                value = inner_ref[freq, row - 2]
             else:
-                store_row(sink, row, outer_ref[freq, row if row < 2 else row - wave_rows + 4])
-        copies.append(pltpu.make_async_copy(field_ref.at[freq], out_hbm.at[freq], sems.at[freq]))
-        copies[-1].start()
+                value = outer_ref[freq, row if row < 2 else row - wave_rows + 4]
+            store_row(sink, row, value)
+        for other, copy in moves:
+            if other == freq:
+                copy.start()
     count = wave_rows + 1
     for which, tile in enumerate(chosen_tiles(axis, aligned, tiles)):
         for place in range(9):
@@ -492,7 +479,7 @@
                 vreg, line = tail_slot(which, place * tail_rows + row)
                 coupling_ref[which, place, row : row + 1, :] = tail_ref[vreg, line : line + 1, :]
             coupling_ref[which, place, tail_rows:count] = table_ref[place, tile, 0 : count - tail_rows]
-    for copy in copies:
+    for _, copy in moves:
         copy.wait()
 
 
@@ -574,16 +561,14 @@
     for tile in range(tiles):
         after, before = (tile + 1) % tiles, (tile - 1) % tiles
         for kind in range(kinds):
-            upper, lower = stress_column(own_ref[kind, tile], prev_ref[kind, tile], half)
-            stress_ref[0, kind, 0 : half + 2] = upper
-            stress_ref[0, kind, half + 2 : wave_rows + 3] = lower
-            upper, lower = stress_column(
-                edge_tile(own_ref[kind, after], own_ref[kind, before]),
-                edge_tile(prev_ref[kind, after], prev_ref[kind, before]),
-                half,
-            )
-            stress_ref[1, kind, 0 : half + 2] = upper
-            stress_ref[1, kind, half + 2 : wave_rows + 3] = lower
+            stress_ref[0, kind, 0 : half + 2] = prev_ref[kind, tile][wave_rows - half - 2 :]
+            stress_ref[0, kind, half + 2 : wave_rows + 3] = own_ref[kind, tile][: half + 1]
+            stress_ref[1, kind, 0 : half + 2] = edge_tile(prev_ref[kind, after], prev_ref[kind, before])[
+                wave_rows - half - 2 :
+            ]
+            stress_ref[1, kind, half + 2 : wave_rows + 3] = edge_tile(own_ref[kind, after], own_ref[kind, before])[
+                : half + 1
+            ]
         pushed = push_tile(stress_ref, coupling_ref, tile, before, push_ref, wave_rows + 1)
         for comp in range(2):
             for parity in range(2):
@@ -620,34 +605,36 @@
     field = jnp.transpose(action.reshape(freqs, directions, wave_rows, tiles, LANES), (0, 1, 3, 2, 4))
     source, weight = jnp.transpose(src, (0, 2, 1)), jnp.transpose(weights, (0, 2, 1))
     cell = (groups, tiles, 8, LANES)
-    masked, wet_float, held, near, far = call(
-        functools.partial(open_kernel, "space"),
-        (currents.shape, wet.shape, field.shape, (lead, tiles, 8, LANES), (lead, tiles, 8, LANES)),
-        [HBM] * 3,
+    home = (freqs, tiles, directions, wave_rows, LANES)
+    masked, wet_float, tables, tail, held, low, high = call(
+        functools.partial(open_kernel, ocean_cols, tail_rows, "spec", aligned),
+        (
+            currents.shape,
+            wet.shape,
+            (9, tiles, padded, LANES),
+            (chosen * TAIL_VREGS, 8, LANES),
+            home,
+            (lead, tiles, 8, LANES),
+            (lead, tiles, 8, LANES),
+        ),
+        [HBM] * 5,
         scratch_shapes=[
             pltpu.VMEM(currents.shape, f32),
             pltpu.VMEM(wet.shape, jnp.int32),
-            pltpu.SemaphoreType.DMA((3,)),
+            pltpu.VMEM(source.shape, jnp.int32),
+            pltpu.VMEM(weight.shape, f32),
+            pltpu.SemaphoreType.DMA((4,)),
+            pltpu.SemaphoreType.DMA((freqs, tiles)),
         ],
-    )(*in_hbm(currents, wet, field))
+    )(*in_hbm(currents, wet, source, weight, field))
     if aligned:
         xz = from_mesh(masked, 1, 1)
         z = from_mesh(masked, 1, 0)
         x = from_mesh(masked, 0, 1)
     else:
         z = from_offset(masked, "space", 1)
-    far = swap_pairs(far, "space", 1)
-    near = swap_pairs(near, "space", 0)
-    tables, tail = call(
-        functools.partial(tables_kernel, ocean_cols, wave_rows, tail_rows, "spec", aligned),
-        ((9, tiles, padded, LANES), (chosen * TAIL_VREGS, 8, LANES)),
-        [HBM] * 2,
-        scratch_shapes=[
-            pltpu.VMEM(source.shape, jnp.int32),
-            pltpu.VMEM(weight.shape, f32),
-            pltpu.SemaphoreType.DMA((2,)),
-        ],
-    )(*in_hbm(source, weight))
+    low = from_offset(low, "space", -1)
+    high = from_offset(high, "space", 1)
     tail = from_offset(tail, "space", -1)
     if aligned:
         (part,) = call(
@@ -684,7 +671,7 @@
         ],
     )(*parts, trig, courant, energy, held)
     outer, stress = call(
-        functools.partial(outer_kernel, freqs * spec, ("space", "spec")),
+        functools.partial(outer_kernel, freqs * spec, "spec"),
         ((freqs, 4) + cell, (3, tiles, wave_rows, LANES)),
         [VMEM] + [SMEM] * 2 + [VMEM] * 7,
         scratch_shapes=[
@@ -692,7 +679,7 @@
             pltpu.VMEM((3, 4, tiles, 8, LANES), f32),
             pltpu.VMEM((4, list_rows) + cell, f32),
         ],
-    )(trig, courant, energy, held, near, far, flow, turn, middle, inner_stress)
+    )(trig, courant, energy, held, low, high, flow, turn, middle, inner_stress)
     if aligned:
         xz = from_mesh(stress, -1, 1)
         z = from_mesh(stress, -1, 0)
@@ -702,7 +689,7 @@
         (field.shape, (chosen, 9, 2 * wave_rows, LANES)),
         [VMEM] * 4,
         out_specs=(HBM, VMEM),
-        scratch_shapes=[pltpu.VMEM(field.shape, f32), pltpu.SemaphoreType.DMA((freqs,))],
+        scratch_shapes=[pltpu.VMEM(home, f32), pltpu.SemaphoreType.DMA((freqs, tiles))],
     )(inner, outer, tail, tables)
     new_action = jnp.transpose(out_field, (0, 1, 3, 2, 4)).reshape(action.shape)
     column = (2, 3, 2 * wave_rows, LANES)

time: 43.7 us -> 43.4 us (level)
  starting transfers between devices: 12.8 us -> 15.5 us
  Pallas kernels: 13.1 us -> 11.1 us
  waiting for transfers between devices: 16.9 us -> 16 us
    ppermute x2 -> x0, starting transfers between devices: 5.26 us -> none  [swap_pairs(): return lax.ppermute(block, axis, route)]
    ppermute x1 -> x3, starting transfers between devices: 0.01 us -> 4.64 us  [from_offset(): lax.ppermute(block, axis, [((i + offset) % count, i) for i in range(count)])]
    ppermute x8, starting transfers between devices: 7.57 us -> 10.9 us  [from_mesh(): return lax.ppermute(block, ('space', 'spec'), route)]
    pallas_call x3 -> x2, Pallas kernels: 6.17 us -> 4.96 us  [the longest x1 2.85 us: window(): call(functools.partial(outer_kernel, freqs * spec, 'spec'), ((freqs, 4) +...]
    ppermute x8, waiting for transfers between devices: 11.8 us -> 10.8 us  [from_mesh(): return lax.ppermute(block, ('space', 'spec'), route)]
    pallas_call x1, Pallas kernels: 3.79 us -> 3.32 us  [window(): call(functools.partial(inner_kernel, freqs * spec, 'spec', list_rows, len...]
    ppermute x1 -> x3, waiting for transfers between devices: 5.13 us -> 5.14 us  [from_offset(): lax.ppermute(block, axis, [((i + offset) % count, i) for i in range(count)])]
  transfers between devices with their start and end apart: 11 -> 11, of which waited for: 7 -> 6; matrix products, arithmetic and copies ran while one was open for 0% -> 0% of each run, Pallas kernels for 16% -> 12%
where the time goes in v3:
time: 43.4 us; the launch traced here: 43.3 us
  waiting for transfers between devices  16 us (37%)
  starting transfers between devices  15.5 us (36%)
  Pallas kernels  11.1 us (26%)
  between operations  0.74 us (2%)
    ppermute x8, starting transfers between devices, from_mesh(): return lax.ppermute(block, ('space', 'spec'), route)  10.9 us
    ppermute x8, waiting for transfers between devices, from_mesh(): return lax.ppermute(block, ('space', 'spec'), route)  10.8 us
    ppermute x3, waiting for transfers between devices, from_offset(): lax.ppermute(block, axis, [((i + offset) % count, i) for i in range(count)])  5.14 us
    ppermute x3, starting transfers between devices, from_offset(): lax.ppermute(block, axis, [((i + offset) % count, i) for i in range(count)])  4.64 us
    pallas_call x1, Pallas kernels, window(): call(functools.partial(inner_kernel, freqs * spec, 'spec', list_rows, len...  3.32 us
    pallas_call x1, Pallas kernels, window(): call(functools.partial(outer_kernel, freqs * spec, 'spec'), ((freqs, 4) +...  2.85 us
    pallas_call x1, Pallas kernels, window(): call(functools.partial(open_kernel, ocean_cols, tail_rows, 'spec', aligne...  2.11 us
    pallas_call x1, Pallas kernels, window(): call(functools.partial(settle_kernel, 'spec', aligned, tail_rows), (field...  1.36 us
  transfers between devices with their start and end apart: 11, of which 6 were waited for; matrix products, arithmetic and copies ran while one was open for 0% of the time, Pallas kernels for 12%

profile of v3, /device:TPU:0, one launch (start us, length us, event | category | flops | bytes accessed | tf_op | source)
XLA Modules:
  0.0 43.3 jit_solution(754880553904707847)
XLA Ops:
  0.6 0.0 copy-start
  0.6 0.0 copy-start.2
  0.7 0.0 copy-start.1
  0.7 2.1 %shard_map.95 = (f32[2,16,256]{2,1,0:T(8,128)S(1)}, f32[16,256]{1,0:T(8,128)S(1)}, f32[9,4,16,128]{3,2,1,0:T(8,128)S(1)}, f32[8,8,128]{2,1,0:T(8,128)S(1)}, f32[...) custom-call(f32[2,16,256]{2,1,0:T(8,128)} %current_hbm.1, ...), custom_call_target="tpu_custom_call" | custom-call | tf_op jit(solution)/shard_map/pallas_call | solution.py:609
  2.8 0.5 %collective-permute-start.4 = (f32[24,4,8,128]{3,2,1,0:T(8,128)S(1)}, f32[24,4,8,128]{3,2,1,0:T(8,128)S(1)}, u32[]{:S(2)}, u32[]{:S(2)}) collective-permute-start(f32[24,4,8,128]{3,2,1,0:T(8,128)S(1)} %get-tuple-element.24), channel_id=1, source_target_pairs={{28,0},{0,4},{4,8},{8,12},{12,16},{16,20},{20,24},{24,28},{29,1},{... | collective-permute-start | bytes 1179656 | tf_op jit(solution)/shard_map/ppermute | solution.py:28
  3.3 4.1 %collective-permute-start.5 = (f32[24,4,8,128]{3,2,1,0:T(8,128)S(1)}, f32[24,4,8,128]{3,2,1,0:T(8,128)S(1)}, u32[]{:S(2)}, u32[]{:S(2)}) collective-permute-start(f32[24,4,8,128]{3,2,1,0:T(8,128)S(1)} %get-tuple-element.25), channel_id=1, source_target_pairs={{4,0},{8,4},{12,8},{16,12},{20,16},{24,20},{28,24},{0,28},{5,1},{9... | collective-permute-start | bytes 1179656 | tf_op jit(solution)/shard_map/ppermute | solution.py:28
  7.4 1.6 %collective-permute-start.2 = (f32[2,16,256]{2,1,0:T(8,128)S(1)}, f32[2,16,256]{2,1,0:T(8,128)S(1)}, u32[]{:S(2)}, u32[]{:S(2)}) collective-permute-start(f32[2,16,256]{2,1,0:T(8,128)S(1)} %get-tuple-element.20.own_ref.masked_ref), channel_id=1, source_target_pairs={{5,0},{4,1},{7,2},{6,3},{9,4},{8,5},{11,6},{10,7},{13,8},{12,9},{1... | collective-permute-start | bytes 98312 | tf_op jit(solution)/shard_map/ppermute | solution.py:36
  9.0 1.8 %collective-permute-start.1 = (f32[2,16,256]{2,1,0:T(8,128)S(1)}, f32[2,16,256]{2,1,0:T(8,128)S(1)}, u32[]{:S(2)}, u32[]{:S(2)}) collective-permute-start(f32[2,16,256]{2,1,0:T(8,128)S(1)} %get-tuple-element.20.own_ref.masked_ref), channel_id=1, source_target_pairs={{4,0},{5,1},{6,2},{7,3},{8,4},{9,5},{10,6},{11,7},{12,8},{13,9},{1... | collective-permute-start | bytes 98312 | tf_op jit(solution)/shard_map/ppermute | solution.py:36
  10.9 0.5 %collective-permute-start = (f32[2,16,256]{2,1,0:T(8,128)S(1)}, f32[2,16,256]{2,1,0:T(8,128)S(1)}, u32[]{:S(2)}, u32[]{:S(2)}) collective-permute-start(f32[2,16,256]{2,1,0:T(8,128)S(1)} %get-tuple-element.20.own_ref.masked_ref), channel_id=1, source_target_pairs={{1,0},{0,1},{3,2},{2,3},{5,4},{4,5},{7,6},{6,7},{9,8},{8,9},{11,10... | collective-permute-start | bytes 98312 | tf_op jit(solution)/shard_map/ppermute | solution.py:36
  11.4 3.8 %collective-permute-done.2.xz_ref = f32[2,16,256]{2,1,0:T(8,128)S(1)} collective-permute-done((f32[2,16,256]{2,1,0:T(8,128)S(1)}, f32[2,16,256]{2,1,0:T(8,128)S(1)}, u32[]{:S(2)}, u32[]{:S(2)}) %collective-permute-start.2) | collective-permute-done | bytes 32800 | tf_op jit(solution)/shard_map/ppermute | solution.py:36
  15.2 0.4 collective-permute-done.1.z_ref
  15.6 0.0 collective-permute-done.x_ref
  15.6 0.4 shard_map.96.refs_0_
  16.0 1.6 %collective-permute-start.3 = (f32[3,2,16,128]{3,2,1,0:T(8,128)S(1)}, f32[3,2,16,128]{3,2,1,0:T(8,128)S(1)}, u32[]{:S(2)}, u32[]{:S(2)}) collective-permute-start(f32[3,2,16,128]{3,2,1,0:T(8,128)S(1)} %shard_map.96.refs_0_), channel_id=1, source_target_pairs={{2,0},{3,1},{0,2},{1,3},{6,4},{7,5},{4,6},{5,7},{10,8},{11,9},{8,1... | collective-permute-start | bytes 147464 | tf_op jit(solution)/shard_map/ppermute | solution.py:36
  17.6 2.6 %collective-permute-done.3.refs_1_ = f32[3,2,16,128]{3,2,1,0:T(8,128)S(1)} collective-permute-done((f32[3,2,16,128]{3,2,1,0:T(8,128)S(1)}, f32[3,2,16,128]{3,2,1,0:T(8,128)S(1)}, u32[]{:S(2)}, u32[]{:S(2)}) %collective-permute-start.3) | collective-permute-done | bytes 49184 | tf_op jit(solution)/shard_map/ppermute | solution.py:36
  20.1 0.0 copy-done
  20.1 0.0 copy-done.2
  20.1 0.0 copy-done.1
  20.1 3.3 %shard_map.97 = (f32[2,4,16,128]{3,2,1,0:T(8,128)S(1)}, f32[2,10,3,4,8,128]{5,4,3,2,1,0:T(8,128)S(1)}, f32[4,6,3,4,8,128]{5,4,3,2,1,0:T(8,128)S(1)}, f32[4,4,3,4...) custom-call(f32[3,2,16,128]{3,2,1,0:T(8,128)S(1)} %shard_map.96.refs_0_, ...), custom_call_target="tpu_custom_call" | custom-call | tf_op jit(solution)/shard_map/pallas_call | solution.py:658
  23.5 0.0 collective-permute-done.4.low_ref
  23.5 0.0 collective-permute-done.5.high_ref
  23.5 2.8 %shard_map.98 = (f32[4,4,3,4,8,128]{5,4,3,2,1,0:T(8,128)S(1)}, f32[3,4,8,128]{3,2,1,0:T(8,128)S(1)}) custom-call(f32[5,3,8,128]{3,2,1,0:T(8,128)S(1)} %copy-done, f32[16]{0:T(128)S(1)} %copy-done.1, f32[16]{0:T(128)S(1)} %copy-done.2, f32[4,4,24,8,128]{4,3,2,1,0:T(8,128)S(1)} %get-tuple-element.22.refs_5_.field_ref, ...), custom_call_target="tpu_custom_call" | custom-call | tf_op jit(solution)/shard_map/pallas_call | solution.py:673
  26.3 2.5 %collective-permute-start.9 = (f32[3,4,8,128]{3,2,1,0:T(8,128)S(1)}, f32[3,4,8,128]{3,2,1,0:T(8,128)S(1)}, u32[]{:S(2)}, u32[]{:S(2)}) collective-permute-start(f32[3,4,8,128]{3,2,1,0:T(8,128)S(1)} %get-tuple-element.33.own_ref), channel_id=1, source_target_pairs={{29,0},{28,1},{31,2},{30,3},{1,4},{0,5},{3,6},{2,7},{5,8},{4,9},{7... | collective-permute-start | bytes 147464 | tf_op jit(solution)/shard_map/ppermute | solution.py:36
  28.8 1.2 %collective-permute-start.8 = (f32[3,4,8,128]{3,2,1,0:T(8,128)S(1)}, f32[3,4,8,128]{3,2,1,0:T(8,128)S(1)}, u32[]{:S(2)}, u32[]{:S(2)}) collective-permute-start(f32[3,4,8,128]{3,2,1,0:T(8,128)S(1)} %get-tuple-element.33.own_ref), channel_id=1, source_target_pairs={{28,0},{29,1},{30,2},{31,3},{0,4},{1,5},{2,6},{3,7},{4,8},{5,9},{6... | collective-permute-start | bytes 147464 | tf_op jit(solution)/shard_map/ppermute | solution.py:36
  30.0 0.0 collective-permute-start.7
  30.0 2.6 %collective-permute-done.9.xz_ref = f32[3,4,8,128]{3,2,1,0:T(8,128)S(1)} collective-permute-done((f32[3,4,8,128]{3,2,1,0:T(8,128)S(1)}, f32[3,4,8,128]{3,2,1,0:T(8,128)S(1)}, u32[]{:S(2)}, u32[]{:S(2)}) %collective-permute-start.9) | collective-permute-done | bytes 49184 | tf_op jit(solution)/shard_map/ppermute | solution.py:36
  32.6 1.5 %collective-permute-done.8.z_ref = f32[3,4,8,128]{3,2,1,0:T(8,128)S(1)} collective-permute-done((f32[3,4,8,128]{3,2,1,0:T(8,128)S(1)}, f32[3,4,8,128]{3,2,1,0:T(8,128)S(1)}, u32[]{:S(2)}, u32[]{:S(2)}) %collective-permute-start.8) | collective-permute-done | bytes 49184 | tf_op jit(solution)/shard_map/ppermute | solution.py:36
  34.1 0.0 collective-permute-done.7.x_ref
  34.2 1.6 %collective-permute-start.10 = (f32[2,3,16,128]{3,2,1,0:T(8,128)S(1)}, f32[2,3,16,128]{3,2,1,0:T(8,128)S(1)}, u32[]{:S(2)}, u32[]{:S(2)}) collective-permute-start(f32[2,3,16,128]{3,2,1,0:T(8,128)S(1)} %get-tuple-element.35), channel_id=1, source_target_pairs={{2,0},{3,1},{0,2},{1,3},{6,4},{7,5},{4,6},{5,7},{10,8},{11,9},{8,1... | collective-permute-start | bytes 147464 | tf_op jit(solution)/shard_map/ppermute | solution.py:36
  35.8 0.0 collective-permute-start.6
  35.8 5.1 %collective-permute-done.6.tail_ref = f32[8,8,128]{2,1,0:T(8,128)S(1)} collective-permute-done((f32[8,8,128]{2,1,0:T(8,128)S(1)}, f32[8,8,128]{2,1,0:T(8,128)S(1)}, u32[]{:S(2)}, u32[]{:S(2)}) %collective-permute-start.6) | collective-permute-done | bytes 32800 | tf_op jit(solution)/shard_map/ppermute | solution.py:28
  40.9 1.4 %shard_map.99 = (f32[4,24,4,8,128]{4,3,2,1,0:T(8,128)}, f32[2,9,16,128]{3,2,1,0:T(8,128)S(1)}) custom-call(f32[4,4,3,4,8,128]{5,4,3,2,1,0:T(8,128)S(1)} %get-tuple-element.23.inner_ref, f32[4,4,3,4,8,128]{5,4,3,2,1,0:T(8,128)S(1)} %get-tuple-element.30.outer_ref, f32[8,8,128]{2,1,0:T(8,128)S(1)} %collective-permute-done.6.tail_ref, ...), custom_call_target="tpu_custom_call" | custom-call | tf_op jit(solution)/shard_map/pallas_call | solution.py:687
  42.3 0.0 collective-permute-done.10.come_ref
  42.3 1.0 %shard_map.101 = f32[2,16,256]{2,1,0:T(8,128)} custom-call(f32[2,3,16,128]{3,2,1,0:T(8,128)S(1)} %get-tuple-element.34.keep_ref, f32[2,3,16,128]{3,2,1,0:T(8,128)S(1)} %collective-permute-done.10.come_ref, f32[2,9,16,128]{3,2,1,0:T(8,128)S(1)} %get-tuple-element.36.coupling_ref, f32[2,16,256]{2,1,0:T(8,128)S(1)} %get-tuple-element.20.own_ref.masked_ref, ...), custom_call_target="tpu_custom_call" | custom-call | tf_op jit(solution)/shard_map/pallas_call | solution.py:700
  (1 shorter events, 0.0 us)
Async XLA Ops:
  0.6 19.5 %copy-start = (f32[5,3,8,128]{3,2,1,0:T(8,128)S(1)}, f32[5,3,8,128]{3,2,1,0:T(8,128)}, u32[]{:S(2)}) copy-start(f32[5,3,8,128]{3,2,1,0:T(8,128)} %constant.2.clone.refs_2_.trig_ref) | copy-start | bytes 184324
  0.6 19.5 %copy-start.2 = (f32[16]{0:T(128)S(1)}, f32[16]{0:T(128)}, u32[]{:S(2)}) copy-start(f32[16]{0:T(128)} %energy_ref.1) | copy-start | bytes 196
  0.7 19.5 %copy-start.1 = (f32[16]{0:T(128)S(1)}, f32[16]{0:T(128)}, u32[]{:S(2)}) copy-start(f32[16]{0:T(128)} %speed_ref.1) | copy-start | bytes 196
  2.8 20.7 %collective-permute-start.4 = (f32[24,4,8,128]{3,2,1,0:T(8,128)S(1)}, f32[24,4,8,128]{3,2,1,0:T(8,128)S(1)}, u32[]{:S(2)}, u32[]{:S(2)}) collective-permute-start(f32[24,4,8,128]{3,2,1,0:T(8,128)S(1)} %get-tuple-element.24), channel_id=1, source_target_pairs={{28,0},{0,4},{4,8},{8,12},{12,16},{16,20},{20,24},{24,28},{29,1},{... | collective-permute-start | bytes 1179656 | tf_op jit(solution)/shard_map/ppermute | solution.py:28
  3.3 20.2 %collective-permute-start.5 = (f32[24,4,8,128]{3,2,1,0:T(8,128)S(1)}, f32[24,4,8,128]{3,2,1,0:T(8,128)S(1)}, u32[]{:S(2)}, u32[]{:S(2)}) collective-permute-start(f32[24,4,8,128]{3,2,1,0:T(8,128)S(1)} %get-tuple-element.25), channel_id=1, source_target_pairs={{4,0},{8,4},{12,8},{16,12},{20,16},{24,20},{28,24},{0,28},{5,1},{9... | collective-permute-start | bytes 1179656 | tf_op jit(solution)/shard_map/ppermute | solution.py:28
  7.4 7.8 %collective-permute-start.2 = (f32[2,16,256]{2,1,0:T(8,128)S(1)}, f32[2,16,256]{2,1,0:T(8,128)S(1)}, u32[]{:S(2)}, u32[]{:S(2)}) collective-permute-start(f32[2,16,256]{2,1,0:T(8,128)S(1)} %get-tuple-element.20.own_ref.masked_ref), channel_id=1, source_target_pairs={{5,0},{4,1},{7,2},{6,3},{9,4},{8,5},{11,6},{10,7},{13,8},{12,9},{1... | collective-permute-start | bytes 98312 | tf_op jit(solution)/shard_map/ppermute | solution.py:36
  9.0 6.5 %collective-permute-start.1 = (f32[2,16,256]{2,1,0:T(8,128)S(1)}, f32[2,16,256]{2,1,0:T(8,128)S(1)}, u32[]{:S(2)}, u32[]{:S(2)}) collective-permute-start(f32[2,16,256]{2,1,0:T(8,128)S(1)} %get-tuple-element.20.own_ref.masked_ref), channel_id=1, source_target_pairs={{4,0},{5,1},{6,2},{7,3},{8,4},{9,5},{10,6},{11,7},{12,8},{13,9},{1... | collective-permute-start | bytes 98312 | tf_op jit(solution)/shard_map/ppermute | solution.py:36
  10.9 4.7 %collective-permute-start = (f32[2,16,256]{2,1,0:T(8,128)S(1)}, f32[2,16,256]{2,1,0:T(8,128)S(1)}, u32[]{:S(2)}, u32[]{:S(2)}) collective-permute-start(f32[2,16,256]{2,1,0:T(8,128)S(1)} %get-tuple-element.20.own_ref.masked_ref), channel_id=1, source_target_pairs={{1,0},{0,1},{3,2},{2,3},{5,4},{4,5},{7,6},{6,7},{9,8},{8,9},{11,10... | collective-permute-start | bytes 98312 | tf_op jit(solution)/shard_map/ppermute | solution.py:36
  16.0 4.2 %collective-permute-start.3 = (f32[3,2,16,128]{3,2,1,0:T(8,128)S(1)}, f32[3,2,16,128]{3,2,1,0:T(8,128)S(1)}, u32[]{:S(2)}, u32[]{:S(2)}) collective-permute-start(f32[3,2,16,128]{3,2,1,0:T(8,128)S(1)} %shard_map.96.refs_0_), channel_id=1, source_target_pairs={{2,0},{3,1},{0,2},{1,3},{6,4},{7,5},{4,6},{5,7},{10,8},{11,9},{8,1... | collective-permute-start | bytes 147464 | tf_op jit(solution)/shard_map/ppermute | solution.py:36
  26.3 6.3 %collective-permute-start.9 = (f32[3,4,8,128]{3,2,1,0:T(8,128)S(1)}, f32[3,4,8,128]{3,2,1,0:T(8,128)S(1)}, u32[]{:S(2)}, u32[]{:S(2)}) collective-permute-start(f32[3,4,8,128]{3,2,1,0:T(8,128)S(1)} %get-tuple-element.33.own_ref), channel_id=1, source_target_pairs={{29,0},{28,1},{31,2},{30,3},{1,4},{0,5},{3,6},{2,7},{5,8},{4,9},{7... | collective-permute-start | bytes 147464 | tf_op jit(solution)/shard_map/ppermute | solution.py:36
  28.8 5.3 %collective-permute-start.8 = (f32[3,4,8,128]{3,2,1,0:T(8,128)S(1)}, f32[3,4,8,128]{3,2,1,0:T(8,128)S(1)}, u32[]{:S(2)}, u32[]{:S(2)}) collective-permute-start(f32[3,4,8,128]{3,2,1,0:T(8,128)S(1)} %get-tuple-element.33.own_ref), channel_id=1, source_target_pairs={{28,0},{29,1},{30,2},{31,3},{0,4},{1,5},{2,6},{3,7},{4,8},{5,9},{6... | collective-permute-start | bytes 147464 | tf_op jit(solution)/shard_map/ppermute | solution.py:36
  30.0 4.1 %collective-permute-start.7 = (f32[3,4,8,128]{3,2,1,0:T(8,128)S(1)}, f32[3,4,8,128]{3,2,1,0:T(8,128)S(1)}, u32[]{:S(2)}, u32[]{:S(2)}) collective-permute-start(f32[3,4,8,128]{3,2,1,0:T(8,128)S(1)} %get-tuple-element.33.own_ref), channel_id=1, source_target_pairs={{1,0},{0,1},{3,2},{2,3},{5,4},{4,5},{7,6},{6,7},{9,8},{8,9},{11,10... | collective-permute-start | bytes 147464 | tf_op jit(solution)/shard_map/ppermute | solution.py:36
  34.2 8.1 %collective-permute-start.10 = (f32[2,3,16,128]{3,2,1,0:T(8,128)S(1)}, f32[2,3,16,128]{3,2,1,0:T(8,128)S(1)}, u32[]{:S(2)}, u32[]{:S(2)}) collective-permute-start(f32[2,3,16,128]{3,2,1,0:T(8,128)S(1)} %get-tuple-element.35), channel_id=1, source_target_pairs={{2,0},{3,1},{0,2},{1,3},{6,4},{7,5},{4,6},{5,7},{10,8},{11,9},{8,1... | collective-permute-start | bytes 147464 | tf_op jit(solution)/shard_map/ppermute | solution.py:36
  35.8 5.1 %collective-permute-start.6 = (f32[8,8,128]{2,1,0:T(8,128)S(1)}, f32[8,8,128]{2,1,0:T(8,128)S(1)}, u32[]{:S(2)}, u32[]{:S(2)}) collective-permute-start(f32[8,8,128]{2,1,0:T(8,128)S(1)} %get-tuple-element.31), channel_id=1, source_target_pairs={{28,0},{0,4},{4,8},{8,12},{12,16},{16,20},{20,24},{24,28},{29,1},{... | collective-permute-start | bytes 98312 | tf_op jit(solution)/shard_map/ppermute | solution.py:28

commit v4 on v3

--- a/solution.py
+++ b/solution.py
@@ -117,43 +117,34 @@
     return [index, lax.rem(index + tiles - 1, tiles)]
 
 
-def tile_copies(tiled, whole, sems, out):
+def tile_copies(tiled, whole, sems):
     freqs, tiles = tiled.shape[:2]
     for freq in range(freqs):
         for tile in range(tiles):
-            ends = (tiled.at[freq, tile], whole.at[freq, :, tile])
-            yield freq, pltpu.make_async_copy(*(ends if out else ends[::-1]), sems.at[freq, tile])
+            yield freq, pltpu.make_async_copy(tiled.at[freq, tile], whole.at[freq, :, tile], sems.at[freq, tile])
 
 
 def open_kernel(
     ocean_cols, tail_rows, axis, aligned, current_hbm, wet_hbm, src_hbm, weight_hbm, field_hbm,
     masked_ref, wet_out, table_ref, tail_ref, field_ref, low_ref, high_ref,
-    current_ref, wet_ref, src_ref, weight_ref, sems, field_sems,
+    current_ref, wet_ref, src_ref, weight_ref, raw_ref, sems, field_sems,
 ):
     copies = [
         pltpu.make_async_copy(source, target, sems.at[k])
         for k, (source, target) in enumerate(
-            (
-                (current_hbm, current_ref),
-                (wet_hbm, wet_ref),
-                (src_hbm, src_ref),
-                (weight_hbm, weight_ref),
-            )
+            ((current_hbm, current_ref), (wet_hbm, wet_ref), (src_hbm, src_ref), (weight_hbm, weight_ref))
         )
     ]
-    moves = list(tile_copies(field_ref, field_hbm, field_sems, False))
+    list_rows, corners, columns = src_ref.shape
+    freqs, tiles, directions, wave_rows, _ = field_ref.shape
+    moves = [
+        pltpu.make_async_copy(field_hbm.at[freq], raw_ref.at[freq], field_sems.at[freq]) for freq in range(freqs)
+    ]
     for copy in copies:
         copy.start()
-    for _, copy in moves:
+    for copy in moves:
         copy.start()
-    list_rows, corners, columns = src_ref.shape
-    freqs, tiles, directions, wave_rows, _ = field_ref.shape
     groups = directions // 8
-    copies[0].wait()
-    copies[1].wait()
-    wet = wet_ref[...].astype(jnp.float32)
-    wet_out[...] = wet
-    masked_ref[...] = current_ref[...] * wet[None]
     shape = (list_rows, columns)
     entry_row = lax.broadcasted_iota(jnp.int32, shape, 0)
     column = lax.broadcasted_iota(jnp.int32, shape, 1)
@@ -162,8 +153,11 @@
         base + jnp.where(2 * column + step >= ocean_cols, 2 * column + step - ocean_cols, 2 * column + step)
         for step in range(3)
     ]
-    copies[2].wait()
-    copies[3].wait()
+    for copy in copies:
+        copy.wait()
+    wet = wet_ref[...].astype(jnp.float32)
+    wet_out[...] = wet
+    masked_ref[...] = current_ref[...] * wet[None]
     sums = [jnp.zeros(shape, jnp.float32) for _ in range(9)]
     for corner in range(corners):
         source = src_ref[:, corner, :]
@@ -183,9 +177,9 @@
                 vreg, line = tail_slot(which, place * tail_rows + row)
                 tail_ref[vreg, line : line + 1, :] = table_ref[place, tile, first + row : first + row + 1, :]
     for freq in range(freqs):
-        for other, copy in moves:
-            if other == freq:
-                copy.wait()
+        moves[freq].wait()
+        for tile in range(tiles):
+            field_ref[freq, tile] = raw_ref[freq, :, tile]
         view = row_view(field_ref, freq)
         for row in range(2):
             at = (freq * 2 + row) * groups
@@ -211,38 +205,32 @@
     return [ref[parity, tile, comp, pl.ds(first + step, list_rows, stride=2), :] for step in range(3)]
 
 
-def flow_kernel(axis, list_rows, first, own_ref, x_ref, z_ref, xz_ref, table_ref, part_ref, ocean_ref):
+def flow_kernel(axis, list_rows, first, own_ref, current_ref, wet_ref, table_ref, part_ref, ocean_ref):
     comps, rows, width = own_ref.shape
     tiles = table_ref.shape[1]
     half = width // 2
-    index = lax.axis_index(axis)
-    place = lax.rem(index, 2)
-    matrix = split_matrix(width)
-    cells = jnp.concatenate(
-        [ref[...].reshape(comps * rows, width) for ref in (own_ref, z_ref, x_ref, xz_ref)], axis=0
-    )
-    split = jnp.dot(cells, matrix, precision=HIGHEST, preferred_element_type=jnp.float32)
-    split = split.reshape(4, comps, rows, width)
+    tile = lax.axis_index(axis)
+    after = current_ref[...] * wet_ref[...].astype(jnp.float32)[None]
+    cells = jnp.concatenate([x.reshape(comps * rows, width) for x in (own_ref[...], after)], axis=0)
+    split = jnp.dot(cells, split_matrix(width), precision=HIGHEST, preferred_element_type=jnp.float32)
+    split = split.reshape(2, comps, rows, width)
     for parity in range(2):
-        lanes = slice(parity * half, (parity + 1) * half)
         for block in range(2):
-            at = slice(block * rows, (block + 1) * rows)
-            ocean_ref[parity, place, :, at] = split[block, :, :, lanes]
-            ocean_ref[parity, 1 - place, :, at] = split[2 + block, :, :, lanes]
-    tile = index - place
+            ocean_ref[parity, 0, :, block * rows : (block + 1) * rows] = split[
+                block, :, :, parity * half : (parity + 1) * half
+            ]
     before = lax.rem(tile + tiles - 1, tiles)
+    lane = lax.broadcasted_iota(jnp.int32, (list_rows, LANES), 1)
     for comp in range(comps):
-        evens = [row_steps(ocean_ref, 0, k, comp, first, list_rows) for k in range(2)]
-        odds = [row_steps(ocean_ref, 1, k, comp, first, list_rows) for k in range(2)]
-        part_ref[0, comp, :list_rows] = flow_tile(table_ref, tile, evens[0], odds[0], evens[1])
-        part_ref[1, comp, :list_rows] = flow_tile(table_ref, tile + 1, evens[1], odds[1], None)
-        lane = lax.broadcasted_iota(jnp.int32, (list_rows, LANES), 1)
+        even = row_steps(ocean_ref, 0, 0, comp, first, list_rows)
+        odd = row_steps(ocean_ref, 1, 0, comp, first, list_rows)
+        part_ref[0, comp, :list_rows] = flow_tile(table_ref, tile, even, odd, None)
         spill = None
         for step in range(3):
-            edge = jnp.where(lane == LANES - 1, pltpu.roll(evens[0][step], LANES - 1, 1), 0.0)
+            edge = jnp.where(lane == LANES - 1, pltpu.roll(even[step], LANES - 1, 1), 0.0)
             term = table_ref[3 * step + 2, before, :list_rows] * edge
             spill = term if spill is None else spill + term
-        part_ref[2, comp, :list_rows] = spill
+        part_ref[1, comp, :list_rows] = spill
 
 
 def flow_all_kernel(list_rows, first, ocean_ref, table_ref, flow_ref):
@@ -333,13 +321,10 @@
             for tile in range(tiles):
                 flow_ref[comp, tile] = part_refs[0][tile, comp]
         else:
-            tile = index - lax.rem(index, 2)
-            other = tiles // 2 - tile
-            own, theirs = part_refs
-            flow_ref[comp, tile] = own[0, comp]
-            flow_ref[comp, tile + 1] = own[1, comp] + theirs[2, comp]
-            flow_ref[comp, other] = theirs[0, comp]
-            flow_ref[comp, other + 1] = theirs[1, comp] + own[2, comp]
+            for bits in range(parts):
+                flow_ref[comp, index ^ bits] = part_refs[bits][0, comp]
+            for bits in range(parts):
+                flow_ref[comp, lax.rem((index ^ bits) + tiles - 1, tiles)] += part_refs[bits][1, comp]
     inner = list_rows - 2
     east, north = flow_ref[0, :, 1 : 1 + inner], flow_ref[1, :, 1 : 1 + inner]
     east_y = (flow_ref[0, :, 2 : 2 + inner] - flow_ref[0, :, 0:inner]) * 0.5
@@ -460,7 +445,7 @@
     axis, aligned, tail_rows, inner_ref, outer_ref, tail_ref, table_ref, out_hbm, coupling_ref, field_ref, sems
 ):
     freqs, tiles, _, wave_rows, _ = field_ref.shape
-    moves = list(tile_copies(field_ref, out_hbm, sems, True))
+    moves = list(tile_copies(field_ref, out_hbm, sems))
     for freq in range(freqs):
         sink = row_view(field_ref, freq)
         for row in range(wave_rows):
@@ -606,6 +591,8 @@
     source, weight = jnp.transpose(src, (0, 2, 1)), jnp.transpose(weights, (0, 2, 1))
     cell = (groups, tiles, 8, LANES)
     home = (freqs, tiles, directions, wave_rows, LANES)
+    z_current = from_offset(currents, "space", 1)
+    z_wet = from_offset(wet, "space", 1)
     masked, wet_float, tables, tail, held, low, high = call(
         functools.partial(open_kernel, ocean_cols, tail_rows, "spec", aligned),
         (
@@ -623,28 +610,26 @@
             pltpu.VMEM(wet.shape, jnp.int32),
             pltpu.VMEM(source.shape, jnp.int32),
             pltpu.VMEM(weight.shape, f32),
+            pltpu.VMEM(field.shape, f32),
             pltpu.SemaphoreType.DMA((4,)),
-            pltpu.SemaphoreType.DMA((freqs, tiles)),
+            pltpu.SemaphoreType.DMA((freqs,)),
         ],
     )(*in_hbm(currents, wet, source, weight, field))
-    if aligned:
-        xz = from_mesh(masked, 1, 1)
-        z = from_mesh(masked, 1, 0)
-        x = from_mesh(masked, 0, 1)
-    else:
-        z = from_offset(masked, "space", 1)
     low = from_offset(low, "space", -1)
     high = from_offset(high, "space", 1)
     tail = from_offset(tail, "space", -1)
     if aligned:
         (part,) = call(
             functools.partial(flow_kernel, "spec", list_rows, first),
-            ((3, 2, padded, LANES),),
-            [VMEM] * 5,
-            scratch_shapes=[pltpu.VMEM((2, 2, 2, 2 * ocean_rows, LANES), f32)],
-        )(masked, x, z, xz, tables)
-        parts = [part, from_mesh(part, 0, 2)]
+            ((2, 2, padded, LANES),),
+            [VMEM] * 4,
+            scratch_shapes=[pltpu.VMEM((2, 1, 2, 2 * ocean_rows, LANES), f32)],
+        )(masked, z_current, z_wet, tables)
+        parts = [part]
+        for bits in range(1, spec):
+            parts.append(from_mesh(part, 0, bits))
     else:
+        z = z_current * z_wet.astype(f32)[None]
         both = lax.all_gather(jnp.concatenate([masked, z], axis=1), "spec", axis=2, tiled=True)
         ocean = both.reshape(2, 2 * ocean_rows, tiles, LANES, 2).transpose(4, 2, 0, 1, 3)
         parts = call(

time: 43.4 us -> 44.8 us (1.032)
  waiting for transfers between devices: 16 us -> 17.1 us
  starting transfers between devices: 15.5 us -> 16 us
    ppermute x3 -> x5, waiting for transfers between devices: 5.14 us -> 10.8 us  [from_offset(): lax.ppermute(block, axis, [((i + offset) % count, i) for i in range(count)])]
    ppermute x8 -> x7, waiting for transfers between devices: 10.8 us -> 6.34 us  [from_mesh(): return lax.ppermute(block, ('space', 'spec'), route)]
    ppermute x3 -> x5, starting transfers between devices: 4.64 us -> 6.99 us  [from_offset(): lax.ppermute(block, axis, [((i + offset) % count, i) for i in range(count)])]
    ppermute x8 -> x7, starting transfers between devices: 10.9 us -> 8.97 us  [from_mesh(): return lax.ppermute(block, ('space', 'spec'), route)]
  transfers between devices with their start and end apart: 11 -> 12, of which waited for: 6 -> 7; matrix products, arithmetic and copies ran while one was open for 0% -> 0% of each run, Pallas kernels for 12% -> 11%
where the time goes in v4:
time: 44.8 us; the launch traced here: 44.6 us
  waiting for transfers between devices  17.1 us (38%)
  starting transfers between devices  16 us (36%)
  Pallas kernels  10.8 us (24%)
  between operations  0.75 us (2%)
    ppermute x5, waiting for transfers between devices, from_offset(): lax.ppermute(block, axis, [((i + offset) % count, i) for i in range(count)])  10.8 us
    ppermute x7, starting transfers between devices, from_mesh(): return lax.ppermute(block, ('space', 'spec'), route)  8.97 us
    ppermute x5, starting transfers between devices, from_offset(): lax.ppermute(block, axis, [((i + offset) % count, i) for i in range(count)])  6.99 us
    ppermute x7, waiting for transfers between devices, from_mesh(): return lax.ppermute(block, ('space', 'spec'), route)  6.34 us
    pallas_call x1, Pallas kernels, window(): call(functools.partial(inner_kernel, freqs * spec, 'spec', list_rows, len...  3.31 us
    pallas_call x1, Pallas kernels, window(): call(functools.partial(outer_kernel, freqs * spec, 'spec'), ((freqs, 4) +...  2.85 us
    pallas_call x1, Pallas kernels, window(): call(functools.partial(open_kernel, ocean_cols, tail_rows, 'spec', aligne...  1.87 us
    pallas_call x1, Pallas kernels, window(): call(functools.partial(settle_kernel, 'spec', aligned, tail_rows), (field...  1.36 us
  transfers between devices with their start and end apart: 12, of which 7 were waited for; matrix products, arithmetic and copies ran while one was open for 0% of the time, Pallas kernels for 11%

profile of v4, /device:TPU:0, one launch (start us, length us, event | category | flops | bytes accessed | tf_op | source)
XLA Modules:
  0.0 44.6 jit_solution(11206598919151140250)
XLA Ops:
  0.6 0.0 copy-start
  0.6 0.0 copy-start.4
  0.7 0.0 copy-start.3
  0.7 0.0 copy-start.2
  0.7 0.0 copy-start.1
  0.7 1.9 %shard_map.95 = (f32[2,16,256]{2,1,0:T(8,128)S(1)}, f32[16,256]{1,0:T(8,128)S(1)}, f32[9,4,16,128]{3,2,1,0:T(8,128)S(1)}, f32[8,8,128]{2,1,0:T(8,128)S(1)}, f32[...) custom-call(f32[2,16,256]{2,1,0:T(8,128)} %current_hbm.1, ...), custom_call_target="tpu_custom_call" | custom-call | tf_op jit(solution)/shard_map/pallas_call | solution.py:596
  2.6 0.5 %collective-permute-start.5 = (f32[24,4,8,128]{3,2,1,0:T(8,128)S(1)}, f32[24,4,8,128]{3,2,1,0:T(8,128)S(1)}, u32[]{:S(2)}, u32[]{:S(2)}) collective-permute-start(f32[24,4,8,128]{3,2,1,0:T(8,128)S(1)} %get-tuple-element.24), channel_id=1, source_target_pairs={{28,0},{0,4},{4,8},{8,12},{12,16},{16,20},{20,24},{24,28},{29,1},{... | collective-permute-start | bytes 1179656 | tf_op jit(solution)/shard_map/ppermute | solution.py:28
  3.1 4.1 %collective-permute-start.6 = (f32[24,4,8,128]{3,2,1,0:T(8,128)S(1)}, f32[24,4,8,128]{3,2,1,0:T(8,128)S(1)}, u32[]{:S(2)}, u32[]{:S(2)}) collective-permute-start(f32[24,4,8,128]{3,2,1,0:T(8,128)S(1)} %get-tuple-element.25), channel_id=1, source_target_pairs={{4,0},{8,4},{12,8},{16,12},{20,16},{24,20},{28,24},{0,28},{5,1},{9... | collective-permute-start | bytes 1179656 | tf_op jit(solution)/shard_map/ppermute | solution.py:28
  7.2 0.0 copy-done.3
  7.2 0.7 %collective-permute-start = (f32[2,16,256]{2,1,0:T(8,128)S(1)}, f32[2,16,256]{2,1,0:T(8,128)S(1)}, u32[]{:S(2)}, u32[]{:S(2)}) collective-permute-start(f32[2,16,256]{2,1,0:T(8,128)S(1)} %copy-done.3), channel_id=1, source_target_pairs={{4,0},{8,4},{12,8},{16,12},{20,16},{24,20},{28,24},{0,28},{5,1},{9... | collective-permute-start | bytes 98312 | tf_op jit(solution)/shard_map/ppermute | solution.py:28
  7.9 0.0 copy-done.4
  7.9 1.7 %collective-permute-start.1 = (s32[16,256]{1,0:T(8,128)S(1)}, s32[16,256]{1,0:T(8,128)S(1)}, u32[]{:S(2)}, u32[]{:S(2)}) collective-permute-start(s32[16,256]{1,0:T(8,128)S(1)} %copy-done.4), channel_id=1, source_target_pairs={{4,0},{8,4},{12,8},{16,12},{20,16},{24,20},{28,24},{0,28},{5,1},{9... | collective-permute-start | bytes 49160 | tf_op jit(solution)/shard_map/ppermute | solution.py:28
  9.6 5.6 %collective-permute-done.1.wet_ref = s32[16,256]{1,0:T(8,128)S(1)} collective-permute-done((s32[16,256]{1,0:T(8,128)S(1)}, s32[16,256]{1,0:T(8,128)S(1)}, u32[]{:S(2)}, u32[]{:S(2)}) %collective-permute-start.1) | collective-permute-done | bytes 16416 | tf_op jit(solution)/shard_map/ppermute | solution.py:28
  15.2 0.0 collective-permute-done.current_ref
  15.2 0.3 shard_map.96.refs_0_
  15.5 2.5 %collective-permute-start.4 = (f32[2,2,16,128]{3,2,1,0:T(8,128)S(1)}, f32[2,2,16,128]{3,2,1,0:T(8,128)S(1)}, u32[]{:S(2)}, u32[]{:S(2)}) collective-permute-start(f32[2,2,16,128]{3,2,1,0:T(8,128)S(1)} %shard_map.96.refs_0_), channel_id=1, source_target_pairs={{3,0},{2,1},{1,2},{0,3},{7,4},{6,5},{5,6},{4,7},{11,8},{10,9},{9,1... | collective-permute-start | bytes 98312 | tf_op jit(solution)/shard_map/ppermute | solution.py:36
  18.0 0.5 %collective-permute-start.3 = (f32[2,2,16,128]{3,2,1,0:T(8,128)S(1)}, f32[2,2,16,128]{3,2,1,0:T(8,128)S(1)}, u32[]{:S(2)}, u32[]{:S(2)}) collective-permute-start(f32[2,2,16,128]{3,2,1,0:T(8,128)S(1)} %shard_map.96.refs_0_), channel_id=1, source_target_pairs={{2,0},{3,1},{0,2},{1,3},{6,4},{7,5},{4,6},{5,7},{10,8},{11,9},{8,1... | collective-permute-start | bytes 98312 | tf_op jit(solution)/shard_map/ppermute | solution.py:36
  18.6 0.5 %collective-permute-start.2 = (f32[2,2,16,128]{3,2,1,0:T(8,128)S(1)}, f32[2,2,16,128]{3,2,1,0:T(8,128)S(1)}, u32[]{:S(2)}, u32[]{:S(2)}) collective-permute-start(f32[2,2,16,128]{3,2,1,0:T(8,128)S(1)} %shard_map.96.refs_0_), channel_id=1, source_target_pairs={{1,0},{0,1},{3,2},{2,3},{5,4},{4,5},{7,6},{6,7},{9,8},{8,9},{11,10... | collective-permute-start | bytes 98312 | tf_op jit(solution)/shard_map/ppermute | solution.py:36
  19.1 1.3 %collective-permute-done.4.refs_3_ = f32[2,2,16,128]{3,2,1,0:T(8,128)S(1)} collective-permute-done((f32[2,2,16,128]{3,2,1,0:T(8,128)S(1)}, f32[2,2,16,128]{3,2,1,0:T(8,128)S(1)}, u32[]{:S(2)}, u32[]{:S(2)}) %collective-permute-start.4) | collective-permute-done | bytes 32800 | tf_op jit(solution)/shard_map/ppermute | solution.py:36
  20.4 1.7 %collective-permute-done.3.refs_2_ = f32[2,2,16,128]{3,2,1,0:T(8,128)S(1)} collective-permute-done((f32[2,2,16,128]{3,2,1,0:T(8,128)S(1)}, f32[2,2,16,128]{3,2,1,0:T(8,128)S(1)}, u32[]{:S(2)}, u32[]{:S(2)}) %collective-permute-start.3) | collective-permute-done | bytes 32800 | tf_op jit(solution)/shard_map/ppermute | solution.py:36
  22.1 0.4 collective-permute-done.2.refs_1_
  22.5 0.0 copy-done
  22.5 0.0 copy-done.2
  22.5 0.0 copy-done.1
  22.5 3.3 %shard_map.97 = (f32[2,4,16,128]{3,2,1,0:T(8,128)S(1)}, f32[2,10,3,4,8,128]{5,4,3,2,1,0:T(8,128)S(1)}, f32[4,6,3,4,8,128]{5,4,3,2,1,0:T(8,128)S(1)}, f32[4,4,3,4...) custom-call(f32[2,2,16,128]{3,2,1,0:T(8,128)S(1)} %shard_map.96.refs_0_, ...), custom_call_target="tpu_custom_call" | custom-call | tf_op jit(solution)/shard_map/pallas_call | solution.py:643
  25.8 0.0 collective-permute-done.5.low_ref
  25.8 0.0 collective-permute-done.6.high_ref
  25.8 2.8 %shard_map.98 = (f32[4,4,3,4,8,128]{5,4,3,2,1,0:T(8,128)S(1)}, f32[3,4,8,128]{3,2,1,0:T(8,128)S(1)}) custom-call(f32[5,3,8,128]{3,2,1,0:T(8,128)S(1)} %copy-done, f32[16]{0:T(128)S(1)} %copy-done.1, f32[16]{0:T(128)S(1)} %copy-done.2, f32[4,4,24,8,128]{4,3,2,1,0:T(8,128)S(1)} %get-tuple-element.22.refs_7_.field_ref, ...), custom_call_target="tpu_custom_call" | custom-call | tf_op jit(solution)/shard_map/pallas_call | solution.py:658
  28.7 0.8 %collective-permute-start.10 = (f32[3,4,8,128]{3,2,1,0:T(8,128)S(1)}, f32[3,4,8,128]{3,2,1,0:T(8,128)S(1)}, u32[]{:S(2)}, u32[]{:S(2)}) collective-permute-start(f32[3,4,8,128]{3,2,1,0:T(8,128)S(1)} %get-tuple-element.33.own_ref), channel_id=1, source_target_pairs={{29,0},{28,1},{31,2},{30,3},{1,4},{0,5},{3,6},{2,7},{5,8},{4,9},{7... | collective-permute-start | bytes 147464 | tf_op jit(solution)/shard_map/ppermute | solution.py:36
  29.5 1.4 %collective-permute-start.9 = (f32[3,4,8,128]{3,2,1,0:T(8,128)S(1)}, f32[3,4,8,128]{3,2,1,0:T(8,128)S(1)}, u32[]{:S(2)}, u32[]{:S(2)}) collective-permute-start(f32[3,4,8,128]{3,2,1,0:T(8,128)S(1)} %get-tuple-element.33.own_ref), channel_id=1, source_target_pairs={{28,0},{29,1},{30,2},{31,3},{0,4},{1,5},{2,6},{3,7},{4,8},{5,9},{6... | collective-permute-start | bytes 147464 | tf_op jit(solution)/shard_map/ppermute | solution.py:36
  30.9 1.6 %collective-permute-start.8 = (f32[3,4,8,128]{3,2,1,0:T(8,128)S(1)}, f32[3,4,8,128]{3,2,1,0:T(8,128)S(1)}, u32[]{:S(2)}, u32[]{:S(2)}) collective-permute-start(f32[3,4,8,128]{3,2,1,0:T(8,128)S(1)} %get-tuple-element.33.own_ref), channel_id=1, source_target_pairs={{1,0},{0,1},{3,2},{2,3},{5,4},{4,5},{7,6},{6,7},{9,8},{8,9},{11,10... | collective-permute-start | bytes 147464 | tf_op jit(solution)/shard_map/ppermute | solution.py:36
  32.5 2.5 %collective-permute-done.10.xz_ref = f32[3,4,8,128]{3,2,1,0:T(8,128)S(1)} collective-permute-done((f32[3,4,8,128]{3,2,1,0:T(8,128)S(1)}, f32[3,4,8,128]{3,2,1,0:T(8,128)S(1)}, u32[]{:S(2)}, u32[]{:S(2)}) %collective-permute-start.10) | collective-permute-done | bytes 49184 | tf_op jit(solution)/shard_map/ppermute | solution.py:36
  35.0 0.0 collective-permute-done.9.z_ref
  35.0 0.5 %collective-permute-done.8.x_ref = f32[3,4,8,128]{3,2,1,0:T(8,128)S(1)} collective-permute-done((f32[3,4,8,128]{3,2,1,0:T(8,128)S(1)}, f32[3,4,8,128]{3,2,1,0:T(8,128)S(1)}, u32[]{:S(2)}, u32[]{:S(2)}) %collective-permute-start.8) | collective-permute-done | bytes 49184 | tf_op jit(solution)/shard_map/ppermute | solution.py:36
  35.5 1.6 %collective-permute-start.11 = (f32[2,3,16,128]{3,2,1,0:T(8,128)S(1)}, f32[2,3,16,128]{3,2,1,0:T(8,128)S(1)}, u32[]{:S(2)}, u32[]{:S(2)}) collective-permute-start(f32[2,3,16,128]{3,2,1,0:T(8,128)S(1)} %get-tuple-element.35), channel_id=1, source_target_pairs={{2,0},{3,1},{0,2},{1,3},{6,4},{7,5},{4,6},{5,7},{10,8},{11,9},{8,1... | collective-permute-start | bytes 147464 | tf_op jit(solution)/shard_map/ppermute | solution.py:36
  37.1 0.0 collective-permute-start.7
  37.1 5.1 %collective-permute-done.7.tail_ref = f32[8,8,128]{2,1,0:T(8,128)S(1)} collective-permute-done((f32[8,8,128]{2,1,0:T(8,128)S(1)}, f32[8,8,128]{2,1,0:T(8,128)S(1)}, u32[]{:S(2)}, u32[]{:S(2)}) %collective-permute-start.7) | collective-permute-done | bytes 32800 | tf_op jit(solution)/shard_map/ppermute | solution.py:28
  42.2 1.4 %shard_map.99 = (f32[4,24,4,8,128]{4,3,2,1,0:T(8,128)}, f32[2,9,16,128]{3,2,1,0:T(8,128)S(1)}) custom-call(f32[4,4,3,4,8,128]{5,4,3,2,1,0:T(8,128)S(1)} %get-tuple-element.23.inner_ref, f32[4,4,3,4,8,128]{5,4,3,2,1,0:T(8,128)S(1)} %get-tuple-element.30.outer_ref, f32[8,8,128]{2,1,0:T(8,128)S(1)} %collective-permute-done.7.tail_ref, ...), custom_call_target="tpu_custom_call" | custom-call | tf_op jit(solution)/shard_map/pallas_call | solution.py:672
  43.6 0.0 collective-permute-done.11.come_ref
  43.6 1.0 %shard_map.101 = f32[2,16,256]{2,1,0:T(8,128)} custom-call(f32[2,3,16,128]{3,2,1,0:T(8,128)S(1)} %get-tuple-element.34.keep_ref, f32[2,3,16,128]{3,2,1,0:T(8,128)S(1)} %collective-permute-done.11.come_ref, f32[2,9,16,128]{3,2,1,0:T(8,128)S(1)} %get-tuple-element.36.coupling_ref, f32[2,16,256]{2,1,0:T(8,128)S(1)} %get-tuple-element.20.own_ref.masked_ref, ...), custom_call_target="tpu_custom_call" | custom-call | tf_op jit(solution)/shard_map/pallas_call | solution.py:685
  (1 shorter events, 0.0 us)
Async XLA Ops:
  0.6 21.8 %copy-start = (f32[5,3,8,128]{3,2,1,0:T(8,128)S(1)}, f32[5,3,8,128]{3,2,1,0:T(8,128)}, u32[]{:S(2)}) copy-start(f32[5,3,8,128]{3,2,1,0:T(8,128)} %constant.2.clone.refs_4_.trig_ref) | copy-start | bytes 184324
  0.6 7.2 %copy-start.4 = (s32[16,256]{1,0:T(8,128)S(1)}, s32[16,256]{1,0:T(8,128)}, u32[]{:S(2)}) copy-start(s32[16,256]{1,0:T(8,128)} %wet_hbm.1) | copy-start | bytes 49156
  0.7 6.5 %copy-start.3 = (f32[2,16,256]{2,1,0:T(8,128)S(1)}, f32[2,16,256]{2,1,0:T(8,128)}, u32[]{:S(2)}) copy-start(f32[2,16,256]{2,1,0:T(8,128)} %current_hbm.1) | copy-start | bytes 98308
  0.7 21.8 %copy-start.2 = (f32[16]{0:T(128)S(1)}, f32[16]{0:T(128)}, u32[]{:S(2)}) copy-start(f32[16]{0:T(128)} %energy_ref.1) | copy-start | bytes 196
  0.7 21.8 %copy-start.1 = (f32[16]{0:T(128)S(1)}, f32[16]{0:T(128)}, u32[]{:S(2)}) copy-start(f32[16]{0:T(128)} %speed_ref.1) | copy-start | bytes 196
  2.6 23.2 %collective-permute-start.5 = (f32[24,4,8,128]{3,2,1,0:T(8,128)S(1)}, f32[24,4,8,128]{3,2,1,0:T(8,128)S(1)}, u32[]{:S(2)}, u32[]{:S(2)}) collective-permute-start(f32[24,4,8,128]{3,2,1,0:T(8,128)S(1)} %get-tuple-element.24), channel_id=1, source_target_pairs={{28,0},{0,4},{4,8},{8,12},{12,16},{16,20},{20,24},{24,28},{29,1},{... | collective-permute-start | bytes 1179656 | tf_op jit(solution)/shard_map/ppermute | solution.py:28
  3.1 22.7 %collective-permute-start.6 = (f32[24,4,8,128]{3,2,1,0:T(8,128)S(1)}, f32[24,4,8,128]{3,2,1,0:T(8,128)S(1)}, u32[]{:S(2)}, u32[]{:S(2)}) collective-permute-start(f32[24,4,8,128]{3,2,1,0:T(8,128)S(1)} %get-tuple-element.25), channel_id=1, source_target_pairs={{4,0},{8,4},{12,8},{16,12},{20,16},{24,20},{28,24},{0,28},{5,1},{9... | collective-permute-start | bytes 1179656 | tf_op jit(solution)/shard_map/ppermute | solution.py:28
  7.2 8.0 %collective-permute-start = (f32[2,16,256]{2,1,0:T(8,128)S(1)}, f32[2,16,256]{2,1,0:T(8,128)S(1)}, u32[]{:S(2)}, u32[]{:S(2)}) collective-permute-start(f32[2,16,256]{2,1,0:T(8,128)S(1)} %copy-done.3), channel_id=1, source_target_pairs={{4,0},{8,4},{12,8},{16,12},{20,16},{24,20},{28,24},{0,28},{5,1},{9... | collective-permute-start | bytes 98312 | tf_op jit(solution)/shard_map/ppermute | solution.py:28
  7.9 7.3 %collective-permute-start.1 = (s32[16,256]{1,0:T(8,128)S(1)}, s32[16,256]{1,0:T(8,128)S(1)}, u32[]{:S(2)}, u32[]{:S(2)}) collective-permute-start(s32[16,256]{1,0:T(8,128)S(1)} %copy-done.4), channel_id=1, source_target_pairs={{4,0},{8,4},{12,8},{16,12},{20,16},{24,20},{28,24},{0,28},{5,1},{9... | collective-permute-start | bytes 49160 | tf_op jit(solution)/shard_map/ppermute | solution.py:28
  15.5 4.9 %collective-permute-start.4 = (f32[2,2,16,128]{3,2,1,0:T(8,128)S(1)}, f32[2,2,16,128]{3,2,1,0:T(8,128)S(1)}, u32[]{:S(2)}, u32[]{:S(2)}) collective-permute-start(f32[2,2,16,128]{3,2,1,0:T(8,128)S(1)} %shard_map.96.refs_0_), channel_id=1, source_target_pairs={{3,0},{2,1},{1,2},{0,3},{7,4},{6,5},{5,6},{4,7},{11,8},{10,9},{9,1... | collective-permute-start | bytes 98312 | tf_op jit(solution)/shard_map/ppermute | solution.py:36
  18.0 4.0 %collective-permute-start.3 = (f32[2,2,16,128]{3,2,1,0:T(8,128)S(1)}, f32[2,2,16,128]{3,2,1,0:T(8,128)S(1)}, u32[]{:S(2)}, u32[]{:S(2)}) collective-permute-start(f32[2,2,16,128]{3,2,1,0:T(8,128)S(1)} %shard_map.96.refs_0_), channel_id=1, source_target_pairs={{2,0},{3,1},{0,2},{1,3},{6,4},{7,5},{4,6},{5,7},{10,8},{11,9},{8,1... | collective-permute-start | bytes 98312 | tf_op jit(solution)/shard_map/ppermute | solution.py:36
  18.6 3.9 %collective-permute-start.2 = (f32[2,2,16,128]{3,2,1,0:T(8,128)S(1)}, f32[2,2,16,128]{3,2,1,0:T(8,128)S(1)}, u32[]{:S(2)}, u32[]{:S(2)}) collective-permute-start(f32[2,2,16,128]{3,2,1,0:T(8,128)S(1)} %shard_map.96.refs_0_), channel_id=1, source_target_pairs={{1,0},{0,1},{3,2},{2,3},{5,4},{4,5},{7,6},{6,7},{9,8},{8,9},{11,10... | collective-permute-start | bytes 98312 | tf_op jit(solution)/shard_map/ppermute | solution.py:36
  28.7 6.3 %collective-permute-start.10 = (f32[3,4,8,128]{3,2,1,0:T(8,128)S(1)}, f32[3,4,8,128]{3,2,1,0:T(8,128)S(1)}, u32[]{:S(2)}, u32[]{:S(2)}) collective-permute-start(f32[3,4,8,128]{3,2,1,0:T(8,128)S(1)} %get-tuple-element.33.own_ref), channel_id=1, source_target_pairs={{29,0},{28,1},{31,2},{30,3},{1,4},{0,5},{3,6},{2,7},{5,8},{4,9},{7... | collective-permute-start | bytes 147464 | tf_op jit(solution)/shard_map/ppermute | solution.py:36
  29.5 5.5 %collective-permute-start.9 = (f32[3,4,8,128]{3,2,1,0:T(8,128)S(1)}, f32[3,4,8,128]{3,2,1,0:T(8,128)S(1)}, u32[]{:S(2)}, u32[]{:S(2)}) collective-permute-start(f32[3,4,8,128]{3,2,1,0:T(8,128)S(1)} %get-tuple-element.33.own_ref), channel_id=1, source_target_pairs={{28,0},{29,1},{30,2},{31,3},{0,4},{1,5},{2,6},{3,7},{4,8},{5,9},{6... | collective-permute-start | bytes 147464 | tf_op jit(solution)/shard_map/ppermute | solution.py:36
  30.9 4.6 %collective-permute-start.8 = (f32[3,4,8,128]{3,2,1,0:T(8,128)S(1)}, f32[3,4,8,128]{3,2,1,0:T(8,128)S(1)}, u32[]{:S(2)}, u32[]{:S(2)}) collective-permute-start(f32[3,4,8,128]{3,2,1,0:T(8,128)S(1)} %get-tuple-element.33.own_ref), channel_id=1, source_target_pairs={{1,0},{0,1},{3,2},{2,3},{5,4},{4,5},{7,6},{6,7},{9,8},{8,9},{11,10... | collective-permute-start | bytes 147464 | tf_op jit(solution)/shard_map/ppermute | solution.py:36
  35.5 8.1 %collective-permute-start.11 = (f32[2,3,16,128]{3,2,1,0:T(8,128)S(1)}, f32[2,3,16,128]{3,2,1,0:T(8,128)S(1)}, u32[]{:S(2)}, u32[]{:S(2)}) collective-permute-start(f32[2,3,16,128]{3,2,1,0:T(8,128)S(1)} %get-tuple-element.35), channel_id=1, source_target_pairs={{2,0},{3,1},{0,2},{1,3},{6,4},{7,5},{4,6},{5,7},{10,8},{11,9},{8,1... | collective-permute-start | bytes 147464 | tf_op jit(solution)/shard_map/ppermute | solution.py:36
  37.1 5.1 %collective-permute-start.7 = (f32[8,8,128]{2,1,0:T(8,128)S(1)}, f32[8,8,128]{2,1,0:T(8,128)S(1)}, u32[]{:S(2)}, u32[]{:S(2)}) collective-permute-start(f32[8,8,128]{2,1,0:T(8,128)S(1)} %get-tuple-element.31), channel_id=1, source_target_pairs={{28,0},{0,4},{4,8},{8,12},{12,16},{16,20},{20,24},{24,28},{29,1},{... | collective-permute-start | bytes 98312 | tf_op jit(solution)/shard_map/ppermute | solution.py:28

commit v5 on v4

--- a/solution.py
+++ b/solution.py
@@ -221,16 +221,17 @@
             ]
     before = lax.rem(tile + tiles - 1, tiles)
     lane = lax.broadcasted_iota(jnp.int32, (list_rows, LANES), 1)
+    spill = None
     for comp in range(comps):
         even = row_steps(ocean_ref, 0, 0, comp, first, list_rows)
         odd = row_steps(ocean_ref, 1, 0, comp, first, list_rows)
-        part_ref[0, comp, :list_rows] = flow_tile(table_ref, tile, even, odd, None)
-        spill = None
+        part_ref[comp * list_rows : (comp + 1) * list_rows] = flow_tile(table_ref, tile, even, odd, None)
         for step in range(3):
-            edge = jnp.where(lane == LANES - 1, pltpu.roll(even[step], LANES - 1, 1), 0.0)
-            term = table_ref[3 * step + 2, before, :list_rows] * edge
-            spill = term if spill is None else spill + term
-        part_ref[1, comp, :list_rows] = spill
+            weight = table_ref[3 * step + 2, before, :list_rows]
+            weight = weight if comp == 0 else pltpu.roll(weight, LANES - comp, 1)
+            edge = jnp.where(lane == LANES - 1 - comp, pltpu.roll(even[step], LANES - 1 - comp, 1), 0.0)
+            spill = weight * edge if spill is None else spill + weight * edge
+    part_ref[comps * list_rows : (comps + 1) * list_rows] = spill
 
 
 def flow_all_kernel(list_rows, first, ocean_ref, table_ref, flow_ref):
@@ -290,7 +291,21 @@
         face_before, here, up = face_here, after, up_after
 
 
-def add_stress(value, trig_ref, scale, rest, sum_ref, slot):
+def add_stress(value, tables, sum_ref, slot):
+    for kind, table in enumerate(tables):
+        sum_ref[kind, slot] += jnp.sum(table * value, axis=0)
+
+
+def stress_tables(trig_ref, energy_ref, number, total_freq, shape):
+    directions = shape[0] * 8
+    ratio = 0.5 + 0.5 * number.astype(jnp.float32) / (total_freq - 1)
+    amplitude = energy_ref[number] / math.sqrt(directions * total_freq)
+    scale, rest = amplitude * ratio, amplitude * (ratio - 0.5)
+    tables = (scale * trig_ref[4] + rest, scale * trig_ref[3] + rest, scale * trig_ref[2])
+    return [jnp.broadcast_to(table[:, None], shape) for table in tables]
+
+
+def add_stress_plain(value, trig_ref, scale, rest, sum_ref, slot):
     shape = value.shape
     cross = jnp.broadcast_to(trig_ref[2][:, None], shape)
     cos2 = jnp.broadcast_to(trig_ref[4][:, None], shape)
@@ -322,9 +337,14 @@
                 flow_ref[comp, tile] = part_refs[0][tile, comp]
         else:
             for bits in range(parts):
-                flow_ref[comp, index ^ bits] = part_refs[bits][0, comp]
+                rows = slice(comp * list_rows, (comp + 1) * list_rows)
+                flow_ref[comp, index ^ bits, :list_rows] = part_refs[bits][rows]
+            lane = lax.broadcasted_iota(jnp.int32, (list_rows, LANES), 1)
             for bits in range(parts):
-                flow_ref[comp, lax.rem((index ^ bits) + tiles - 1, tiles)] += part_refs[bits][1, comp]
+                before = lax.rem((index ^ bits) + tiles - 1, tiles)
+                spill = part_refs[bits][2 * list_rows : 3 * list_rows]
+                spill = spill if comp == 0 else pltpu.roll(spill, comp, 1)
+                flow_ref[comp, before, :list_rows] += jnp.where(lane == LANES - 1, spill, 0.0)
     inner = list_rows - 2
     east, north = flow_ref[0, :, 1 : 1 + inner], flow_ref[1, :, 1 : 1 + inner]
     east_y = (flow_ref[0, :, 2 : 2 + inner] - flow_ref[0, :, 0:inner]) * 0.5
@@ -359,7 +379,7 @@
 
         def finish(row, value):
             out_ref[freq, row - 2] = value
-            add_stress(value, trig_ref, scale, rest, sum_ref, row - 2)
+            add_stress_plain(value, trig_ref, scale, rest, sum_ref, row - 2)
 
         sweep(lambda row: mid_ref[freq, row - 1], speeds, turn_ref, 2, wave_rows - 2, finish)
         return carry
@@ -394,11 +414,11 @@
         def middle(row):
             return rim_ref[rim[row]] if row in rim else mid_ref[freq, row - 1]
 
-        scale, rest = stress_scales(energy_ref, start + freq, total_freq, directions)
+        tables = stress_tables(trig_ref, energy_ref, start + freq, total_freq, (groups, tiles, 8, LANES))
 
         def finish(row, value):
             out_ref[freq, last[row]] = value
-            add_stress(value, trig_ref, scale, rest, sum_ref, last[row])
+            add_stress(value, tables, sum_ref, last[row])
 
         sweep(cells, speeds, turn_ref, -1, 1, keep)
         sweep(cells, speeds, turn_ref, wave_rows - 1, wave_rows + 1, keep)
@@ -420,25 +440,55 @@
     return jnp.where(lane < LANES // 2, after, before)
 
 
+def pack_stress(out_ref, center, edge, count):
+    merged = None
+    for kind in range(3):
+        upper, lower = center(kind)
+        cut = kind * count + upper.shape[0]
+        out_ref[kind * count : cut] = upper
+        out_ref[cut : (kind + 1) * count] = lower
+        parts = edge(kind)
+        if kind == 0:
+            merged = list(parts)
+            continue
+        for k, part in enumerate(parts):
+            lane = lax.broadcasted_iota(jnp.int32, part.shape, 1) - 4 * kind
+            mine = jnp.logical_and(lane >= -2, lane <= 0)
+            merged[k] = jnp.where(mine, pltpu.roll(part, 4 * kind, 1), merged[k])
+    cut = 3 * count + merged[0].shape[0]
+    out_ref[3 * count : cut] = merged[0]
+    out_ref[cut : 4 * count] = merged[1]
+
+
+def packed_rows(count):
+    return -(-4 * count // 8) * 8
+
+
 def pair_kernel(axis, own_ref, x_ref, z_ref, xz_ref, keep_ref, send_ref):
-    kinds, tiles, wave_rows, _ = own_ref.shape
+    tiles, wave_rows = own_ref.shape[1:3]
     half = wave_rows // 2
     index = lax.axis_index(axis)
+
+    def own(kind, tile):
+        return own_ref[kind, tile] + x_ref[kind, tile]
+
+    def prev(kind, tile):
+        return z_ref[kind, tile] + xz_ref[kind, tile]
+
     for target, out_ref in ((index, keep_ref), (index ^ 2, send_ref)):
         after = lax.rem(target + 1, tiles)
         before = lax.rem(target + tiles - 1, tiles)
-        for kind in range(kinds):
-
-            def own(tile):
-                return own_ref[kind, tile] + x_ref[kind, tile]
-
-            def prev(tile):
-                return z_ref[kind, tile] + xz_ref[kind, tile]
-
-            out_ref[0, kind, 0 : half + 2] = prev(target)[wave_rows - half - 2 :]
-            out_ref[0, kind, half + 2 : wave_rows + 3] = own(target)[: half + 1]
-            out_ref[1, kind, 0 : half + 2] = edge_tile(prev(after), prev(before))[wave_rows - half - 2 :]
-            out_ref[1, kind, half + 2 : wave_rows + 3] = edge_tile(own(after), own(before))[: half + 1]
+
+        def center(kind):
+            return prev(kind, target)[wave_rows - half - 2 :], own(kind, target)[: half + 1]
+
+        def edge(kind):
+            return (
+                edge_tile(prev(kind, after), prev(kind, before))[wave_rows - half - 2 :],
+                edge_tile(own(kind, after), own(kind, before))[: half + 1],
+            )
+
+        pack_stress(out_ref, center, edge, wave_rows + 3)
 
 
 def settle_kernel(
@@ -470,15 +520,19 @@
 
 def push_tile(stress_ref, coupling_ref, here, edge, push_ref, count):
     lane = lax.broadcasted_iota(jnp.int32, (count, LANES), 1)
-
-    def middle(part, kind):
-        return stress_ref[part, kind, 1 : 1 + count]
+    span = count + 2
+
+    def rows(part, kind, low):
+        if part == 0:
+            return stress_ref[kind * span + low : kind * span + low + count]
+        value = stress_ref[3 * span + low : 3 * span + low + count]
+        return value if kind == 0 else pltpu.roll(value, LANES - 4 * kind, 1)
 
     def along_y(part, kind):
-        return (stress_ref[part, kind, 2 : 2 + count] - stress_ref[part, kind, 0:count]) * 0.5
+        return (rows(part, kind, 2) - rows(part, kind, 0)) * 0.5
 
     def along_x(part, kind):
-        tile, rim = middle(0, kind), middle(1, kind)
+        tile, rim = rows(0, kind, 1), rows(1, kind, 1)
         after = jnp.where(lane == LANES - 1, pltpu.roll(rim, LANES - 1, 1), pltpu.roll(tile, LANES - 1, 1))
         if part == 0:
             before = jnp.where(lane == 0, pltpu.roll(rim, 1, 1), pltpu.roll(tile, 1, 1))
@@ -541,19 +595,21 @@
 
 
 def push_all_kernel(own_ref, prev_ref, coupling_ref, out_ref, stress_ref, push_ref):
-    kinds, tiles, wave_rows, _ = own_ref.shape
+    tiles, wave_rows = own_ref.shape[1:3]
     half = wave_rows // 2
     for tile in range(tiles):
         after, before = (tile + 1) % tiles, (tile - 1) % tiles
-        for kind in range(kinds):
-            stress_ref[0, kind, 0 : half + 2] = prev_ref[kind, tile][wave_rows - half - 2 :]
-            stress_ref[0, kind, half + 2 : wave_rows + 3] = own_ref[kind, tile][: half + 1]
-            stress_ref[1, kind, 0 : half + 2] = edge_tile(prev_ref[kind, after], prev_ref[kind, before])[
-                wave_rows - half - 2 :
-            ]
-            stress_ref[1, kind, half + 2 : wave_rows + 3] = edge_tile(own_ref[kind, after], own_ref[kind, before])[
-                : half + 1
-            ]
+
+        def center(kind):
+            return prev_ref[kind, tile][wave_rows - half - 2 :], own_ref[kind, tile][: half + 1]
+
+        def edge(kind):
+            return (
+                edge_tile(prev_ref[kind, after], prev_ref[kind, before])[wave_rows - half - 2 :],
+                edge_tile(own_ref[kind, after], own_ref[kind, before])[: half + 1],
+            )
+
+        pack_stress(stress_ref, center, edge, wave_rows + 3)
         pushed = push_tile(stress_ref, coupling_ref, tile, before, push_ref, wave_rows + 1)
         for comp in range(2):
             for parity in range(2):
@@ -621,7 +677,7 @@
     if aligned:
         (part,) = call(
             functools.partial(flow_kernel, "spec", list_rows, first),
-            ((2, 2, padded, LANES),),
+            ((-(-3 * list_rows // 8) * 8, LANES),),
             [VMEM] * 4,
             scratch_shapes=[pltpu.VMEM((2, 1, 2, 2 * ocean_rows, LANES), f32)],
         )(masked, z_current, z_wet, tables)
@@ -677,7 +733,7 @@
         scratch_shapes=[pltpu.VMEM(home, f32), pltpu.SemaphoreType.DMA((freqs, tiles))],
     )(inner, outer, tail, tables)
     new_action = jnp.transpose(out_field, (0, 1, 3, 2, 4)).reshape(action.shape)
-    column = (2, 3, 2 * wave_rows, LANES)
+    column = (packed_rows(wave_rows + 3), LANES)
     scratch = [pltpu.VMEM(column, f32), pltpu.VMEM((9, 2 * wave_rows, LANES), f32)]
     if aligned:
         keep, send = call(functools.partial(pair_kernel, "spec"), (column, column), [VMEM] * 4)(stress, x, z, xz)

time: 44.8 us -> 40.4 us (0.902)
  waiting for transfers between devices: 17.1 us -> 12.4 us
    ppermute x5, waiting for transfers between devices: 10.8 us -> 6.14 us  [from_offset(): lax.ppermute(block, axis, [((i + offset) % count, i) for i in range(count)])]
  transfers between devices with their start and end apart: 12 -> 12, of which waited for: 7 -> 8; matrix products, arithmetic and copies ran while one was open for 0% -> 0% of each run, Pallas kernels for 11% -> 13%
where the time goes in v5:
time: 40.4 us; the launch traced here: 40.2 us
  starting transfers between devices  16.1 us (40%)
  waiting for transfers between devices  12.4 us (31%)
  Pallas kernels  10.9 us (27%)
  between operations  0.74 us (2%)
    ppermute x7, starting transfers between devices, from_mesh(): return lax.ppermute(block, ('space', 'spec'), route)  9.12 us
    ppermute x5, starting transfers between devices, from_offset(): lax.ppermute(block, axis, [((i + offset) % count, i) for i in range(count)])  6.99 us
    ppermute x7, waiting for transfers between devices, from_mesh(): return lax.ppermute(block, ('space', 'spec'), route)  6.25 us
    ppermute x5, waiting for transfers between devices, from_offset(): lax.ppermute(block, axis, [((i + offset) % count, i) for i in range(count)])  6.14 us
    pallas_call x1, Pallas kernels, window(): call(functools.partial(inner_kernel, freqs * spec, 'spec', list_rows, len...  3.38 us
    pallas_call x1, Pallas kernels, window(): call(functools.partial(outer_kernel, freqs * spec, 'spec'), ((freqs, 4) +...  2.84 us
    pallas_call x1, Pallas kernels, window(): call(functools.partial(open_kernel, ocean_cols, tail_rows, 'spec', aligne...  1.87 us
    pallas_call x1, Pallas kernels, window(): call(functools.partial(settle_kernel, 'spec', aligned, tail_rows), (field...  1.36 us
  transfers between devices with their start and end apart: 12, of which 8 were waited for; matrix products, arithmetic and copies ran while one was open for 0% of the time, Pallas kernels for 13%

profile of v5, /device:TPU:0, one launch (start us, length us, event | category | flops | bytes accessed | tf_op | source)
XLA Modules:
  0.0 40.2 jit_solution(8555955625131331091)
XLA Ops:
  0.6 0.0 copy-start
  0.6 0.0 copy-start.4
  0.7 0.0 copy-start.3
  0.7 0.0 copy-start.2
  0.7 0.0 copy-start.1
  0.7 1.9 %shard_map.95 = (f32[2,16,256]{2,1,0:T(8,128)S(1)}, f32[16,256]{1,0:T(8,128)S(1)}, f32[9,4,16,128]{3,2,1,0:T(8,128)S(1)}, f32[8,8,128]{2,1,0:T(8,128)S(1)}, f32[...) custom-call(f32[2,16,256]{2,1,0:T(8,128)} %current_hbm.1, ...), custom_call_target="tpu_custom_call" | custom-call | tf_op jit(solution)/shard_map/pallas_call | solution.py:652
  2.6 0.5 %collective-permute-start.5 = (f32[24,4,8,128]{3,2,1,0:T(8,128)S(1)}, f32[24,4,8,128]{3,2,1,0:T(8,128)S(1)}, u32[]{:S(2)}, u32[]{:S(2)}) collective-permute-start(f32[24,4,8,128]{3,2,1,0:T(8,128)S(1)} %get-tuple-element.24), channel_id=1, source_target_pairs={{28,0},{0,4},{4,8},{8,12},{12,16},{16,20},{20,24},{24,28},{29,1},{... | collective-permute-start | bytes 1179656 | tf_op jit(solution)/shard_map/ppermute | solution.py:28
  3.1 4.1 %collective-permute-start.6 = (f32[24,4,8,128]{3,2,1,0:T(8,128)S(1)}, f32[24,4,8,128]{3,2,1,0:T(8,128)S(1)}, u32[]{:S(2)}, u32[]{:S(2)}) collective-permute-start(f32[24,4,8,128]{3,2,1,0:T(8,128)S(1)} %get-tuple-element.25), channel_id=1, source_target_pairs={{4,0},{8,4},{12,8},{16,12},{20,16},{24,20},{28,24},{0,28},{5,1},{9... | collective-permute-start | bytes 1179656 | tf_op jit(solution)/shard_map/ppermute | solution.py:28
  7.2 0.0 copy-done.3
  7.2 0.7 %collective-permute-start = (f32[2,16,256]{2,1,0:T(8,128)S(1)}, f32[2,16,256]{2,1,0:T(8,128)S(1)}, u32[]{:S(2)}, u32[]{:S(2)}) collective-permute-start(f32[2,16,256]{2,1,0:T(8,128)S(1)} %copy-done.3), channel_id=1, source_target_pairs={{4,0},{8,4},{12,8},{16,12},{20,16},{24,20},{28,24},{0,28},{5,1},{9... | collective-permute-start | bytes 98312 | tf_op jit(solution)/shard_map/ppermute | solution.py:28
  7.9 0.0 copy-done.4
  7.9 1.7 %collective-permute-start.1 = (s32[16,256]{1,0:T(8,128)S(1)}, s32[16,256]{1,0:T(8,128)S(1)}, u32[]{:S(2)}, u32[]{:S(2)}) collective-permute-start(s32[16,256]{1,0:T(8,128)S(1)} %copy-done.4), channel_id=1, source_target_pairs={{4,0},{8,4},{12,8},{16,12},{20,16},{24,20},{28,24},{0,28},{5,1},{9... | collective-permute-start | bytes 49160 | tf_op jit(solution)/shard_map/ppermute | solution.py:28
  9.6 5.6 %collective-permute-done.1.wet_ref = s32[16,256]{1,0:T(8,128)S(1)} collective-permute-done((s32[16,256]{1,0:T(8,128)S(1)}, s32[16,256]{1,0:T(8,128)S(1)}, u32[]{:S(2)}, u32[]{:S(2)}) %collective-permute-start.1) | collective-permute-done | bytes 16416 | tf_op jit(solution)/shard_map/ppermute | solution.py:28
  15.2 0.0 collective-permute-done.current_ref
  15.2 0.3 shard_map.96.refs_0_
  15.5 2.5 %collective-permute-start.4 = (f32[40,128]{1,0:T(8,128)S(1)}, f32[40,128]{1,0:T(8,128)S(1)}, u32[]{:S(2)}, u32[]{:S(2)}) collective-permute-start(f32[40,128]{1,0:T(8,128)S(1)} %shard_map.96.refs_0_), channel_id=1, source_target_pairs={{3,0},{2,1},{1,2},{0,3},{7,4},{6,5},{5,6},{4,7},{11,8},{10,9},{9,1... | collective-permute-start | bytes 61448 | tf_op jit(solution)/shard_map/ppermute | solution.py:36
  18.0 0.5 %collective-permute-start.3 = (f32[40,128]{1,0:T(8,128)S(1)}, f32[40,128]{1,0:T(8,128)S(1)}, u32[]{:S(2)}, u32[]{:S(2)}) collective-permute-start(f32[40,128]{1,0:T(8,128)S(1)} %shard_map.96.refs_0_), channel_id=1, source_target_pairs={{2,0},{3,1},{0,2},{1,3},{6,4},{7,5},{4,6},{5,7},{10,8},{11,9},{8,1... | collective-permute-start | bytes 61448 | tf_op jit(solution)/shard_map/ppermute | solution.py:36
  18.6 0.5 %collective-permute-start.2 = (f32[40,128]{1,0:T(8,128)S(1)}, f32[40,128]{1,0:T(8,128)S(1)}, u32[]{:S(2)}, u32[]{:S(2)}) collective-permute-start(f32[40,128]{1,0:T(8,128)S(1)} %shard_map.96.refs_0_), channel_id=1, source_target_pairs={{1,0},{0,1},{3,2},{2,3},{5,4},{4,5},{7,6},{6,7},{9,8},{8,9},{11,10... | collective-permute-start | bytes 61448 | tf_op jit(solution)/shard_map/ppermute | solution.py:36
  19.1 1.2 %collective-permute-done.4.refs_3_ = f32[40,128]{1,0:T(8,128)S(1)} collective-permute-done((f32[40,128]{1,0:T(8,128)S(1)}, f32[40,128]{1,0:T(8,128)S(1)}, u32[]{:S(2)}, u32[]{:S(2)}) %collective-permute-start.4) | collective-permute-done | bytes 20512 | tf_op jit(solution)/shard_map/ppermute | solution.py:36
  20.3 1.5 %collective-permute-done.3.refs_2_ = f32[40,128]{1,0:T(8,128)S(1)} collective-permute-done((f32[40,128]{1,0:T(8,128)S(1)}, f32[40,128]{1,0:T(8,128)S(1)}, u32[]{:S(2)}, u32[]{:S(2)}) %collective-permute-start.3) | collective-permute-done | bytes 20512 | tf_op jit(solution)/shard_map/ppermute | solution.py:36
  21.8 0.5 %collective-permute-done.2.refs_1_ = f32[40,128]{1,0:T(8,128)S(1)} collective-permute-done((f32[40,128]{1,0:T(8,128)S(1)}, f32[40,128]{1,0:T(8,128)S(1)}, u32[]{:S(2)}, u32[]{:S(2)}) %collective-permute-start.2) | collective-permute-done | bytes 20512 | tf_op jit(solution)/shard_map/ppermute | solution.py:36
  22.3 0.0 copy-done
  22.3 0.0 copy-done.2
  22.3 0.0 copy-done.1
  22.4 3.4 %shard_map.97 = (f32[2,4,16,128]{3,2,1,0:T(8,128)S(1)}, f32[2,10,3,4,8,128]{5,4,3,2,1,0:T(8,128)S(1)}, f32[4,6,3,4,8,128]{5,4,3,2,1,0:T(8,128)S(1)}, f32[4,4,3,4...) custom-call(f32[40,128]{1,0:T(8,128)S(1)} %shard_map.96.refs_0_, f32[40,128]{1,0:T(8,128)S(1)} %collective-permute-done.2.refs_1_, ...), custom_call_target="tpu_custom_call" | custom-call | tf_op jit(solution)/shard_map/pallas_call | solution.py:699
  25.7 0.0 collective-permute-done.5.low_ref
  25.7 0.0 collective-permute-done.6.high_ref
  25.8 2.8 %shard_map.98 = (f32[4,4,3,4,8,128]{5,4,3,2,1,0:T(8,128)S(1)}, f32[3,4,8,128]{3,2,1,0:T(8,128)S(1)}) custom-call(f32[5,3,8,128]{3,2,1,0:T(8,128)S(1)} %copy-done, f32[16]{0:T(128)S(1)} %copy-done.1, f32[16]{0:T(128)S(1)} %copy-done.2, f32[4,4,24,8,128]{4,3,2,1,0:T(8,128)S(1)} %get-tuple-element.22.refs_7_.field_ref, ...), custom_call_target="tpu_custom_call" | custom-call | tf_op jit(solution)/shard_map/pallas_call | solution.py:714
  28.6 0.8 %collective-permute-start.10 = (f32[3,4,8,128]{3,2,1,0:T(8,128)S(1)}, f32[3,4,8,128]{3,2,1,0:T(8,128)S(1)}, u32[]{:S(2)}, u32[]{:S(2)}) collective-permute-start(f32[3,4,8,128]{3,2,1,0:T(8,128)S(1)} %get-tuple-element.33.own_ref), channel_id=1, source_target_pairs={{29,0},{28,1},{31,2},{30,3},{1,4},{0,5},{3,6},{2,7},{5,8},{4,9},{7... | collective-permute-start | bytes 147464 | tf_op jit(solution)/shard_map/ppermute | solution.py:36
  29.4 1.1 %collective-permute-start.9 = (f32[3,4,8,128]{3,2,1,0:T(8,128)S(1)}, f32[3,4,8,128]{3,2,1,0:T(8,128)S(1)}, u32[]{:S(2)}, u32[]{:S(2)}) collective-permute-start(f32[3,4,8,128]{3,2,1,0:T(8,128)S(1)} %get-tuple-element.33.own_ref), channel_id=1, source_target_pairs={{28,0},{29,1},{30,2},{31,3},{0,4},{1,5},{2,6},{3,7},{4,8},{5,9},{6... | collective-permute-start | bytes 147464 | tf_op jit(solution)/shard_map/ppermute | solution.py:36
  30.5 1.9 %collective-permute-start.8 = (f32[3,4,8,128]{3,2,1,0:T(8,128)S(1)}, f32[3,4,8,128]{3,2,1,0:T(8,128)S(1)}, u32[]{:S(2)}, u32[]{:S(2)}) collective-permute-start(f32[3,4,8,128]{3,2,1,0:T(8,128)S(1)} %get-tuple-element.33.own_ref), channel_id=1, source_target_pairs={{1,0},{0,1},{3,2},{2,3},{5,4},{4,5},{7,6},{6,7},{9,8},{8,9},{11,10... | collective-permute-start | bytes 147464 | tf_op jit(solution)/shard_map/ppermute | solution.py:36
  32.4 0.0 collective-permute-start.7
  32.4 2.5 %collective-permute-done.10.xz_ref = f32[3,4,8,128]{3,2,1,0:T(8,128)S(1)} collective-permute-done((f32[3,4,8,128]{3,2,1,0:T(8,128)S(1)}, f32[3,4,8,128]{3,2,1,0:T(8,128)S(1)}, u32[]{:S(2)}, u32[]{:S(2)}) %collective-permute-start.10) | collective-permute-done | bytes 49184 | tf_op jit(solution)/shard_map/ppermute | solution.py:36
  35.0 0.0 collective-permute-done.9.z_ref
  35.0 0.2 collective-permute-done.8.x_ref
  35.2 0.1 shard_map.100
  35.3 1.7 %collective-permute-start.11 = (f32[48,128]{1,0:T(8,128)S(1)}, f32[48,128]{1,0:T(8,128)S(1)}, u32[]{:S(2)}, u32[]{:S(2)}) collective-permute-start(f32[48,128]{1,0:T(8,128)S(1)} %get-tuple-element.35), channel_id=1, source_target_pairs={{2,0},{3,1},{0,2},{1,3},{6,4},{7,5},{4,6},{5,7},{10,8},{11,9},{8,1... | collective-permute-start | bytes 73736 | tf_op jit(solution)/shard_map/ppermute | solution.py:36
  37.1 0.5 %collective-permute-done.7.tail_ref = f32[8,8,128]{2,1,0:T(8,128)S(1)} collective-permute-done((f32[8,8,128]{2,1,0:T(8,128)S(1)}, f32[8,8,128]{2,1,0:T(8,128)S(1)}, u32[]{:S(2)}, u32[]{:S(2)}) %collective-permute-start.7) | collective-permute-done | bytes 32800 | tf_op jit(solution)/shard_map/ppermute | solution.py:28
  37.6 1.4 %shard_map.99 = (f32[4,24,4,8,128]{4,3,2,1,0:T(8,128)}, f32[2,9,16,128]{3,2,1,0:T(8,128)S(1)}) custom-call(f32[4,4,3,4,8,128]{5,4,3,2,1,0:T(8,128)S(1)} %get-tuple-element.23.inner_ref, f32[4,4,3,4,8,128]{5,4,3,2,1,0:T(8,128)S(1)} %get-tuple-element.30.outer_ref, f32[8,8,128]{2,1,0:T(8,128)S(1)} %collective-permute-done.7.tail_ref, ...), custom_call_target="tpu_custom_call" | custom-call | tf_op jit(solution)/shard_map/pallas_call | solution.py:728
  38.9 0.2 collective-permute-done.11.come_ref
  39.2 1.0 %shard_map.101 = f32[2,16,256]{2,1,0:T(8,128)} custom-call(f32[48,128]{1,0:T(8,128)S(1)} %get-tuple-element.34.keep_ref, f32[48,128]{1,0:T(8,128)S(1)} %collective-permute-done.11.come_ref, f32[2,9,16,128]{3,2,1,0:T(8,128)S(1)} %get-tuple-element.36.coupling_ref, f32[2,16,256]{2,1,0:T(8,128)S(1)} %get-tuple-element.20.own_ref.masked_ref, ...), custom_call_target="tpu_custom_call" | custom-call | tf_op jit(solution)/shard_map/pallas_call | solution.py:741
Async XLA Ops:
  0.6 21.7 %copy-start = (f32[5,3,8,128]{3,2,1,0:T(8,128)S(1)}, f32[5,3,8,128]{3,2,1,0:T(8,128)}, u32[]{:S(2)}) copy-start(f32[5,3,8,128]{3,2,1,0:T(8,128)} %constant.2.clone.refs_4_.trig_ref) | copy-start | bytes 184324
  0.6 7.2 %copy-start.4 = (s32[16,256]{1,0:T(8,128)S(1)}, s32[16,256]{1,0:T(8,128)}, u32[]{:S(2)}) copy-start(s32[16,256]{1,0:T(8,128)} %wet_hbm.1) | copy-start | bytes 49156
  0.7 6.5 %copy-start.3 = (f32[2,16,256]{2,1,0:T(8,128)S(1)}, f32[2,16,256]{2,1,0:T(8,128)}, u32[]{:S(2)}) copy-start(f32[2,16,256]{2,1,0:T(8,128)} %current_hbm.1) | copy-start | bytes 98308
  0.7 21.7 %copy-start.2 = (f32[16]{0:T(128)S(1)}, f32[16]{0:T(128)}, u32[]{:S(2)}) copy-start(f32[16]{0:T(128)} %energy_ref.1) | copy-start | bytes 196
  0.7 21.7 %copy-start.1 = (f32[16]{0:T(128)S(1)}, f32[16]{0:T(128)}, u32[]{:S(2)}) copy-start(f32[16]{0:T(128)} %speed_ref.1) | copy-start | bytes 196
  2.6 23.2 %collective-permute-start.5 = (f32[24,4,8,128]{3,2,1,0:T(8,128)S(1)}, f32[24,4,8,128]{3,2,1,0:T(8,128)S(1)}, u32[]{:S(2)}, u32[]{:S(2)}) collective-permute-start(f32[24,4,8,128]{3,2,1,0:T(8,128)S(1)} %get-tuple-element.24), channel_id=1, source_target_pairs={{28,0},{0,4},{4,8},{8,12},{12,16},{16,20},{20,24},{24,28},{29,1},{... | collective-permute-start | bytes 1179656 | tf_op jit(solution)/shard_map/ppermute | solution.py:28
  3.1 22.6 %collective-permute-start.6 = (f32[24,4,8,128]{3,2,1,0:T(8,128)S(1)}, f32[24,4,8,128]{3,2,1,0:T(8,128)S(1)}, u32[]{:S(2)}, u32[]{:S(2)}) collective-permute-start(f32[24,4,8,128]{3,2,1,0:T(8,128)S(1)} %get-tuple-element.25), channel_id=1, source_target_pairs={{4,0},{8,4},{12,8},{16,12},{20,16},{24,20},{28,24},{0,28},{5,1},{9... | collective-permute-start | bytes 1179656 | tf_op jit(solution)/shard_map/ppermute | solution.py:28
  7.2 8.0 %collective-permute-start = (f32[2,16,256]{2,1,0:T(8,128)S(1)}, f32[2,16,256]{2,1,0:T(8,128)S(1)}, u32[]{:S(2)}, u32[]{:S(2)}) collective-permute-start(f32[2,16,256]{2,1,0:T(8,128)S(1)} %copy-done.3), channel_id=1, source_target_pairs={{4,0},{8,4},{12,8},{16,12},{20,16},{24,20},{28,24},{0,28},{5,1},{9... | collective-permute-start | bytes 98312 | tf_op jit(solution)/shard_map/ppermute | solution.py:28
  7.9 7.3 %collective-permute-start.1 = (s32[16,256]{1,0:T(8,128)S(1)}, s32[16,256]{1,0:T(8,128)S(1)}, u32[]{:S(2)}, u32[]{:S(2)}) collective-permute-start(s32[16,256]{1,0:T(8,128)S(1)} %copy-done.4), channel_id=1, source_target_pairs={{4,0},{8,4},{12,8},{16,12},{20,16},{24,20},{28,24},{0,28},{5,1},{9... | collective-permute-start | bytes 49160 | tf_op jit(solution)/shard_map/ppermute | solution.py:28
  15.5 4.7 %collective-permute-start.4 = (f32[40,128]{1,0:T(8,128)S(1)}, f32[40,128]{1,0:T(8,128)S(1)}, u32[]{:S(2)}, u32[]{:S(2)}) collective-permute-start(f32[40,128]{1,0:T(8,128)S(1)} %shard_map.96.refs_0_), channel_id=1, source_target_pairs={{3,0},{2,1},{1,2},{0,3},{7,4},{6,5},{5,6},{4,7},{11,8},{10,9},{9,1... | collective-permute-start | bytes 61448 | tf_op jit(solution)/shard_map/ppermute | solution.py:36
  18.0 3.8 %collective-permute-start.3 = (f32[40,128]{1,0:T(8,128)S(1)}, f32[40,128]{1,0:T(8,128)S(1)}, u32[]{:S(2)}, u32[]{:S(2)}) collective-permute-start(f32[40,128]{1,0:T(8,128)S(1)} %shard_map.96.refs_0_), channel_id=1, source_target_pairs={{2,0},{3,1},{0,2},{1,3},{6,4},{7,5},{4,6},{5,7},{10,8},{11,9},{8,1... | collective-permute-start | bytes 61448 | tf_op jit(solution)/shard_map/ppermute | solution.py:36
  18.6 3.8 %collective-permute-start.2 = (f32[40,128]{1,0:T(8,128)S(1)}, f32[40,128]{1,0:T(8,128)S(1)}, u32[]{:S(2)}, u32[]{:S(2)}) collective-permute-start(f32[40,128]{1,0:T(8,128)S(1)} %shard_map.96.refs_0_), channel_id=1, source_target_pairs={{1,0},{0,1},{3,2},{2,3},{5,4},{4,5},{7,6},{6,7},{9,8},{8,9},{11,10... | collective-permute-start | bytes 61448 | tf_op jit(solution)/shard_map/ppermute | solution.py:36
  28.6 6.4 %collective-permute-start.10 = (f32[3,4,8,128]{3,2,1,0:T(8,128)S(1)}, f32[3,4,8,128]{3,2,1,0:T(8,128)S(1)}, u32[]{:S(2)}, u32[]{:S(2)}) collective-permute-start(f32[3,4,8,128]{3,2,1,0:T(8,128)S(1)} %get-tuple-element.33.own_ref), channel_id=1, source_target_pairs={{29,0},{28,1},{31,2},{30,3},{1,4},{0,5},{3,6},{2,7},{5,8},{4,9},{7... | collective-permute-start | bytes 147464 | tf_op jit(solution)/shard_map/ppermute | solution.py:36
  29.4 5.5 %collective-permute-start.9 = (f32[3,4,8,128]{3,2,1,0:T(8,128)S(1)}, f32[3,4,8,128]{3,2,1,0:T(8,128)S(1)}, u32[]{:S(2)}, u32[]{:S(2)}) collective-permute-start(f32[3,4,8,128]{3,2,1,0:T(8,128)S(1)} %get-tuple-element.33.own_ref), channel_id=1, source_target_pairs={{28,0},{29,1},{30,2},{31,3},{0,4},{1,5},{2,6},{3,7},{4,8},{5,9},{6... | collective-permute-start | bytes 147464 | tf_op jit(solution)/shard_map/ppermute | solution.py:36
  30.5 4.7 %collective-permute-start.8 = (f32[3,4,8,128]{3,2,1,0:T(8,128)S(1)}, f32[3,4,8,128]{3,2,1,0:T(8,128)S(1)}, u32[]{:S(2)}, u32[]{:S(2)}) collective-permute-start(f32[3,4,8,128]{3,2,1,0:T(8,128)S(1)} %get-tuple-element.33.own_ref), channel_id=1, source_target_pairs={{1,0},{0,1},{3,2},{2,3},{5,4},{4,5},{7,6},{6,7},{9,8},{8,9},{11,10... | collective-permute-start | bytes 147464 | tf_op jit(solution)/shard_map/ppermute | solution.py:36
  32.4 5.1 %collective-permute-start.7 = (f32[8,8,128]{2,1,0:T(8,128)S(1)}, f32[8,8,128]{2,1,0:T(8,128)S(1)}, u32[]{:S(2)}, u32[]{:S(2)}) collective-permute-start(f32[8,8,128]{2,1,0:T(8,128)S(1)} %get-tuple-element.31), channel_id=1, source_target_pairs={{28,0},{0,4},{4,8},{8,12},{12,16},{16,20},{20,24},{24,28},{29,1},{... | collective-permute-start | bytes 98312 | tf_op jit(solution)/shard_map/ppermute | solution.py:28
  35.3 3.9 %collective-permute-start.11 = (f32[48,128]{1,0:T(8,128)S(1)}, f32[48,128]{1,0:T(8,128)S(1)}, u32[]{:S(2)}, u32[]{:S(2)}) collective-permute-start(f32[48,128]{1,0:T(8,128)S(1)} %get-tuple-element.35), channel_id=1, source_target_pairs={{2,0},{3,1},{0,2},{1,3},{6,4},{7,5},{4,6},{5,7},{10,8},{11,9},{8,1... | collective-permute-start | bytes 73736 | tf_op jit(solution)/shard_map/ppermute | solution.py:36

commit v6 on v5

--- a/solution.py
+++ b/solution.py
@@ -16,7 +16,6 @@
 force_gain = 0.5
 
 LANES = 128
-HIGHEST = lax.Precision.HIGHEST
 VMEM = pl.BlockSpec(memory_space=pltpu.VMEM)
 SMEM = pl.BlockSpec(memory_space=pltpu.SMEM)
 HBM = pl.BlockSpec(memory_space=pltpu.MemorySpace.HBM)
@@ -45,7 +44,7 @@
     col = lax.broadcasted_iota(jnp.int32, (width, width), 1)
     half = width // 2
     source = jnp.where(col < half, 2 * col, 2 * (col - half) + 1)
-    return (row == source).astype(jnp.float32)
+    return (row == source).astype(jnp.float32).astype(jnp.bfloat16)
 
 
 def merge_matrix(width):
@@ -53,7 +52,19 @@
     col = lax.broadcasted_iota(jnp.int32, (width, width), 1)
     half = width // 2
     target = jnp.where(row < half, 2 * row, 2 * (row - half) + 1)
-    return (col == target).astype(jnp.float32)
+    return (col == target).astype(jnp.float32).astype(jnp.bfloat16)
+
+
+def pick_columns(cells, matrix):
+    rows = cells.shape[0]
+    first = cells.astype(jnp.bfloat16)
+    rest = cells - first.astype(jnp.float32)
+    second = rest.astype(jnp.bfloat16)
+    third = (rest - second.astype(jnp.float32)).astype(jnp.bfloat16)
+    parts = jnp.dot(
+        jnp.concatenate([first, second, third], axis=0), matrix, preferred_element_type=jnp.float32
+    )
+    return parts[:rows] + parts[rows : 2 * rows] + parts[2 * rows :]
 
 
 def roll_lanes(x, shift):
@@ -212,7 +223,7 @@
     tile = lax.axis_index(axis)
     after = current_ref[...] * wet_ref[...].astype(jnp.float32)[None]
     cells = jnp.concatenate([x.reshape(comps * rows, width) for x in (own_ref[...], after)], axis=0)
-    split = jnp.dot(cells, split_matrix(width), precision=HIGHEST, preferred_element_type=jnp.float32)
+    split = pick_columns(cells, split_matrix(width))
     split = split.reshape(2, comps, rows, width)
     for parity in range(2):
         for block in range(2):
@@ -579,9 +590,7 @@
         ],
         axis=0,
     )
-    merged = jnp.dot(
-        cells, merge_matrix(width), precision=HIGHEST, preferred_element_type=jnp.float32
-    ).reshape(2, 2, wave_rows, width)
+    merged = pick_columns(cells, merge_matrix(width)).reshape(2, 2, wave_rows, width)
     wet = wet_ref[...]
     for comp in range(2):
         for tile in range(width // LANES):

time: 40.4 us -> 40.3 us (level)
  no operation moved by 1% of the time
where the time goes in v6:
time: 40.3 us; the launch traced here: 40.1 us
  starting transfers between devices  16.1 us (40%)
  waiting for transfers between devices  12.4 us (31%)
  Pallas kernels  10.8 us (27%)
  between operations  0.74 us (2%)
    ppermute x7, starting transfers between devices, from_mesh(): return lax.ppermute(block, ('space', 'spec'), route)  9.12 us
    ppermute x5, starting transfers between devices, from_offset(): lax.ppermute(block, axis, [((i + offset) % count, i) for i in range(count)])  6.99 us
    ppermute x7, waiting for transfers between devices, from_mesh(): return lax.ppermute(block, ('space', 'spec'), route)  6.25 us
    ppermute x5, waiting for transfers between devices, from_offset(): lax.ppermute(block, axis, [((i + offset) % count, i) for i in range(count)])  6.14 us
    pallas_call x1, Pallas kernels, window(): call(functools.partial(inner_kernel, freqs * spec, 'spec', list_rows, len...  3.38 us
    pallas_call x1, Pallas kernels, window(): call(functools.partial(outer_kernel, freqs * spec, 'spec'), ((freqs, 4) +...  2.84 us
    pallas_call x1, Pallas kernels, window(): call(functools.partial(open_kernel, ocean_cols, tail_rows, 'spec', aligne...  1.87 us
    pallas_call x1, Pallas kernels, window(): call(functools.partial(settle_kernel, 'spec', aligned, tail_rows), (field...  1.36 us
  transfers between devices with their start and end apart: 12, of which 8 were waited for; matrix products, arithmetic and copies ran while one was open for 0% of the time, Pallas kernels for 13%

profile of v6, /device:TPU:0, one launch (start us, length us, event | category | flops | bytes accessed | tf_op | source)
XLA Modules:
  0.0 40.1 jit_solution(441990779653438517)
XLA Ops:
  0.6 0.0 copy-start
  0.6 0.0 copy-start.4
  0.7 0.0 copy-start.3
  0.7 0.0 copy-start.2
  0.7 0.0 copy-start.1
  0.7 1.9 %shard_map.95 = (f32[2,16,256]{2,1,0:T(8,128)S(1)}, f32[16,256]{1,0:T(8,128)S(1)}, f32[9,4,16,128]{3,2,1,0:T(8,128)S(1)}, f32[8,8,128]{2,1,0:T(8,128)S(1)}, f32[...) custom-call(f32[2,16,256]{2,1,0:T(8,128)} %current_hbm.1, ...), custom_call_target="tpu_custom_call" | custom-call | tf_op jit(solution)/shard_map/pallas_call | solution.py:661
  2.6 0.5 %collective-permute-start.5 = (f32[24,4,8,128]{3,2,1,0:T(8,128)S(1)}, f32[24,4,8,128]{3,2,1,0:T(8,128)S(1)}, u32[]{:S(2)}, u32[]{:S(2)}) collective-permute-start(f32[24,4,8,128]{3,2,1,0:T(8,128)S(1)} %get-tuple-element.24), channel_id=1, source_target_pairs={{28,0},{0,4},{4,8},{8,12},{12,16},{16,20},{20,24},{24,28},{29,1},{... | collective-permute-start | bytes 1179656 | tf_op jit(solution)/shard_map/ppermute | solution.py:27
  3.1 4.1 %collective-permute-start.6 = (f32[24,4,8,128]{3,2,1,0:T(8,128)S(1)}, f32[24,4,8,128]{3,2,1,0:T(8,128)S(1)}, u32[]{:S(2)}, u32[]{:S(2)}) collective-permute-start(f32[24,4,8,128]{3,2,1,0:T(8,128)S(1)} %get-tuple-element.25), channel_id=1, source_target_pairs={{4,0},{8,4},{12,8},{16,12},{20,16},{24,20},{28,24},{0,28},{5,1},{9... | collective-permute-start | bytes 1179656 | tf_op jit(solution)/shard_map/ppermute | solution.py:27
  7.2 0.0 copy-done.3
  7.2 0.7 %collective-permute-start = (f32[2,16,256]{2,1,0:T(8,128)S(1)}, f32[2,16,256]{2,1,0:T(8,128)S(1)}, u32[]{:S(2)}, u32[]{:S(2)}) collective-permute-start(f32[2,16,256]{2,1,0:T(8,128)S(1)} %copy-done.3), channel_id=1, source_target_pairs={{4,0},{8,4},{12,8},{16,12},{20,16},{24,20},{28,24},{0,28},{5,1},{9... | collective-permute-start | bytes 98312 | tf_op jit(solution)/shard_map/ppermute | solution.py:27
  7.9 0.0 copy-done.4
  7.9 1.7 %collective-permute-start.1 = (s32[16,256]{1,0:T(8,128)S(1)}, s32[16,256]{1,0:T(8,128)S(1)}, u32[]{:S(2)}, u32[]{:S(2)}) collective-permute-start(s32[16,256]{1,0:T(8,128)S(1)} %copy-done.4), channel_id=1, source_target_pairs={{4,0},{8,4},{12,8},{16,12},{20,16},{24,20},{28,24},{0,28},{5,1},{9... | collective-permute-start | bytes 49160 | tf_op jit(solution)/shard_map/ppermute | solution.py:27
  9.6 5.6 %collective-permute-done.1.wet_ref = s32[16,256]{1,0:T(8,128)S(1)} collective-permute-done((s32[16,256]{1,0:T(8,128)S(1)}, s32[16,256]{1,0:T(8,128)S(1)}, u32[]{:S(2)}, u32[]{:S(2)}) %collective-permute-start.1) | collective-permute-done | bytes 16416 | tf_op jit(solution)/shard_map/ppermute | solution.py:27
  15.2 0.0 collective-permute-done.current_ref
  15.2 0.3 shard_map.96.refs_0_
  15.5 2.5 %collective-permute-start.4 = (f32[40,128]{1,0:T(8,128)S(1)}, f32[40,128]{1,0:T(8,128)S(1)}, u32[]{:S(2)}, u32[]{:S(2)}) collective-permute-start(f32[40,128]{1,0:T(8,128)S(1)} %shard_map.96.refs_0_), channel_id=1, source_target_pairs={{3,0},{2,1},{1,2},{0,3},{7,4},{6,5},{5,6},{4,7},{11,8},{10,9},{9,1... | collective-permute-start | bytes 61448 | tf_op jit(solution)/shard_map/ppermute | solution.py:35
  18.0 0.5 %collective-permute-start.3 = (f32[40,128]{1,0:T(8,128)S(1)}, f32[40,128]{1,0:T(8,128)S(1)}, u32[]{:S(2)}, u32[]{:S(2)}) collective-permute-start(f32[40,128]{1,0:T(8,128)S(1)} %shard_map.96.refs_0_), channel_id=1, source_target_pairs={{2,0},{3,1},{0,2},{1,3},{6,4},{7,5},{4,6},{5,7},{10,8},{11,9},{8,1... | collective-permute-start | bytes 61448 | tf_op jit(solution)/shard_map/ppermute | solution.py:35
  18.5 0.5 %collective-permute-start.2 = (f32[40,128]{1,0:T(8,128)S(1)}, f32[40,128]{1,0:T(8,128)S(1)}, u32[]{:S(2)}, u32[]{:S(2)}) collective-permute-start(f32[40,128]{1,0:T(8,128)S(1)} %shard_map.96.refs_0_), channel_id=1, source_target_pairs={{1,0},{0,1},{3,2},{2,3},{5,4},{4,5},{7,6},{6,7},{9,8},{8,9},{11,10... | collective-permute-start | bytes 61448 | tf_op jit(solution)/shard_map/ppermute | solution.py:35
  19.0 1.2 %collective-permute-done.4.refs_3_ = f32[40,128]{1,0:T(8,128)S(1)} collective-permute-done((f32[40,128]{1,0:T(8,128)S(1)}, f32[40,128]{1,0:T(8,128)S(1)}, u32[]{:S(2)}, u32[]{:S(2)}) %collective-permute-start.4) | collective-permute-done | bytes 20512 | tf_op jit(solution)/shard_map/ppermute | solution.py:35
  20.2 1.6 %collective-permute-done.3.refs_2_ = f32[40,128]{1,0:T(8,128)S(1)} collective-permute-done((f32[40,128]{1,0:T(8,128)S(1)}, f32[40,128]{1,0:T(8,128)S(1)}, u32[]{:S(2)}, u32[]{:S(2)}) %collective-permute-start.3) | collective-permute-done | bytes 20512 | tf_op jit(solution)/shard_map/ppermute | solution.py:35
  21.8 0.5 %collective-permute-done.2.refs_1_ = f32[40,128]{1,0:T(8,128)S(1)} collective-permute-done((f32[40,128]{1,0:T(8,128)S(1)}, f32[40,128]{1,0:T(8,128)S(1)}, u32[]{:S(2)}, u32[]{:S(2)}) %collective-permute-start.2) | collective-permute-done | bytes 20512 | tf_op jit(solution)/shard_map/ppermute | solution.py:35
  22.3 0.0 copy-done
  22.3 0.0 copy-done.2
  22.3 0.0 copy-done.1
  22.3 3.4 %shard_map.97 = (f32[2,4,16,128]{3,2,1,0:T(8,128)S(1)}, f32[2,10,3,4,8,128]{5,4,3,2,1,0:T(8,128)S(1)}, f32[4,6,3,4,8,128]{5,4,3,2,1,0:T(8,128)S(1)}, f32[4,4,3,4...) custom-call(f32[40,128]{1,0:T(8,128)S(1)} %shard_map.96.refs_0_, f32[40,128]{1,0:T(8,128)S(1)} %collective-permute-done.2.refs_1_, ...), custom_call_target="tpu_custom_call" | custom-call | tf_op jit(solution)/shard_map/pallas_call | solution.py:708
  25.7 0.0 collective-permute-done.5.low_ref
  25.7 0.0 collective-permute-done.6.high_ref
  25.7 2.8 %shard_map.98 = (f32[4,4,3,4,8,128]{5,4,3,2,1,0:T(8,128)S(1)}, f32[3,4,8,128]{3,2,1,0:T(8,128)S(1)}) custom-call(f32[5,3,8,128]{3,2,1,0:T(8,128)S(1)} %copy-done, f32[16]{0:T(128)S(1)} %copy-done.1, f32[16]{0:T(128)S(1)} %copy-done.2, f32[4,4,24,8,128]{4,3,2,1,0:T(8,128)S(1)} %get-tuple-element.22.refs_7_.field_ref, ...), custom_call_target="tpu_custom_call" | custom-call | tf_op jit(solution)/shard_map/pallas_call | solution.py:723
  28.5 0.8 %collective-permute-start.10 = (f32[3,4,8,128]{3,2,1,0:T(8,128)S(1)}, f32[3,4,8,128]{3,2,1,0:T(8,128)S(1)}, u32[]{:S(2)}, u32[]{:S(2)}) collective-permute-start(f32[3,4,8,128]{3,2,1,0:T(8,128)S(1)} %get-tuple-element.33.own_ref), channel_id=1, source_target_pairs={{29,0},{28,1},{31,2},{30,3},{1,4},{0,5},{3,6},{2,7},{5,8},{4,9},{7... | collective-permute-start | bytes 147464 | tf_op jit(solution)/shard_map/ppermute | solution.py:35
  29.4 1.1 %collective-permute-start.9 = (f32[3,4,8,128]{3,2,1,0:T(8,128)S(1)}, f32[3,4,8,128]{3,2,1,0:T(8,128)S(1)}, u32[]{:S(2)}, u32[]{:S(2)}) collective-permute-start(f32[3,4,8,128]{3,2,1,0:T(8,128)S(1)} %get-tuple-element.33.own_ref), channel_id=1, source_target_pairs={{28,0},{29,1},{30,2},{31,3},{0,4},{1,5},{2,6},{3,7},{4,8},{5,9},{6... | collective-permute-start | bytes 147464 | tf_op jit(solution)/shard_map/ppermute | solution.py:35
  30.5 1.9 %collective-permute-start.8 = (f32[3,4,8,128]{3,2,1,0:T(8,128)S(1)}, f32[3,4,8,128]{3,2,1,0:T(8,128)S(1)}, u32[]{:S(2)}, u32[]{:S(2)}) collective-permute-start(f32[3,4,8,128]{3,2,1,0:T(8,128)S(1)} %get-tuple-element.33.own_ref), channel_id=1, source_target_pairs={{1,0},{0,1},{3,2},{2,3},{5,4},{4,5},{7,6},{6,7},{9,8},{8,9},{11,10... | collective-permute-start | bytes 147464 | tf_op jit(solution)/shard_map/ppermute | solution.py:35
  32.4 0.0 collective-permute-start.7
  32.4 2.5 %collective-permute-done.10.xz_ref = f32[3,4,8,128]{3,2,1,0:T(8,128)S(1)} collective-permute-done((f32[3,4,8,128]{3,2,1,0:T(8,128)S(1)}, f32[3,4,8,128]{3,2,1,0:T(8,128)S(1)}, u32[]{:S(2)}, u32[]{:S(2)}) %collective-permute-start.10) | collective-permute-done | bytes 49184 | tf_op jit(solution)/shard_map/ppermute | solution.py:35
  34.9 0.0 collective-permute-done.9.z_ref
  34.9 0.2 collective-permute-done.8.x_ref
  35.1 0.1 shard_map.100
  35.2 1.7 %collective-permute-start.11 = (f32[48,128]{1,0:T(8,128)S(1)}, f32[48,128]{1,0:T(8,128)S(1)}, u32[]{:S(2)}, u32[]{:S(2)}) collective-permute-start(f32[48,128]{1,0:T(8,128)S(1)} %get-tuple-element.35), channel_id=1, source_target_pairs={{2,0},{3,1},{0,2},{1,3},{6,4},{7,5},{4,6},{5,7},{10,8},{11,9},{8,1... | collective-permute-start | bytes 73736 | tf_op jit(solution)/shard_map/ppermute | solution.py:35
  37.0 0.5 %collective-permute-done.7.tail_ref = f32[8,8,128]{2,1,0:T(8,128)S(1)} collective-permute-done((f32[8,8,128]{2,1,0:T(8,128)S(1)}, f32[8,8,128]{2,1,0:T(8,128)S(1)}, u32[]{:S(2)}, u32[]{:S(2)}) %collective-permute-start.7) | collective-permute-done | bytes 32800 | tf_op jit(solution)/shard_map/ppermute | solution.py:27
  37.5 1.4 %shard_map.99 = (f32[4,24,4,8,128]{4,3,2,1,0:T(8,128)}, f32[2,9,16,128]{3,2,1,0:T(8,128)S(1)}) custom-call(f32[4,4,3,4,8,128]{5,4,3,2,1,0:T(8,128)S(1)} %get-tuple-element.23.inner_ref, f32[4,4,3,4,8,128]{5,4,3,2,1,0:T(8,128)S(1)} %get-tuple-element.30.outer_ref, f32[8,8,128]{2,1,0:T(8,128)S(1)} %collective-permute-done.7.tail_ref, ...), custom_call_target="tpu_custom_call" | custom-call | tf_op jit(solution)/shard_map/pallas_call | solution.py:737
  38.9 0.2 collective-permute-done.11.come_ref
  39.1 1.0 %shard_map.101 = f32[2,16,256]{2,1,0:T(8,128)} custom-call(f32[48,128]{1,0:T(8,128)S(1)} %get-tuple-element.34.keep_ref, f32[48,128]{1,0:T(8,128)S(1)} %collective-permute-done.11.come_ref, f32[2,9,16,128]{3,2,1,0:T(8,128)S(1)} %get-tuple-element.36.coupling_ref, f32[2,16,256]{2,1,0:T(8,128)S(1)} %get-tuple-element.20.own_ref.masked_ref, ...), custom_call_target="tpu_custom_call" | custom-call | tf_op jit(solution)/shard_map/pallas_call | solution.py:750
Async XLA Ops:
  0.6 21.6 %copy-start = (f32[5,3,8,128]{3,2,1,0:T(8,128)S(1)}, f32[5,3,8,128]{3,2,1,0:T(8,128)}, u32[]{:S(2)}) copy-start(f32[5,3,8,128]{3,2,1,0:T(8,128)} %constant.2.clone.refs_4_.trig_ref) | copy-start | bytes 184324
  0.6 7.2 %copy-start.4 = (s32[16,256]{1,0:T(8,128)S(1)}, s32[16,256]{1,0:T(8,128)}, u32[]{:S(2)}) copy-start(s32[16,256]{1,0:T(8,128)} %wet_hbm.1) | copy-start | bytes 49156
  0.7 6.5 %copy-start.3 = (f32[2,16,256]{2,1,0:T(8,128)S(1)}, f32[2,16,256]{2,1,0:T(8,128)}, u32[]{:S(2)}) copy-start(f32[2,16,256]{2,1,0:T(8,128)} %current_hbm.1) | copy-start | bytes 98308
  0.7 21.6 %copy-start.2 = (f32[16]{0:T(128)S(1)}, f32[16]{0:T(128)}, u32[]{:S(2)}) copy-start(f32[16]{0:T(128)} %energy_ref.1) | copy-start | bytes 196
  0.7 21.6 %copy-start.1 = (f32[16]{0:T(128)S(1)}, f32[16]{0:T(128)}, u32[]{:S(2)}) copy-start(f32[16]{0:T(128)} %speed_ref.1) | copy-start | bytes 196
  2.6 23.1 %collective-permute-start.5 = (f32[24,4,8,128]{3,2,1,0:T(8,128)S(1)}, f32[24,4,8,128]{3,2,1,0:T(8,128)S(1)}, u32[]{:S(2)}, u32[]{:S(2)}) collective-permute-start(f32[24,4,8,128]{3,2,1,0:T(8,128)S(1)} %get-tuple-element.24), channel_id=1, source_target_pairs={{28,0},{0,4},{4,8},{8,12},{12,16},{16,20},{20,24},{24,28},{29,1},{... | collective-permute-start | bytes 1179656 | tf_op jit(solution)/shard_map/ppermute | solution.py:27
  3.1 22.6 %collective-permute-start.6 = (f32[24,4,8,128]{3,2,1,0:T(8,128)S(1)}, f32[24,4,8,128]{3,2,1,0:T(8,128)S(1)}, u32[]{:S(2)}, u32[]{:S(2)}) collective-permute-start(f32[24,4,8,128]{3,2,1,0:T(8,128)S(1)} %get-tuple-element.25), channel_id=1, source_target_pairs={{4,0},{8,4},{12,8},{16,12},{20,16},{24,20},{28,24},{0,28},{5,1},{9... | collective-permute-start | bytes 1179656 | tf_op jit(solution)/shard_map/ppermute | solution.py:27
  7.2 8.0 %collective-permute-start = (f32[2,16,256]{2,1,0:T(8,128)S(1)}, f32[2,16,256]{2,1,0:T(8,128)S(1)}, u32[]{:S(2)}, u32[]{:S(2)}) collective-permute-start(f32[2,16,256]{2,1,0:T(8,128)S(1)} %copy-done.3), channel_id=1, source_target_pairs={{4,0},{8,4},{12,8},{16,12},{20,16},{24,20},{28,24},{0,28},{5,1},{9... | collective-permute-start | bytes 98312 | tf_op jit(solution)/shard_map/ppermute | solution.py:27
  7.9 7.3 %collective-permute-start.1 = (s32[16,256]{1,0:T(8,128)S(1)}, s32[16,256]{1,0:T(8,128)S(1)}, u32[]{:S(2)}, u32[]{:S(2)}) collective-permute-start(s32[16,256]{1,0:T(8,128)S(1)} %copy-done.4), channel_id=1, source_target_pairs={{4,0},{8,4},{12,8},{16,12},{20,16},{24,20},{28,24},{0,28},{5,1},{9... | collective-permute-start | bytes 49160 | tf_op jit(solution)/shard_map/ppermute | solution.py:27
  15.5 4.7 %collective-permute-start.4 = (f32[40,128]{1,0:T(8,128)S(1)}, f32[40,128]{1,0:T(8,128)S(1)}, u32[]{:S(2)}, u32[]{:S(2)}) collective-permute-start(f32[40,128]{1,0:T(8,128)S(1)} %shard_map.96.refs_0_), channel_id=1, source_target_pairs={{3,0},{2,1},{1,2},{0,3},{7,4},{6,5},{5,6},{4,7},{11,8},{10,9},{9,1... | collective-permute-start | bytes 61448 | tf_op jit(solution)/shard_map/ppermute | solution.py:35
  18.0 3.8 %collective-permute-start.3 = (f32[40,128]{1,0:T(8,128)S(1)}, f32[40,128]{1,0:T(8,128)S(1)}, u32[]{:S(2)}, u32[]{:S(2)}) collective-permute-start(f32[40,128]{1,0:T(8,128)S(1)} %shard_map.96.refs_0_), channel_id=1, source_target_pairs={{2,0},{3,1},{0,2},{1,3},{6,4},{7,5},{4,6},{5,7},{10,8},{11,9},{8,1... | collective-permute-start | bytes 61448 | tf_op jit(solution)/shard_map/ppermute | solution.py:35
  18.5 3.8 %collective-permute-start.2 = (f32[40,128]{1,0:T(8,128)S(1)}, f32[40,128]{1,0:T(8,128)S(1)}, u32[]{:S(2)}, u32[]{:S(2)}) collective-permute-start(f32[40,128]{1,0:T(8,128)S(1)} %shard_map.96.refs_0_), channel_id=1, source_target_pairs={{1,0},{0,1},{3,2},{2,3},{5,4},{4,5},{7,6},{6,7},{9,8},{8,9},{11,10... | collective-permute-start | bytes 61448 | tf_op jit(solution)/shard_map/ppermute | solution.py:35
  28.5 6.4 %collective-permute-start.10 = (f32[3,4,8,128]{3,2,1,0:T(8,128)S(1)}, f32[3,4,8,128]{3,2,1,0:T(8,128)S(1)}, u32[]{:S(2)}, u32[]{:S(2)}) collective-permute-start(f32[3,4,8,128]{3,2,1,0:T(8,128)S(1)} %get-tuple-element.33.own_ref), channel_id=1, source_target_pairs={{29,0},{28,1},{31,2},{30,3},{1,4},{0,5},{3,6},{2,7},{5,8},{4,9},{7... | collective-permute-start | bytes 147464 | tf_op jit(solution)/shard_map/ppermute | solution.py:35
  29.4 5.5 %collective-permute-start.9 = (f32[3,4,8,128]{3,2,1,0:T(8,128)S(1)}, f32[3,4,8,128]{3,2,1,0:T(8,128)S(1)}, u32[]{:S(2)}, u32[]{:S(2)}) collective-permute-start(f32[3,4,8,128]{3,2,1,0:T(8,128)S(1)} %get-tuple-element.33.own_ref), channel_id=1, source_target_pairs={{28,0},{29,1},{30,2},{31,3},{0,4},{1,5},{2,6},{3,7},{4,8},{5,9},{6... | collective-permute-start | bytes 147464 | tf_op jit(solution)/shard_map/ppermute | solution.py:35
  30.5 4.7 %collective-permute-start.8 = (f32[3,4,8,128]{3,2,1,0:T(8,128)S(1)}, f32[3,4,8,128]{3,2,1,0:T(8,128)S(1)}, u32[]{:S(2)}, u32[]{:S(2)}) collective-permute-start(f32[3,4,8,128]{3,2,1,0:T(8,128)S(1)} %get-tuple-element.33.own_ref), channel_id=1, source_target_pairs={{1,0},{0,1},{3,2},{2,3},{5,4},{4,5},{7,6},{6,7},{9,8},{8,9},{11,10... | collective-permute-start | bytes 147464 | tf_op jit(solution)/shard_map/ppermute | solution.py:35
  32.4 5.1 %collective-permute-start.7 = (f32[8,8,128]{2,1,0:T(8,128)S(1)}, f32[8,8,128]{2,1,0:T(8,128)S(1)}, u32[]{:S(2)}, u32[]{:S(2)}) collective-permute-start(f32[8,8,128]{2,1,0:T(8,128)S(1)} %get-tuple-element.31), channel_id=1, source_target_pairs={{28,0},{0,4},{4,8},{8,12},{12,16},{16,20},{20,24},{24,28},{29,1},{... | collective-permute-start | bytes 98312 | tf_op jit(solution)/shard_map/ppermute | solution.py:27
  35.2 3.9 %collective-permute-start.11 = (f32[48,128]{1,0:T(8,128)S(1)}, f32[48,128]{1,0:T(8,128)S(1)}, u32[]{:S(2)}, u32[]{:S(2)}) collective-permute-start(f32[48,128]{1,0:T(8,128)S(1)} %get-tuple-element.35), channel_id=1, source_target_pairs={{2,0},{3,1},{0,2},{1,3},{6,4},{7,5},{4,6},{5,7},{10,8},{11,9},{8,1... | collective-permute-start | bytes 73736 | tf_op jit(solution)/shard_map/ppermute | solution.py:35
